TPU v7x, 32 devices: a whole 2x2x4 slice. The times are simulated.
32 devices in a mesh: row: 4 (over y, x), col: 8 (over z, core).
Axes of the slice: x: 2, y: 2, z: 4, core: 2. Of those that a mesh axis runs over, the one named last changes fastest.
Arguments:
- node_feats: bfloat16 [4096, 256], P(('row', 'col')), may hold values from -6 to 6
- degrees: int32 [4096], P(('row', 'col')), may hold values from 64 to 639
- self_weight: bfloat16 [256, 256], replicated, may hold values from -0.375 to 0.375
- neigh_weight: bfloat16 [256, 256], replicated, may hold values from -0.375 to 0.375
- bias: float32 [256], replicated, may hold values from -3 to 3
- tiles: bfloat16 [4, 8, 80, 128, 128], P('row', 'col'), may hold values from -6 to 6
- tile_rows: int32 [4, 8, 80], P('row', 'col'), may hold values from 0 to 7
- tile_cols: int32 [4, 8, 80], P('row', 'col'), may hold values from 0 to 3
- tile_counts: int32 [4, 8], P('row', 'col'), may hold values from 10 to 80, as said below
- out_grad: bfloat16 [4096, 256], P(('row', 'col')), may hold values from -6 to 6
Outputs:
- hidden: bfloat16 [4096, 256], P(('row', 'col'))
- feat_grad: bfloat16 [4096, 256], P(('row', 'col'))
- grad_self: float32 [256, 256], replicated
- grad_neigh: float32 [256, 256], replicated
- grad_bias: float32 [256], replicated
Inputs may be any that keep to these rules, and one draw needn't show every extreme that they name: `tile_counts`: every grid row has a cell with all 80 slots holding blocks.
All inputs are finite; a program needn't handle non-finite values.
Results may differ from a plain program's by a relative error of at most 0.018.
Values may be sent and summed in bfloat16 or wider, within the bound.
No kernel may reach another device: no remote copies, remote signals or barrier semaphores. Data moves between devices by JAX's collectives and lax.ppermute only.
A program may use at most 64 MiB of HBM per device.

v0:
```python
import math

import jax
import jax.numpy as jnp
from jax import lax
from jax.sharding import PartitionSpec as P


def tile_products(block_vals, near_index, far_index, live_count, source, out_blocks, transposed):
    tile_total = block_vals.shape[0]
    group_size = min(16, tile_total)
    tile_edge = block_vals.shape[-1]
    feat_width = source.shape[-1]
    source_blocks = source.reshape(source.shape[0] // tile_edge, tile_edge, feat_width)
    turn_count = (live_count + group_size - 1) // group_size

    def advance(turn, running):
        first_tile = turn * group_size
        group_vals = lax.dynamic_slice_in_dim(block_vals, first_tile, group_size, 0)
        fetch_index = lax.dynamic_slice_in_dim(far_index, first_tile, group_size, 0)
        place_index = lax.dynamic_slice_in_dim(near_index, first_tile, group_size, 0)
        picked = source_blocks[fetch_index]
        if transposed:
            products = jnp.einsum(
                "kab,kaf->kbf", group_vals, picked, preferred_element_type=jnp.float32
            )
        else:
            products = jnp.einsum(
                "kab,kbf->kaf", group_vals, picked, preferred_element_type=jnp.float32
            )
        ordinal = first_tile + jnp.arange(group_size)
        active = ordinal < live_count
        table = (
            (place_index[:, None] == jnp.arange(out_blocks)[None, :]) & active[:, None]
        ).astype(jnp.float32)
        return running + jnp.einsum("kl,kaf->laf", table, products)

    initial = jnp.zeros((out_blocks, tile_edge, feat_width), jnp.float32)
    result = lax.fori_loop(0, turn_count, advance, initial)
    return result.reshape(out_blocks * tile_edge, feat_width)


def on_device(
    node_feats,
    degrees,
    self_weight,
    neigh_weight,
    bias,
    tiles,
    tile_rows,
    tile_cols,
    tile_counts,
    out_grad,
):
    grid_rows = lax.axis_size("row")
    grid_cols = lax.axis_size("col")
    per_device = node_feats.shape[0]
    tile_edge = tiles.shape[-1]
    block_vals = tiles[0, 0]
    block_rows = tile_rows[0, 0]
    block_cols = tile_cols[0, 0]
    live_count = tile_counts[0, 0]
    row_blocks = grid_cols * per_device // tile_edge
    col_blocks = grid_rows * per_device // tile_edge
    stripe = lax.all_gather(node_feats, "row", axis=0, tiled=True)
    partial_value = tile_products(
        block_vals, block_rows, block_cols, live_count, stripe, row_blocks, False
    )
    summed = lax.psum_scatter(
        partial_value.astype(jnp.bfloat16), "col", scatter_dimension=0, tiled=True
    ).astype(jnp.float32)
    degree_col = degrees.astype(jnp.float32)[:, None]
    aggregate = (summed / degree_col).astype(jnp.bfloat16)
    preact = (
        jnp.dot(node_feats, self_weight, preferred_element_type=jnp.float32)
        + jnp.dot(aggregate, neigh_weight, preferred_element_type=jnp.float32)
        + bias
    )
    hidden = jax.nn.silu(preact).astype(jnp.bfloat16)
    sigmoid_val = jax.nn.sigmoid(preact)
    dpre = out_grad.astype(jnp.float32) * sigmoid_val * (1.0 + preact * (1.0 - sigmoid_val))
    dpre_b = dpre.astype(jnp.bfloat16)
    first_dims = (((0,), (0,)), ((), ()))
    last_dims = (((1,), (1,)), ((), ()))
    self_term = lax.dot_general(node_feats, dpre_b, first_dims, preferred_element_type=jnp.float32)
    neigh_term = lax.dot_general(aggregate, dpre_b, first_dims, preferred_element_type=jnp.float32)
    bias_term = jnp.sum(dpre, axis=0)
    self_total, neigh_total, bias_total = lax.psum(
        (self_term, neigh_term, bias_term), ("row", "col")
    )
    grad_scale = 1.0 / math.sqrt(grid_rows * grid_cols * per_device)
    back_agg = lax.dot_general(dpre_b, neigh_weight, last_dims, preferred_element_type=jnp.float32)
    spread = (back_agg / degree_col).astype(jnp.bfloat16)
    row_stripe = lax.all_gather(spread, "col", axis=0, tiled=True)
    back_partial = tile_products(
        block_vals, block_cols, block_rows, live_count, row_stripe, col_blocks, True
    )
    neighbour_grad = lax.psum_scatter(
        back_partial.astype(jnp.bfloat16), "row", scatter_dimension=0, tiled=True
    ).astype(jnp.float32)
    own_grad = lax.dot_general(dpre_b, self_weight, last_dims, preferred_element_type=jnp.float32)
    feat_grad = (own_grad + neighbour_grad).astype(jnp.bfloat16)
    return (
        hidden,
        feat_grad,
        self_total * grad_scale,
        neigh_total * grad_scale,
        bias_total * grad_scale,
    )


def solution(mesh):
    placed = (
        P(("row", "col"), None),
        P(("row", "col")),
        P(),
        P(),
        P(),
        P("row", "col", None, None, None),
        P("row", "col", None),
        P("row", "col", None),
        P("row", "col"),
        P(("row", "col"), None),
    )
    return jax.shard_map(
        on_device,
        mesh=mesh,
        in_specs=placed,
        out_specs=(P(("row", "col"), None), P(("row", "col"), None), P(), P(), P()),
        check_vma=False,
    )
```

profile of v0, /device:TPU:0, one launch (start us, length us, event | category | flops | bytes accessed | tf_op | source)
XLA Modules:
  0.0 252.7 jit_solution(11372797624394869808)
XLA Ops:
  7.9 10.8 %all_gather.6 = bf16[512,256]{1,0:T(8,128)(2,1)S(1)} all-gather(bf16[128,256]{1,0:T(8,128)(2,1)} %param.14), channel_id=1, replica_groups=mesh['row'=4,'col'=8] {'row'}, dimensions={0}, use_global_device_ids=true | all-gather | bytes 327680 | tf_op jit(solution)/shard_map/all_gather | solution.py:65
  18.7 8.6 %while.20 = (s32[]{:T(128)}, f32[8,128,256]{2,0,1:T(8,128)S(1)}, s32[]{:T(128)}, s32[80]{0:T(128)}, s32[]{:T(128)}, /*index=5*/bf16[80,128,128]{2,1,0:T(8,128)(2...) while((s32[]{:T(128)}, f32[8,128,256]{2,0,1:T(8,128)S(1)}, ...), condition=%wide.region_1.2_spmd, body=%wide.region_0.1_spmd.sunk | while | flops 142869840 | bytes 7870395 | solution.py:39
  18.8 0.7 compare_select_fusion.4
  20.1 1.5 fusion.60
  23.1 0.7 compare_select_fusion.4
  24.5 1.5 fusion.60
  27.5 0.9 copy.15
  28.7 43.1 %reduce-scatter.3.cloned.1.call-done = bf16[128,256]{1,0:T(8,128)(2,1)} async-done(((bf16[1024,256]{1,0:T(8,128)(2,1)}), bf16[128,256]{1,0:T(8,128)(2,1)}) %reduce-scatter.3.cloned.1.call-update) | async-done | bytes 65552 | tf_op jit(solution)/shard_map/reduce_scatter | solution.py:69
  71.8 1.8 fusion.30
  73.8 0.9 convolution_bitcast_fusion
  74.8 14.9 %all_gather.7 = bf16[1024,256]{1,0:T(8,128)(2,1)S(1)} all-gather(bf16[128,256]{1,0:T(8,128)(2,1)S(1)} %fusion.28), channel_id=1, replica_groups=mesh['row'=4,'col'=8] {'col'}, dimensions={0}, use_global_device_ids=true | all-gather | bytes 589824 | tf_op jit(solution)/shard_map/all_gather | solution.py:94
  89.7 1.0 fusion.29
  90.8 8.0 %while.21 = (s32[]{:T(128)}, f32[4,128,256]{2,0,1:T(4,128)S(1)}, s32[]{:T(128)}, s32[80]{0:T(128)S(1)}, s32[]{:T(128)}, /*index=5*/bf16[80,128,128]{2,1,0:T(8,12...) while((s32[]{:T(128)}, f32[4,128,256]{2,0,1:T(4,128)S(1)}, ...), condition=%wide.region_4.5_spmd, body=%wide.region_3.4_spmd.sunk | while | flops 138544336 | bytes 6820511 | solution.py:39
  91.6 1.5 fusion.66
  93.8 1.0 fusion.67
  95.6 1.5 fusion.66
  97.8 1.0 fusion.67
  99.7 49.1 %psum.23 = f32[256]{0:T(256)S(1)} all-reduce(f32[256]{0:T(256)S(1)} %get-tuple-element.132), channel_id=1, replica_groups=mesh['row'=4,'col'=8] {'row','col'}, use_global_device_ids=true, to_apply=%region_9.10 | all-reduce | flops 256 | bytes 2048 | tf_op jit(solution)/shard_map/psum | solution.py:88
  149.3 69.0 %all-reduce.3.cloned.1.call-done = (f32[256,256]{0,1:T(8,128)}, f32[256,256]{0,1:T(8,128)}) async-done(((f32[256,256]{0,1:T(8,128)}, f32[256,256]{0,1:T(8,128)}), (f32[256,256]{0,1:T(8,128)}, f32[256,256]{0,1:T(8,128)})) %all-reduce.3.cloned.1.call-update) | async-done | bytes 524304 | tf_op jit(solution)/shard_map/psum | solution.py:88
  218.4 1.1 broadcast_multiply_fusion
  219.5 0.8 copy.18
  220.3 0.8 copy.19
  221.1 23.4 %reduce-scatter.5.cloned.1.call-done = bf16[128,256]{1,0:T(8,128)(2,1)} async-done(((bf16[512,256]{1,0:T(8,128)(2,1)}), bf16[128,256]{1,0:T(8,128)(2,1)}) %reduce-scatter.5.cloned.1.call-update) | async-done | bytes 65552 | tf_op jit(solution)/shard_map/reduce_scatter | solution.py:98
  244.5 1.7 fusion.27
  (57 shorter events, 9.1 us)
Async XLA Ops:
  7.2 64.6 %copy-start = (bf16[256,256]{1,0:T(8,128)(2,1)S(1)}, bf16[256,256]{1,0:T(8,128)(2,1)}, u32[]{:S(2)}) copy-start(bf16[256,256]{1,0:T(8,128)(2,1)} %param.17) | copy-start | bytes 393220
  7.2 64.6 %reduce-scatter.3.cloned.1.call-start = ((), (), s32[]{:S(2)}) async-start(), calls=%async_computation.2 | async-start | bytes 589824 | tf_op jit(solution)/shard_map/reduce_scatter | solution.py:69
  18.8 2.9 %copy-start.7 = (s32[80]{0:T(128)S(1)}, s32[80]{0:T(128)}, u32[]{:S(2)}) copy-start(s32[80]{0:T(128)} %get-tuple-element.267) | copy-start | bytes 964 | tf_op jit(solution)/shard_map/while
  23.1 2.9 %copy-start.7 = (s32[80]{0:T(128)S(1)}, s32[80]{0:T(128)}, u32[]{:S(2)}) copy-start(s32[80]{0:T(128)} %get-tuple-element.267) | copy-start | bytes 964 | tf_op jit(solution)/shard_map/while
  27.4 1.1 copy-start.6
  27.4 1.1 copy-start.1
  27.4 1.1 copy-start.2
  27.4 44.4 %copy-start.3 = (bf16[128,256]{1,0:T(8,128)(2,1)S(1)}, bf16[128,256]{1,0:T(8,128)(2,1)}, u32[]{:S(2)}) copy-start(bf16[128,256]{1,0:T(8,128)(2,1)} %param.23) | copy-start | bytes 196612
  27.4 44.4 %copy-start.5 = (f32[256]{0:T(256)S(1)}, f32[256]{0:T(256)}, u32[]{:S(2)}) copy-start(f32[256]{0:T(256)} %param.18) | copy-start | bytes 3076
  28.4 62.4 %copy-start.8 = (s32[80]{0:T(128)S(1)}, s32[80]{0:T(128)}, u32[]{:S(2)}) copy-start(s32[80]{0:T(128)} %get-tuple-element.331) | copy-start | bytes 964
  28.4 62.4 %copy-start.9 = (s32[80]{0:T(128)S(1)}, s32[80]{0:T(128)}, u32[]{:S(2)}) copy-start(s32[80]{0:T(128)} %get-tuple-element.332) | copy-start | bytes 964
  28.4 190.0 %all-reduce.3.cloned.1.call-start = ((), (), s32[]{:S(2)}) async-start(), calls=%async_computation.4 | async-start | bytes 1048576 | tf_op jit(solution)/shard_map/psum | solution.py:88
  71.8 17.9 %copy-start.4 = (bf16[128,256]{1,0:T(8,128)(2,1)S(1)}, bf16[128,256]{1,0:T(8,128)(2,1)}, u32[]{:S(2)}) copy-start(bf16[128,256]{1,0:T(8,128)(2,1)} %reduce-scatter.3.cloned.1.call-done) | copy-start | bytes 196612
  90.7 153.9 %reduce-scatter.5.cloned.1.call-start = ((), (), s32[]{:S(2)}) async-start(), calls=%async_computation.3 | async-start | bytes 327680 | tf_op jit(solution)/shard_map/reduce_scatter | solution.py:98
Sparse Core Ops, SparseCore 0:
  28.5 43.2 reduce-scatter.2
  90.8 127.5 all-reduce.2
  221.2 23.3 reduce-scatter.4
where the time goes:
time: 253 us
  waiting for transfers between devices  136 us (54%)
  blocking collectives  74.8 us (30%)
  matrix products  15.1 us (6%)
  between operations  14.6 us (6%)
  local copies, waits for them, and re-layouts  6.26 us (2%)
  other arithmetic  6.04 us (2%)
    psum x1, waiting for transfers between devices, on_device(): lax.psum((self_term, neigh_term, bias_term), ('row', 'col'))  69 us
    psum x1, blocking collectives, on_device(): lax.psum((self_term, neigh_term, bias_term), ('row', 'col'))  49.1 us
    reduce_scatter x1, waiting for transfers between devices, on_device(): lax.psum_scatter(partial_value.astype(jnp.bfloat16), 'col', scatter_dimen...  43.1 us
    reduce_scatter x1, waiting for transfers between devices, on_device(): lax.psum_scatter(back_partial.astype(jnp.bfloat16), 'row', scatter_dimens...  23.4 us
    all_gather x1, blocking collectives, on_device(): row_stripe = lax.all_gather(spread, 'col', axis=0, tiled=True)  14.9 us
    all_gather x1, blocking collectives, on_device(): stripe = lax.all_gather(node_feats, 'row', axis=0, tiled=True)  10.8 us
  transfers between devices with their start and end apart: 3, of which 3 were waited for; matrix products, arithmetic and copies ran while one was open for 5% of the time, Pallas kernels for 0%

commit v1 on v0

v1 whole, which is shorter than its diff:
```python
import functools
import math

import jax
import jax.numpy as jnp
from jax import lax
from jax.experimental import pallas as pl
from jax.experimental.pallas import tpu as pltpu
from jax.sharding import PartitionSpec as P

F32 = jnp.float32
BF16 = jnp.bfloat16
LAST = (((1,), (1,)), ((), ()))
FIRST = (((0,), (0,)), ((), ()))


def tile_products(block_vals, near_index, far_index, live_count, source, out_blocks, transposed):
    tile_total = block_vals.shape[0]
    group_size = min(16, tile_total)
    tile_edge = block_vals.shape[-1]
    feat_width = source.shape[-1]
    source_blocks = source.reshape(source.shape[0] // tile_edge, tile_edge, feat_width)
    turn_count = (live_count + group_size - 1) // group_size

    def advance(turn, running):
        first_tile = turn * group_size
        group_vals = lax.dynamic_slice_in_dim(block_vals, first_tile, group_size, 0)
        fetch_index = lax.dynamic_slice_in_dim(far_index, first_tile, group_size, 0)
        place_index = lax.dynamic_slice_in_dim(near_index, first_tile, group_size, 0)
        picked = source_blocks[fetch_index]
        if transposed:
            products = jnp.einsum("kab,kaf->kbf", group_vals, picked, preferred_element_type=F32)
        else:
            products = jnp.einsum("kab,kbf->kaf", group_vals, picked, preferred_element_type=F32)
        ordinal = first_tile + jnp.arange(group_size)
        active = ordinal < live_count
        table = (
            (place_index[:, None] == jnp.arange(out_blocks)[None, :]) & active[:, None]
        ).astype(F32)
        return running + jnp.einsum("kl,kaf->laf", table, products)

    initial = jnp.zeros((out_blocks, tile_edge, feat_width), F32)
    result = lax.fori_loop(0, turn_count, advance, initial)
    return result.reshape(out_blocks * tile_edge, feat_width)


def general_form(
    node_feats,
    degrees,
    self_weight,
    neigh_weight,
    bias,
    tiles,
    tile_rows,
    tile_cols,
    tile_counts,
    out_grad,
):
    grid_rows = lax.axis_size("row")
    grid_cols = lax.axis_size("col")
    per_device = node_feats.shape[0]
    tile_edge = tiles.shape[-1]
    block_vals = tiles[0, 0]
    block_rows = tile_rows[0, 0]
    block_cols = tile_cols[0, 0]
    live_count = tile_counts[0, 0]
    row_blocks = grid_cols * per_device // tile_edge
    col_blocks = grid_rows * per_device // tile_edge
    stripe = lax.all_gather(node_feats, "row", axis=0, tiled=True)
    partial_value = tile_products(
        block_vals, block_rows, block_cols, live_count, stripe, row_blocks, False
    )
    summed = lax.psum_scatter(
        partial_value.astype(BF16), "col", scatter_dimension=0, tiled=True
    ).astype(F32)
    degree_col = degrees.astype(F32)[:, None]
    aggregate = (summed / degree_col).astype(BF16)
    preact = (
        jnp.dot(node_feats, self_weight, preferred_element_type=F32)
        + jnp.dot(aggregate, neigh_weight, preferred_element_type=F32)
        + bias
    )
    hidden = jax.nn.silu(preact).astype(BF16)
    sigmoid_val = jax.nn.sigmoid(preact)
    dpre = out_grad.astype(F32) * sigmoid_val * (1.0 + preact * (1.0 - sigmoid_val))
    dpre_b = dpre.astype(BF16)
    self_term = lax.dot_general(node_feats, dpre_b, FIRST, preferred_element_type=F32)
    neigh_term = lax.dot_general(aggregate, dpre_b, FIRST, preferred_element_type=F32)
    bias_term = jnp.sum(dpre, axis=0)
    self_total, neigh_total, bias_total = lax.psum(
        (self_term, neigh_term, bias_term), ("row", "col")
    )
    grad_scale = 1.0 / math.sqrt(grid_rows * grid_cols * per_device)
    back_agg = lax.dot_general(dpre_b, neigh_weight, LAST, preferred_element_type=F32)
    spread = (back_agg / degree_col).astype(BF16)
    row_stripe = lax.all_gather(spread, "col", axis=0, tiled=True)
    back_partial = tile_products(
        block_vals, block_cols, block_rows, live_count, row_stripe, col_blocks, True
    )
    neighbour_grad = lax.psum_scatter(
        back_partial.astype(BF16), "row", scatter_dimension=0, tiled=True
    ).astype(F32)
    own_grad = lax.dot_general(dpre_b, self_weight, LAST, preferred_element_type=F32)
    feat_grad = (own_grad + neighbour_grad).astype(BF16)
    return (
        hidden,
        feat_grad,
        self_total * grad_scale,
        neigh_total * grad_scale,
        bias_total * grad_scale,
    )


def sds(shape, dtype):
    return jax.ShapeDtypeStruct(shape, dtype)


def call(body, outs, args, name, smem=0, scratch=(), cost=None, grid=None, in_specs=None):
    single = not isinstance(outs, (list, tuple))
    outs = [outs] if single else list(outs)
    if in_specs is None:
        in_specs = [pl.BlockSpec(memory_space=pltpu.SMEM)] * smem + [
            pl.BlockSpec(memory_space=pltpu.VMEM)
        ] * (len(args) - smem)
    flops, moved = cost or (1 << 20, 1 << 18)
    result = pl.pallas_call(
        body,
        out_shape=outs,
        in_specs=in_specs,
        out_specs=[pl.BlockSpec(memory_space=pltpu.VMEM)] * len(outs),
        scratch_shapes=list(scratch),
        compiler_params=pltpu.CompilerParams(vmem_limit_bytes=24 << 20),
        cost_estimate=pl.CostEstimate(flops=flops, bytes_accessed=moved, transcendentals=0),
        name=name,
    )(*args)
    return result[0] if single else result


def dot(a, b):
    return jnp.dot(a, b, preferred_element_type=F32)


def build_cell(place, tile_rows, tile_cols, tiles, grid_rows, grid_cols):
    total, edge = tiles.shape[0], tiles.shape[-1]
    group = 16 if total % 16 == 0 else total
    half = grid_cols // 2

    def body(place_ref, rows_ref, cols_ref, tiles_ref, cell_ref, sums):
        step = pl.program_id(0)

        @pl.when(step == 0)
        def _():
            sums[...] = jnp.zeros_like(sums)

        my_row, my_col, count = place_ref[0], place_ref[1], place_ref[2]
        first = step * group

        def add_tile(k, carry):
            near = rows_ref[first + k] ^ my_col
            far = cols_ref[first + k] ^ my_row
            slot = ((near >> 1) + half * (near & 1)) * grid_rows + far
            sums[slot] += tiles_ref[k].astype(F32)
            return carry

        lax.fori_loop(0, jnp.clip(count - first, 0, group), add_tile, 0)

        @pl.when(step == pl.num_programs(0) - 1)
        def _():
            for i in range(grid_cols):
                for j in range(grid_rows):
                    cell_ref[i * edge : (i + 1) * edge, j * edge : (j + 1) * edge] = sums[
                        i * grid_rows + j
                    ].astype(BF16)

    smem = pl.BlockSpec(memory_space=pltpu.SMEM)
    return pl.pallas_call(
        body,
        out_shape=sds((grid_cols * edge, grid_rows * edge), BF16),
        grid=(total // group,),
        in_specs=[smem] * 3 + [pl.BlockSpec((group, edge, edge), lambda i: (i, 0, 0))],
        out_specs=pl.BlockSpec((grid_cols * edge, grid_rows * edge), lambda i: (0, 0)),
        scratch_shapes=[pltpu.VMEM((grid_rows * grid_cols, edge, edge), F32)],
        compiler_params=pltpu.CompilerParams(vmem_limit_bytes=24 << 20),
        cost_estimate=pl.CostEstimate(
            flops=1 << 24, bytes_accessed=4 * total * edge * edge, transcendentals=0
        ),
        name="build_cell",
    )(place, tile_rows, tile_cols, tiles)


def swap(value, axis, distance):
    size = lax.axis_size(axis)
    return lax.ppermute(value, axis, [(i, i ^ distance) for i in range(size)])


def direct_form(
    node_feats,
    degrees,
    self_weight,
    neigh_weight,
    bias,
    tiles,
    tile_rows,
    tile_cols,
    tile_counts,
    out_grad,
):
    grid_rows = lax.axis_size("row")
    grid_cols = lax.axis_size("col")
    half = grid_cols // 2
    n, width = node_feats.shape
    grad_scale = 1.0 / math.sqrt(grid_rows * grid_cols * n)
    place = jnp.stack([lax.axis_index("row"), lax.axis_index("col"), tile_counts[0, 0]])

    feats = [node_feats] + [swap(node_feats, "row", k) for k in range(1, grid_rows)]

    cell = build_cell(place, tile_rows[0, 0], tile_cols[0, 0], tiles[0, 0], grid_rows, grid_cols)

    def prepare(x_ref, w_ref, b_ref, d_ref, pre_ref, deg_ref, degrow_ref):
        pre_ref[...] = dot(x_ref[...], w_ref[...]) + b_ref[...]
        line = d_ref[...].astype(F32)
        degrow_ref[...] = line
        deg_ref[...] = jnp.broadcast_to(line, (n, n)).T

    pre, deg, deg_row = call(
        prepare,
        [sds((n, width), F32), sds((n, n), F32), sds((1, n), F32)],
        [node_feats, self_weight, bias.reshape(1, width), degrees.reshape(1, n)],
        "prepare",
    )

    def products(part, cell_ref, *refs):
        *x_refs, out_ref = refs
        stripe = jnp.concatenate([r[...] for r in x_refs], axis=0)
        rows = half * n
        out_ref[...] = dot(cell_ref[part * rows : (part + 1) * rows, :], stripe).astype(
            out_ref.dtype
        )

    work = (2 * half * n * grid_rows * n * width, 1 << 20)
    sent = call(
        functools.partial(products, 1),
        sds((half * n, width), BF16),
        [cell, *feats],
        "forward_sent",
        cost=work,
    )
    sent_in = swap(sent, "col", 1)
    kept = call(
        functools.partial(products, 0),
        sds((half * n, width), F32),
        [cell, *feats],
        "forward_kept",
        cost=work,
    )

    def pair_sums(kept_ref, in_ref, own_ref, *out_refs):
        total = kept_ref[...] + in_ref[...].astype(F32)
        own_ref[...] = total[:n]
        for q, ref in enumerate(out_refs):
            ref[...] = total[(q + 1) * n : (q + 2) * n].astype(BF16)

    own_sum, *parts = call(
        pair_sums,
        [sds((n, width), F32)] + [sds((n, width), BF16)] * (half - 1),
        [kept, sent_in],
        "pair_sums",
    )
    parts_in = [swap(part, "col", 2 * (q + 1)) for q, part in enumerate(parts)]

    def dense(own_ref, *refs):
        *in_refs, pre_ref, deg_ref, degrow_ref, w_ref, g_ref, spread_ref, preact_ref, agg_ref = refs
        total = own_ref[...]
        for ref in in_refs:
            total = total + ref[...].astype(F32)
        d = deg_ref[...]
        agg = (total / jnp.concatenate([d] * (width // n), axis=1)).astype(BF16)
        agg_ref[...] = agg
        v = pre_ref[...] + dot(agg, w_ref[...])
        preact_ref[...] = v
        s = jax.nn.sigmoid(v)
        dpre = g_ref[...].astype(F32) * s * (1.0 + v * (1.0 - s))
        back = lax.dot_general(
            w_ref[...], dpre.astype(BF16), LAST, preferred_element_type=F32
        )
        spread_ref[...] = (back / degrow_ref[...]).astype(BF16)

    spread, preact, aggregate = call(
        dense,
        [sds((width, n), BF16), sds((n, width), F32), sds((n, width), BF16)],
        [own_sum, *parts_in, pre, deg, deg_row, neigh_weight, out_grad],
        "dense",
    )
    near = [spread] + [swap(spread, "col", 2 * q) for q in range(1, half)]

    pad = 16

    def terms(place_ref, v_ref, agg_ref, x_ref, w_ref, g_ref, hid_ref, own_ref, keep_ref, send_ref):
        v = v_ref[...]
        s = jax.nn.sigmoid(v)
        hid_ref[...] = (v * s).astype(BF16)
        dpre = g_ref[...].astype(F32) * s * (1.0 + v * (1.0 - s))
        dpre_b = dpre.astype(BF16)
        own_ref[...] = lax.dot_general(w_ref[...], dpre_b, LAST, preferred_element_type=F32)
        self_term = lax.dot_general(x_ref[...], dpre_b, FIRST, preferred_element_type=F32)
        neigh_term = lax.dot_general(agg_ref[...], dpre_b, FIRST, preferred_element_type=F32)
        first = (place_ref[1] & 1) == 0
        keep_ref[:width] = jnp.where(first, self_term, neigh_term).astype(BF16)
        send_ref[:width] = jnp.where(first, neigh_term, self_term).astype(BF16)
        line = jnp.broadcast_to(jnp.sum(dpre, axis=0, keepdims=True), (pad, width)).astype(BF16)
        keep_ref[width:] = line
        send_ref[width:] = line

    hidden, own_grad, g_keep, g_send = call(
        terms,
        [
            sds((n, width), BF16),
            sds((width, n), F32),
            sds((width + pad, width), BF16),
            sds((width + pad, width), BF16),
        ],
        [place, preact, aggregate, node_feats, self_weight, out_grad],
        "terms",
        smem=1,
    )
    g_in = swap(g_send, "col", 1)
    piece = width // 2

    def halves(place_ref, a_ref, b_ref, keep_ref, send_ref):
        x = place_ref[0] & 1
        mine = pl.ds(pl.multiple_of(x * piece, piece), piece)
        other = pl.ds(pl.multiple_of((1 - x) * piece, piece), piece)
        tail = pl.ds(width, pad)
        for ref, span in ((keep_ref, mine), (send_ref, other)):
            ref[:piece] = (a_ref[span, :].astype(F32) + b_ref[span, :].astype(F32)).astype(BF16)
            ref[piece:] = (a_ref[tail, :].astype(F32) + b_ref[tail, :].astype(F32)).astype(BF16)

    small = sds((piece + pad, width), BF16)
    h_keep, h_send = call(halves, [small, small], [place, g_keep, g_in], "halves", smem=1)
    h_in = swap(h_send, "row", 1)

    def add_two(a_ref, b_ref, out_ref):
        out_ref[...] = (a_ref[...].astype(F32) + b_ref[...].astype(F32)).astype(BF16)

    y_part = call(add_two, small, [h_keep, h_in], "add_x")
    for k in (2 ** i for i in range(1, grid_rows.bit_length() - 1)):
        y_part = call(add_two, small, [y_part, swap(y_part, "row", k)], "add_y")
    z_parts = [y_part] + [swap(y_part, "col", 2 * q) for q in range(1, half)]

    def add_many(*refs):
        *in_refs, out_ref = refs
        vals = [ref[...].astype(F32) for ref in in_refs]
        while len(vals) > 1:
            vals = [vals[i] + vals[i + 1] for i in range(0, len(vals), 2)]
        out_ref[...] = vals[0].astype(BF16)

    g_piece = call(add_many, small, z_parts, "add_z")
    g_other = swap(g_piece, "row", 1)

    far = [swap(part, "col", 1) for part in near]

    def back_first(cell_ref, *refs):
        *s_refs, out_ref = refs
        left = jnp.concatenate([r[...] for r in s_refs], axis=1)
        out_ref[...] = dot(left, cell_ref[: half * n, :])

    back_a = call(
        back_first, sds((width, grid_rows * n), F32), [cell, *near], "back_first", cost=work
    )

    def back_second(cell_ref, a_ref, base_ref, *refs):
        s_refs, out_refs = refs[:half], refs[half:]
        left = jnp.concatenate([r[...] for r in s_refs], axis=1)
        total = a_ref[...] + dot(left, cell_ref[half * n :, :])
        out_refs[0][...] = total[:, :n] + base_ref[...]
        for k in range(1, grid_rows):
            out_refs[k][...] = total[:, k * n : (k + 1) * n].astype(BF16)

    own_back, *back_parts = call(
        back_second,
        [sds((width, n), F32)] + [sds((width, n), BF16)] * (grid_rows - 1),
        [cell, back_a, own_grad, *far],
        "back_second",
        cost=work,
    )
    back_in = [swap(part, "row", k + 1) for k, part in enumerate(back_parts)]

    def finish(own_ref, *refs):
        *in_refs, out_ref = refs
        total = own_ref[...]
        for ref in in_refs:
            total = total + ref[...].astype(F32)
        out_ref[...] = total.T.astype(BF16)

    feat_grad = call(finish, sds((n, width), BF16), [own_back, *back_in], "finish")

    def join(place_ref, mine_ref, other_ref, out_ref):
        x = place_ref[0] & 1
        out_ref[pl.ds(pl.multiple_of(x * piece, piece), piece), :] = mine_ref[:piece]
        out_ref[pl.ds(pl.multiple_of((1 - x) * piece, piece), piece), :] = other_ref[:piece]

    g_half = call(join, sds((width, width), BF16), [place, g_piece, g_other], "join", smem=1)
    g_half_in = swap(g_half, "col", 1)

    def scale(place_ref, a_ref, b_ref, line_ref, self_ref, neigh_ref, bias_ref):
        first = (place_ref[1] & 1) == 0
        a, b = a_ref[...].astype(F32), b_ref[...].astype(F32)
        self_ref[...] = jnp.where(first, a, b) * grad_scale
        neigh_ref[...] = jnp.where(first, b, a) * grad_scale
        bias_ref[...] = line_ref[piece : piece + 1].astype(F32) * grad_scale

    grad_self, grad_neigh, grad_bias = call(
        scale,
        [sds((width, width), F32), sds((width, width), F32), sds((1, width), F32)],
        [place, g_half, g_half_in, g_piece],
        "scale",
        smem=1,
    )
    return hidden, feat_grad, grad_self, grad_neigh, grad_bias.reshape(width)


def on_device(*args):
    node_feats, tiles = args[0], args[5]
    n, width = node_feats.shape
    grid_rows, grid_cols = lax.axis_size("row"), lax.axis_size("col")
    powers = all(s & (s - 1) == 0 and s >= 2 for s in (grid_rows, grid_cols))
    dense_cell = grid_rows * grid_cols <= tiles.shape[2]
    if powers and dense_cell and n == tiles.shape[-1] and n == 128 and width % 256 == 0:
        return direct_form(*args)
    return general_form(*args)


def solution(mesh):
    placed = (
        P(("row", "col"), None),
        P(("row", "col")),
        P(),
        P(),
        P(),
        P("row", "col", None, None, None),
        P("row", "col", None),
        P("row", "col", None),
        P("row", "col"),
        P(("row", "col"), None),
    )
    return jax.shard_map(
        on_device,
        mesh=mesh,
        in_specs=placed,
        out_specs=(P(("row", "col"), None), P(("row", "col"), None), P(), P(), P()),
        check_vma=False,
    )
```

time: 253 us -> 62.3 us (0.25)
  waiting for transfers between devices: 136 us -> 21.4 us
  blocking collectives: 74.8 us -> 0 us
  starting transfers between devices: 0.12 us -> 28.7 us
  matrix products: 15.1 us -> 0 us
  between operations: 14.6 us -> 1.5 us
  Pallas kernels: 0 us -> 7.55 us
  other arithmetic: 6.04 us -> 0.08 us
  local copies, waits for them, and re-layouts: 6.26 us -> 3.09 us
    psum x1 -> x0, waiting for transfers between devices: 69 us -> none  [on_device(): lax.psum((self_term, neigh_term, bias_term), ('row', 'col'))]
    reduce_scatter x2 -> x0, waiting for transfers between devices: 66.5 us -> none  [the longest x1 43.1 us: on_device(): lax.psum_scatter(partial_value.astype(jnp.bfloat16), 'col', scatter_dimen...]
    psum x1 -> x0, blocking collectives: 49.1 us -> none  [on_device(): lax.psum((self_term, neigh_term, bias_term), ('row', 'col'))]
    ppermute x0 -> x25, starting transfers between devices: none -> 28.7 us  [swap(): return lax.ppermute(value, axis, [(i, i ^ distance) for i in range(size)])]
    all_gather x2 -> x0, blocking collectives: 25.7 us -> none  [the longest x1 14.9 us: on_device(): row_stripe = lax.all_gather(spread, 'col', axis=0, tiled=True)]
    ppermute x0 -> x25, waiting for transfers between devices: none -> 21.4 us  [swap(): return lax.ppermute(value, axis, [(i, i ^ distance) for i in range(size)])]
    dot_general x14 -> x0, matrix products: 15.1 us -> none  [the longest x4 3.41 us: advance(): return running + jnp.einsum('kl,kaf->laf', table, products)]
    pallas_call x0 -> x16, Pallas kernels: none -> 7.55 us  [the longest x15 6.33 us: call(): pl.pallas_call(body, out_shape=outs, in_specs=in_specs, out_specs=[pl.Blo...]
  transfers between devices with their start and end apart: 3 -> 25, of which waited for: 3 -> 13; matrix products, arithmetic and copies ran while one was open for 5% -> 0% of each run, Pallas kernels for 0% -> 6%
where the time goes in v1:
time: 62.3 us
  starting transfers between devices  28.7 us (46%)
  waiting for transfers between devices  21.4 us (34%)
  Pallas kernels  7.55 us (12%)
  local copies, waits for them, and re-layouts  3.09 us (5%)
  between operations  1.5 us (2%)
    ppermute x25, starting transfers between devices, swap(): return lax.ppermute(value, axis, [(i, i ^ distance) for i in range(size)])  28.7 us
    ppermute x25, waiting for transfers between devices, swap(): return lax.ppermute(value, axis, [(i, i ^ distance) for i in range(size)])  21.4 us
    pallas_call x15, Pallas kernels, call(): pl.pallas_call(body, out_shape=outs, in_specs=in_specs, out_specs=[pl.Blo...  6.33 us
    unnamed x18, local copies, waits for them, and re-layouts  3.09 us
  transfers between devices with their start and end apart: 25, of which 13 were waited for; matrix products, arithmetic and copies ran while one was open for 0% of the time, Pallas kernels for 6%

profile of v1, /device:TPU:0, one launch (start us, length us, event | category | flops | bytes accessed | tf_op | source)
XLA Modules:
  0.0 62.3 jit_solution(6118316980384175486)
XLA Ops:
  0.6 3.0 %collective-permute-start = (bf16[128,256]{1,0:T(8,128)(2,1)}, bf16[128,256]{1,0:T(8,128)(2,1)S(1)}, u32[]{:S(2)}, u32[]{:S(2)}) collective-permute-start(bf16[128,256]{1,0:T(8,128)(2,1)} %x_ref.3), channel_id=1, source_target_pairs={{0,8},{8,0},{16,24},{24,16},{1,9},{9,1},{17,25},{25,17},{2,10},{10... | collective-permute-start | bytes 196616 | tf_op jit(solution)/shard_map/ppermute | solution.py:193
  3.7 1.5 %collective-permute-start.1 = (bf16[128,256]{1,0:T(8,128)(2,1)}, bf16[128,256]{1,0:T(8,128)(2,1)S(1)}, u32[]{:S(2)}, u32[]{:S(2)}) collective-permute-start(bf16[128,256]{1,0:T(8,128)(2,1)} %x_ref.3), channel_id=1, source_target_pairs={{0,16},{8,24},{16,0},{24,8},{1,17},{9,25},{17,1},{25,9},{2,18},{10... | collective-permute-start | bytes 196616 | tf_op jit(solution)/shard_map/ppermute | solution.py:193
  5.9 1.7 %copy-done = bf16[1,1,80,128,128]{4,3,2,1,0:T(8,128)(2,1)S(1)} copy-done((bf16[1,1,80,128,128]{4,3,2,1,0:T(8,128)(2,1)S(1)}, bf16[1,1,80,128,128]{4,3,2,1,0:T(8,128)(2,1)}, u32[]{:S(2)}) %copy-start) | copy-done | bytes 2621464
  12.5 1.9 %collective-permute-start.4 = (bf16[128,256]{1,0:T(8,128)(2,1)S(1)}, bf16[128,256]{1,0:T(8,128)(2,1)S(1)}, u32[]{:S(2)}, u32[]{:S(2)}) collective-permute-start(bf16[128,256]{1,0:T(8,128)(2,1)S(1)} %get-tuple-element.29), channel_id=1, source_target_pairs={{0,2},{1,3},{2,0},{3,1},{4,6},{5,7},{6,4},{7,5},{8,10},{9,11},{10,... | collective-permute-start | bytes 196616 | tf_op jit(solution)/shard_map/ppermute | solution.py:193
  14.4 2.6 %collective-permute-start.5 = (bf16[128,256]{1,0:T(8,128)(2,1)S(1)}, bf16[128,256]{1,0:T(8,128)(2,1)S(1)}, u32[]{:S(2)}, u32[]{:S(2)}) collective-permute-start(bf16[128,256]{1,0:T(8,128)(2,1)S(1)} %get-tuple-element.30), channel_id=1, source_target_pairs={{0,4},{1,5},{2,6},{3,7},{4,0},{5,1},{6,2},{7,3},{8,12},{9,13},{10,... | collective-permute-start | bytes 196616 | tf_op jit(solution)/shard_map/ppermute | solution.py:193
  17.9 2.4 %collective-permute-done.5.refs_1_ = bf16[128,256]{1,0:T(8,128)(2,1)S(1)} collective-permute-done((bf16[128,256]{1,0:T(8,128)(2,1)S(1)}, bf16[128,256]{1,0:T(8,128)(2,1)S(1)}, u32[]{:S(2)}, u32[]{:S(2)}) %collective-permute-start.5) | collective-permute-done | bytes 65568 | tf_op jit(solution)/shard_map/ppermute | solution.py:193
  20.3 2.8 %collective-permute-done.6.refs_2_ = bf16[128,256]{1,0:T(8,128)(2,1)S(1)} collective-permute-done((bf16[128,256]{1,0:T(8,128)(2,1)S(1)}, bf16[128,256]{1,0:T(8,128)(2,1)S(1)}, u32[]{:S(2)}, u32[]{:S(2)}) %collective-permute-start.6) | collective-permute-done | bytes 65568 | tf_op jit(solution)/shard_map/ppermute | solution.py:193
  24.7 1.4 %collective-permute-done.17.b_ref = bf16[272,256]{1,0:T(8,128)(2,1)S(1)} collective-permute-done((bf16[272,256]{1,0:T(8,128)(2,1)S(1)}, bf16[272,256]{1,0:T(8,128)(2,1)S(1)}, u32[]{:S(2)}, u32[]{:S(2)}) %collective-permute-start.17) | collective-permute-done | bytes 139296 | tf_op jit(solution)/shard_map/ppermute | solution.py:193
  26.6 1.8 %collective-permute-start.18 = (bf16[144,256]{1,0:T(8,128)(2,1)S(1)}, bf16[144,256]{1,0:T(8,128)(2,1)S(1)}, u32[]{:S(2)}, u32[]{:S(2)}) collective-permute-start(bf16[144,256]{1,0:T(8,128)(2,1)S(1)} %get-tuple-element.47), channel_id=1, source_target_pairs={{0,8},{8,0},{16,24},{24,16},{1,9},{9,1},{17,25},{25,17},{2,10},{10... | collective-permute-start | bytes 221192 | tf_op jit(solution)/shard_map/ppermute | solution.py:193
  28.4 2.7 %collective-permute-done.18.b_ref = bf16[144,256]{1,0:T(8,128)(2,1)S(1)} collective-permute-done((bf16[144,256]{1,0:T(8,128)(2,1)S(1)}, bf16[144,256]{1,0:T(8,128)(2,1)S(1)}, u32[]{:S(2)}, u32[]{:S(2)}) %collective-permute-start.18) | collective-permute-done | bytes 73760 | tf_op jit(solution)/shard_map/ppermute | solution.py:193
  31.1 1.6 %collective-permute-start.19 = (bf16[144,256]{1,0:T(8,128)(2,1)S(1)}, bf16[144,256]{1,0:T(8,128)(2,1)S(1)}, u32[]{:S(2)}, u32[]{:S(2)}) collective-permute-start(bf16[144,256]{1,0:T(8,128)(2,1)S(1)} %add_x.1.a_ref), channel_id=1, source_target_pairs={{0,16},{8,24},{16,0},{24,8},{1,17},{9,25},{17,1},{25,9},{2,18},{10... | collective-permute-start | bytes 221192 | tf_op jit(solution)/shard_map/ppermute | solution.py:193
  32.7 2.8 %collective-permute-done.19.b_ref = bf16[144,256]{1,0:T(8,128)(2,1)S(1)} collective-permute-done((bf16[144,256]{1,0:T(8,128)(2,1)S(1)}, bf16[144,256]{1,0:T(8,128)(2,1)S(1)}, u32[]{:S(2)}, u32[]{:S(2)}) %collective-permute-start.19) | collective-permute-done | bytes 73760 | tf_op jit(solution)/shard_map/ppermute | solution.py:193
  35.5 1.3 %collective-permute-start.20 = (bf16[144,256]{1,0:T(8,128)(2,1)S(1)}, bf16[144,256]{1,0:T(8,128)(2,1)S(1)}, u32[]{:S(2)}, u32[]{:S(2)}) collective-permute-start(bf16[144,256]{1,0:T(8,128)(2,1)S(1)} %add_y.1.refs_0_), channel_id=1, source_target_pairs={{0,2},{1,3},{2,0},{3,1},{4,6},{5,7},{6,4},{7,5},{8,10},{9,11},{10,... | collective-permute-start | bytes 221192 | tf_op jit(solution)/shard_map/ppermute | solution.py:193
  36.8 1.8 %collective-permute-start.21 = (bf16[144,256]{1,0:T(8,128)(2,1)S(1)}, bf16[144,256]{1,0:T(8,128)(2,1)S(1)}, u32[]{:S(2)}, u32[]{:S(2)}) collective-permute-start(bf16[144,256]{1,0:T(8,128)(2,1)S(1)} %add_y.1.refs_0_), channel_id=1, source_target_pairs={{0,4},{1,5},{2,6},{3,7},{4,0},{5,1},{6,2},{7,3},{8,12},{9,13},{10,... | collective-permute-start | bytes 221192 | tf_op jit(solution)/shard_map/ppermute | solution.py:193
  38.6 1.3 %collective-permute-start.22 = (bf16[144,256]{1,0:T(8,128)(2,1)S(1)}, bf16[144,256]{1,0:T(8,128)(2,1)S(1)}, u32[]{:S(2)}, u32[]{:S(2)}) collective-permute-start(bf16[144,256]{1,0:T(8,128)(2,1)S(1)} %add_y.1.refs_0_), channel_id=1, source_target_pairs={{0,6},{1,7},{2,4},{3,5},{4,2},{5,3},{6,0},{7,1},{8,14},{9,15},{10,... | collective-permute-start | bytes 221192 | tf_op jit(solution)/shard_map/ppermute | solution.py:193
  40.3 2.7 %collective-permute-start.8 = (bf16[256,128]{1,0:T(8,128)(2,1)S(1)}, bf16[256,128]{1,0:T(8,128)(2,1)S(1)}, u32[]{:S(2)}, u32[]{:S(2)}) collective-permute-start(bf16[256,128]{1,0:T(8,128)(2,1)S(1)} %get-tuple-element.38.refs_0_), channel_id=1, source_target_pairs={{0,4},{1,5},{2,6},{3,7},{4,0},{5,1},{6,2},{7,3},{8,12},{9,13},{10,... | collective-permute-start | bytes 196616 | tf_op jit(solution)/shard_map/ppermute | solution.py:193
  43.0 1.9 %collective-permute-start.9 = (bf16[256,128]{1,0:T(8,128)(2,1)S(1)}, bf16[256,128]{1,0:T(8,128)(2,1)S(1)}, u32[]{:S(2)}, u32[]{:S(2)}) collective-permute-start(bf16[256,128]{1,0:T(8,128)(2,1)S(1)} %get-tuple-element.38.refs_0_), channel_id=1, source_target_pairs={{0,6},{1,7},{2,4},{3,5},{4,2},{5,3},{6,0},{7,1},{8,14},{9,15},{10,... | collective-permute-start | bytes 196616 | tf_op jit(solution)/shard_map/ppermute | solution.py:193
  45.9 1.4 %collective-permute-start.23 = (bf16[144,256]{1,0:T(8,128)(2,1)S(1)}, bf16[144,256]{1,0:T(8,128)(2,1)S(1)}, u32[]{:S(2)}, u32[]{:S(2)}) collective-permute-start(bf16[144,256]{1,0:T(8,128)(2,1)S(1)} %add_z.1.mine_ref.line_ref), channel_id=1, source_target_pairs={{0,8},{8,0},{16,24},{24,16},{1,9},{9,1},{17,25},{25,17},{2,10},{10... | collective-permute-start | bytes 221192 | tf_op jit(solution)/shard_map/ppermute | solution.py:193
  47.9 1.6 %collective-permute-done.8.refs_2_ = bf16[256,128]{1,0:T(8,128)(2,1)S(1)} collective-permute-done((bf16[256,128]{1,0:T(8,128)(2,1)S(1)}, bf16[256,128]{1,0:T(8,128)(2,1)S(1)}, u32[]{:S(2)}, u32[]{:S(2)}) %collective-permute-start.8) | collective-permute-done | bytes 65568 | tf_op jit(solution)/shard_map/ppermute | solution.py:193
  51.6 1.4 %collective-permute-start.14 = (bf16[256,128]{1,0:T(8,128)(2,1)S(1)}, bf16[256,128]{1,0:T(8,128)(2,1)S(1)}, u32[]{:S(2)}, u32[]{:S(2)}) collective-permute-start(bf16[256,128]{1,0:T(8,128)(2,1)S(1)} %get-tuple-element.41), channel_id=1, source_target_pairs={{0,8},{8,0},{16,24},{24,16},{1,9},{9,1},{17,25},{25,17},{2,10},{10... | collective-permute-start | bytes 196616 | tf_op jit(solution)/shard_map/ppermute | solution.py:193
  53.1 2.0 %collective-permute-start.15 = (bf16[256,128]{1,0:T(8,128)(2,1)S(1)}, bf16[256,128]{1,0:T(8,128)(2,1)S(1)}, u32[]{:S(2)}, u32[]{:S(2)}) collective-permute-start(bf16[256,128]{1,0:T(8,128)(2,1)S(1)} %get-tuple-element.42), channel_id=1, source_target_pairs={{0,16},{8,24},{16,0},{24,8},{1,17},{9,25},{17,1},{25,9},{2,18},{10... | collective-permute-start | bytes 196616 | tf_op jit(solution)/shard_map/ppermute | solution.py:193
  56.2 2.1 %collective-permute-done.15.refs_1_ = bf16[256,128]{1,0:T(8,128)(2,1)S(1)} collective-permute-done((bf16[256,128]{1,0:T(8,128)(2,1)S(1)}, bf16[256,128]{1,0:T(8,128)(2,1)S(1)}, u32[]{:S(2)}, u32[]{:S(2)}) %collective-permute-start.15) | collective-permute-done | bytes 65568 | tf_op jit(solution)/shard_map/ppermute | solution.py:193
  58.3 1.9 %collective-permute-done.16.refs_2_ = bf16[256,128]{1,0:T(8,128)(2,1)S(1)} collective-permute-done((bf16[256,128]{1,0:T(8,128)(2,1)S(1)}, bf16[256,128]{1,0:T(8,128)(2,1)S(1)}, u32[]{:S(2)}, u32[]{:S(2)}) %collective-permute-start.16) | collective-permute-done | bytes 65568 | tf_op jit(solution)/shard_map/ppermute | solution.py:193
  60.9 1.4 %scale.1 = (f32[256,256]{1,0:T(8,128)}, f32[256,256]{1,0:T(8,128)}, f32[1,256]{1,0:T(1,128)}) custom-call(s32[3]{0:T(128)S(1)} %pad_add_fusion.place_ref, bf16[256,256]{1,0:T(8,128)(2,1)S(1)} %join.1.a_ref, bf16[256,256]{1,0:T(8,128)(2,1)S(1)} %collective-permute-done.24.b_ref, bf16[144,256]{1,0:T(8,128)(2,1)S(1)} %add_z.1.mine_ref.line_ref), custom_call_target="tpu_custom_call" | custom-call | flops 1048576 | bytes 262144 | tf_op jit(solution)/shard_map/scale/pallas_call | solution.py:126
  (61 shorter events, 13.9 us)
Async XLA Ops:
  0.6 9.7 %collective-permute-start = (bf16[128,256]{1,0:T(8,128)(2,1)}, bf16[128,256]{1,0:T(8,128)(2,1)S(1)}, u32[]{:S(2)}, u32[]{:S(2)}) collective-permute-start(bf16[128,256]{1,0:T(8,128)(2,1)} %x_ref.3), channel_id=1, source_target_pairs={{0,8},{8,0},{16,24},{24,16},{1,9},{9,1},{17,25},{25,17},{2,10},{10... | collective-permute-start | bytes 196616 | tf_op jit(solution)/shard_map/ppermute | solution.py:193
  3.7 6.6 %collective-permute-start.1 = (bf16[128,256]{1,0:T(8,128)(2,1)}, bf16[128,256]{1,0:T(8,128)(2,1)S(1)}, u32[]{:S(2)}, u32[]{:S(2)}) collective-permute-start(bf16[128,256]{1,0:T(8,128)(2,1)} %x_ref.3), channel_id=1, source_target_pairs={{0,16},{8,24},{16,0},{24,8},{1,17},{9,25},{17,1},{25,9},{2,18},{10... | collective-permute-start | bytes 196616 | tf_op jit(solution)/shard_map/ppermute | solution.py:193
  5.2 5.4 %collective-permute-start.2 = (bf16[128,256]{1,0:T(8,128)(2,1)}, bf16[128,256]{1,0:T(8,128)(2,1)S(1)}, u32[]{:S(2)}, u32[]{:S(2)}) collective-permute-start(bf16[128,256]{1,0:T(8,128)(2,1)} %x_ref.3), channel_id=1, source_target_pairs={{0,24},{8,16},{16,8},{24,0},{1,25},{9,17},{17,9},{25,1},{2,26},{10... | collective-permute-start | bytes 196616 | tf_op jit(solution)/shard_map/ppermute | solution.py:193
  10.9 1.6 %collective-permute-start.3 = (bf16[512,256]{1,0:T(8,128)(2,1)S(1)}, bf16[512,256]{1,0:T(8,128)(2,1)S(1)}, u32[]{:S(2)}, u32[]{:S(2)}) collective-permute-start(bf16[512,256]{1,0:T(8,128)(2,1)S(1)} %forward_sent.1), channel_id=1, source_target_pairs={{0,1},{1,0},{2,3},{3,2},{4,5},{5,4},{6,7},{7,6},{8,9},{9,8},{10,11... | collective-permute-start | bytes 786440 | tf_op jit(solution)/shard_map/ppermute | solution.py:193
  12.5 5.4 %collective-permute-start.4 = (bf16[128,256]{1,0:T(8,128)(2,1)S(1)}, bf16[128,256]{1,0:T(8,128)(2,1)S(1)}, u32[]{:S(2)}, u32[]{:S(2)}) collective-permute-start(bf16[128,256]{1,0:T(8,128)(2,1)S(1)} %get-tuple-element.29), channel_id=1, source_target_pairs={{0,2},{1,3},{2,0},{3,1},{4,6},{5,7},{6,4},{7,5},{8,10},{9,11},{10,... | collective-permute-start | bytes 196616 | tf_op jit(solution)/shard_map/ppermute | solution.py:193
  14.4 5.9 %collective-permute-start.5 = (bf16[128,256]{1,0:T(8,128)(2,1)S(1)}, bf16[128,256]{1,0:T(8,128)(2,1)S(1)}, u32[]{:S(2)}, u32[]{:S(2)}) collective-permute-start(bf16[128,256]{1,0:T(8,128)(2,1)S(1)} %get-tuple-element.30), channel_id=1, source_target_pairs={{0,4},{1,5},{2,6},{3,7},{4,0},{5,1},{6,2},{7,3},{8,12},{9,13},{10,... | collective-permute-start | bytes 196616 | tf_op jit(solution)/shard_map/ppermute | solution.py:193
  17.0 6.1 %collective-permute-start.6 = (bf16[128,256]{1,0:T(8,128)(2,1)S(1)}, bf16[128,256]{1,0:T(8,128)(2,1)S(1)}, u32[]{:S(2)}, u32[]{:S(2)}) collective-permute-start(bf16[128,256]{1,0:T(8,128)(2,1)S(1)} %get-tuple-element.31), channel_id=1, source_target_pairs={{0,6},{1,7},{2,4},{3,5},{4,2},{5,3},{6,0},{7,1},{8,14},{9,15},{10,... | collective-permute-start | bytes 196616 | tf_op jit(solution)/shard_map/ppermute | solution.py:193
  26.6 4.4 %collective-permute-start.18 = (bf16[144,256]{1,0:T(8,128)(2,1)S(1)}, bf16[144,256]{1,0:T(8,128)(2,1)S(1)}, u32[]{:S(2)}, u32[]{:S(2)}) collective-permute-start(bf16[144,256]{1,0:T(8,128)(2,1)S(1)} %get-tuple-element.47), channel_id=1, source_target_pairs={{0,8},{8,0},{16,24},{24,16},{1,9},{9,1},{17,25},{25,17},{2,10},{10... | collective-permute-start | bytes 221192 | tf_op jit(solution)/shard_map/ppermute | solution.py:193
  31.1 4.4 %collective-permute-start.19 = (bf16[144,256]{1,0:T(8,128)(2,1)S(1)}, bf16[144,256]{1,0:T(8,128)(2,1)S(1)}, u32[]{:S(2)}, u32[]{:S(2)}) collective-permute-start(bf16[144,256]{1,0:T(8,128)(2,1)S(1)} %add_x.1.a_ref), channel_id=1, source_target_pairs={{0,16},{8,24},{16,0},{24,8},{1,17},{9,25},{17,1},{25,9},{2,18},{10... | collective-permute-start | bytes 221192 | tf_op jit(solution)/shard_map/ppermute | solution.py:193
  35.5 7.5 %collective-permute-start.20 = (bf16[144,256]{1,0:T(8,128)(2,1)S(1)}, bf16[144,256]{1,0:T(8,128)(2,1)S(1)}, u32[]{:S(2)}, u32[]{:S(2)}) collective-permute-start(bf16[144,256]{1,0:T(8,128)(2,1)S(1)} %add_y.1.refs_0_), channel_id=1, source_target_pairs={{0,2},{1,3},{2,0},{3,1},{4,6},{5,7},{6,4},{7,5},{8,10},{9,11},{10,... | collective-permute-start | bytes 221192 | tf_op jit(solution)/shard_map/ppermute | solution.py:193
  36.8 9.0 %collective-permute-start.21 = (bf16[144,256]{1,0:T(8,128)(2,1)S(1)}, bf16[144,256]{1,0:T(8,128)(2,1)S(1)}, u32[]{:S(2)}, u32[]{:S(2)}) collective-permute-start(bf16[144,256]{1,0:T(8,128)(2,1)S(1)} %add_y.1.refs_0_), channel_id=1, source_target_pairs={{0,4},{1,5},{2,6},{3,7},{4,0},{5,1},{6,2},{7,3},{8,12},{9,13},{10,... | collective-permute-start | bytes 221192 | tf_op jit(solution)/shard_map/ppermute | solution.py:193
  38.6 7.2 %collective-permute-start.22 = (bf16[144,256]{1,0:T(8,128)(2,1)S(1)}, bf16[144,256]{1,0:T(8,128)(2,1)S(1)}, u32[]{:S(2)}, u32[]{:S(2)}) collective-permute-start(bf16[144,256]{1,0:T(8,128)(2,1)S(1)} %add_y.1.refs_0_), channel_id=1, source_target_pairs={{0,6},{1,7},{2,4},{3,5},{4,2},{5,3},{6,0},{7,1},{8,14},{9,15},{10,... | collective-permute-start | bytes 221192 | tf_op jit(solution)/shard_map/ppermute | solution.py:193
  39.9 7.4 %collective-permute-start.7 = (bf16[256,128]{1,0:T(8,128)(2,1)S(1)}, bf16[256,128]{1,0:T(8,128)(2,1)S(1)}, u32[]{:S(2)}, u32[]{:S(2)}) collective-permute-start(bf16[256,128]{1,0:T(8,128)(2,1)S(1)} %get-tuple-element.38.refs_0_), channel_id=1, source_target_pairs={{0,2},{1,3},{2,0},{3,1},{4,6},{5,7},{6,4},{7,5},{8,10},{9,11},{10,... | collective-permute-start | bytes 196616 | tf_op jit(solution)/shard_map/ppermute | solution.py:193
  40.3 9.1 %collective-permute-start.8 = (bf16[256,128]{1,0:T(8,128)(2,1)S(1)}, bf16[256,128]{1,0:T(8,128)(2,1)S(1)}, u32[]{:S(2)}, u32[]{:S(2)}) collective-permute-start(bf16[256,128]{1,0:T(8,128)(2,1)S(1)} %get-tuple-element.38.refs_0_), channel_id=1, source_target_pairs={{0,4},{1,5},{2,6},{3,7},{4,0},{5,1},{6,2},{7,3},{8,12},{9,13},{10,... | collective-permute-start | bytes 196616 | tf_op jit(solution)/shard_map/ppermute | solution.py:193
  43.0 6.5 %collective-permute-start.9 = (bf16[256,128]{1,0:T(8,128)(2,1)S(1)}, bf16[256,128]{1,0:T(8,128)(2,1)S(1)}, u32[]{:S(2)}, u32[]{:S(2)}) collective-permute-start(bf16[256,128]{1,0:T(8,128)(2,1)S(1)} %get-tuple-element.38.refs_0_), channel_id=1, source_target_pairs={{0,6},{1,7},{2,4},{3,5},{4,2},{5,3},{6,0},{7,1},{8,14},{9,15},{10,... | collective-permute-start | bytes 196616 | tf_op jit(solution)/shard_map/ppermute | solution.py:193
  45.9 4.4 %collective-permute-start.23 = (bf16[144,256]{1,0:T(8,128)(2,1)S(1)}, bf16[144,256]{1,0:T(8,128)(2,1)S(1)}, u32[]{:S(2)}, u32[]{:S(2)}) collective-permute-start(bf16[144,256]{1,0:T(8,128)(2,1)S(1)} %add_z.1.mine_ref.line_ref), channel_id=1, source_target_pairs={{0,8},{8,0},{16,24},{24,16},{1,9},{9,1},{17,25},{25,17},{2,10},{10... | collective-permute-start | bytes 221192 | tf_op jit(solution)/shard_map/ppermute | solution.py:193
  47.4 3.9 %collective-permute-start.10 = (bf16[256,128]{1,0:T(8,128)(2,1)S(1)}, bf16[256,128]{1,0:T(8,128)(2,1)S(1)}, u32[]{:S(2)}, u32[]{:S(2)}) collective-permute-start(bf16[256,128]{1,0:T(8,128)(2,1)S(1)} %get-tuple-element.38.refs_0_), channel_id=1, source_target_pairs={{0,1},{1,0},{2,3},{3,2},{4,5},{5,4},{6,7},{7,6},{8,9},{9,8},{10,11... | collective-permute-start | bytes 196616 | tf_op jit(solution)/shard_map/ppermute | solution.py:193
  47.4 3.9 %collective-permute-start.11 = (bf16[256,128]{1,0:T(8,128)(2,1)S(1)}, bf16[256,128]{1,0:T(8,128)(2,1)S(1)}, u32[]{:S(2)}, u32[]{:S(2)}) collective-permute-start(bf16[256,128]{1,0:T(8,128)(2,1)S(1)} %collective-permute-done.7.refs_1_), channel_id=1, source_target_pairs={{0,1},{1,0},{2,3},{3,2},{4,5},{5,4},{6,7},{7,6},{8,9},{9,8},{10,11... | collective-permute-start | bytes 196616 | tf_op jit(solution)/shard_map/ppermute | solution.py:193
  49.5 1.8 %collective-permute-start.12 = (bf16[256,128]{1,0:T(8,128)(2,1)S(1)}, bf16[256,128]{1,0:T(8,128)(2,1)S(1)}, u32[]{:S(2)}, u32[]{:S(2)}) collective-permute-start(bf16[256,128]{1,0:T(8,128)(2,1)S(1)} %collective-permute-done.8.refs_2_), channel_id=1, source_target_pairs={{0,1},{1,0},{2,3},{3,2},{4,5},{5,4},{6,7},{7,6},{8,9},{9,8},{10,11... | collective-permute-start | bytes 196616 | tf_op jit(solution)/shard_map/ppermute | solution.py:193
  49.5 1.8 %collective-permute-start.13 = (bf16[256,128]{1,0:T(8,128)(2,1)S(1)}, bf16[256,128]{1,0:T(8,128)(2,1)S(1)}, u32[]{:S(2)}, u32[]{:S(2)}) collective-permute-start(bf16[256,128]{1,0:T(8,128)(2,1)S(1)} %collective-permute-done.9.refs_3_), channel_id=1, source_target_pairs={{0,1},{1,0},{2,3},{3,2},{4,5},{5,4},{6,7},{7,6},{8,9},{9,8},{10,11... | collective-permute-start | bytes 196616 | tf_op jit(solution)/shard_map/ppermute | solution.py:193
  50.9 10.0 %collective-permute-start.24 = (bf16[256,256]{1,0:T(8,128)(2,1)S(1)}, bf16[256,256]{1,0:T(8,128)(2,1)S(1)}, u32[]{:S(2)}, u32[]{:S(2)}) collective-permute-start(bf16[256,256]{1,0:T(8,128)(2,1)S(1)} %join.1.a_ref), channel_id=1, source_target_pairs={{0,1},{1,0},{2,3},{3,2},{4,5},{5,4},{6,7},{7,6},{8,9},{9,8},{10,11... | collective-permute-start | bytes 393224 | tf_op jit(solution)/shard_map/ppermute | solution.py:193
  51.6 4.6 %collective-permute-start.14 = (bf16[256,128]{1,0:T(8,128)(2,1)S(1)}, bf16[256,128]{1,0:T(8,128)(2,1)S(1)}, u32[]{:S(2)}, u32[]{:S(2)}) collective-permute-start(bf16[256,128]{1,0:T(8,128)(2,1)S(1)} %get-tuple-element.41), channel_id=1, source_target_pairs={{0,8},{8,0},{16,24},{24,16},{1,9},{9,1},{17,25},{25,17},{2,10},{10... | collective-permute-start | bytes 196616 | tf_op jit(solution)/shard_map/ppermute | solution.py:193
  53.1 5.2 %collective-permute-start.15 = (bf16[256,128]{1,0:T(8,128)(2,1)S(1)}, bf16[256,128]{1,0:T(8,128)(2,1)S(1)}, u32[]{:S(2)}, u32[]{:S(2)}) collective-permute-start(bf16[256,128]{1,0:T(8,128)(2,1)S(1)} %get-tuple-element.42), channel_id=1, source_target_pairs={{0,16},{8,24},{16,0},{24,8},{1,17},{9,25},{17,1},{25,9},{2,18},{10... | collective-permute-start | bytes 196616 | tf_op jit(solution)/shard_map/ppermute | solution.py:193
  55.0 5.2 %collective-permute-start.16 = (bf16[256,128]{1,0:T(8,128)(2,1)S(1)}, bf16[256,128]{1,0:T(8,128)(2,1)S(1)}, u32[]{:S(2)}, u32[]{:S(2)}) collective-permute-start(bf16[256,128]{1,0:T(8,128)(2,1)S(1)} %get-tuple-element.43), channel_id=1, source_target_pairs={{0,24},{8,16},{16,8},{24,0},{1,25},{9,17},{17,9},{25,1},{2,26},{10... | collective-permute-start | bytes 196616 | tf_op jit(solution)/shard_map/ppermute | solution.py:193
  (10 other events, 54.1 us)

commit v2 on v1

--- a/solution.py
+++ b/solution.py
@@ -115,24 +115,27 @@
     return jax.ShapeDtypeStruct(shape, dtype)
 
 
-def call(body, outs, args, name, smem=0, scratch=(), cost=None, grid=None, in_specs=None):
+def call(kernel, outs, args, name, smem=0, after=(), cost=None):
     single = not isinstance(outs, (list, tuple))
     outs = [outs] if single else list(outs)
-    if in_specs is None:
-        in_specs = [pl.BlockSpec(memory_space=pltpu.SMEM)] * smem + [
-            pl.BlockSpec(memory_space=pltpu.VMEM)
-        ] * (len(args) - smem)
+    count = len(args)
+    in_specs = [pl.BlockSpec(memory_space=pltpu.SMEM)] * smem
+    in_specs += [pl.BlockSpec(memory_space=pltpu.VMEM)] * (count - smem)
+    in_specs += [pl.BlockSpec(memory_space=pl.ANY)] * len(after)
+
+    def body(*refs):
+        kernel(*refs[:count], *refs[count + len(after) :])
+
     flops, moved = cost or (1 << 20, 1 << 18)
     result = pl.pallas_call(
         body,
         out_shape=outs,
         in_specs=in_specs,
         out_specs=[pl.BlockSpec(memory_space=pltpu.VMEM)] * len(outs),
-        scratch_shapes=list(scratch),
         compiler_params=pltpu.CompilerParams(vmem_limit_bytes=24 << 20),
         cost_estimate=pl.CostEstimate(flops=flops, bytes_accessed=moved, transcendentals=0),
         name=name,
-    )(*args)
+    )(*args, *after)
     return result[0] if single else result
 
 
@@ -140,57 +143,80 @@
     return jnp.dot(a, b, preferred_element_type=F32)
 
 
-def build_cell(place, tile_rows, tile_cols, tiles, grid_rows, grid_cols):
+def build_cell(place, tile_counts, tile_rows, tile_cols, tiles, grid_rows, grid_cols):
     total, edge = tiles.shape[0], tiles.shape[-1]
     group = 16 if total % 16 == 0 else total
+    groups = total // group
     half = grid_cols // 2
 
-    def body(place_ref, rows_ref, cols_ref, tiles_ref, cell_ref, sums):
-        step = pl.program_id(0)
-
-        @pl.when(step == 0)
-        def _():
-            sums[...] = jnp.zeros_like(sums)
-
-        my_row, my_col, count = place_ref[0], place_ref[1], place_ref[2]
-        first = step * group
+    def body(place_ref, *refs):
+        count_ref, rows_hbm, cols_hbm, tiles_hbm, cell_ref = refs[:5]
+        sums, vals, rows, cols, sems = refs[5:]
+        copies = [
+            pltpu.make_async_copy(rows_hbm, rows, sems.at[groups]),
+            pltpu.make_async_copy(cols_hbm, cols, sems.at[groups + 1]),
+        ]
+        for g in range(groups):
+            span = pl.ds(g * group, group)
+            copies.append(pltpu.make_async_copy(tiles_hbm.at[span], vals.at[span], sems.at[g]))
+        for copy in copies:
+            copy.start()
+        sums[...] = jnp.zeros_like(sums)
+        my_row, my_col = place_ref[0], place_ref[1]
 
         def add_tile(k, carry):
-            near = rows_ref[first + k] ^ my_col
-            far = cols_ref[first + k] ^ my_row
+            near = rows[k] ^ my_col
+            far = cols[k] ^ my_row
             slot = ((near >> 1) + half * (near & 1)) * grid_rows + far
-            sums[slot] += tiles_ref[k].astype(F32)
+            sums[slot] += vals[k].astype(F32)
             return carry
 
-        lax.fori_loop(0, jnp.clip(count - first, 0, group), add_tile, 0)
-
-        @pl.when(step == pl.num_programs(0) - 1)
-        def _():
-            for i in range(grid_cols):
-                for j in range(grid_rows):
-                    cell_ref[i * edge : (i + 1) * edge, j * edge : (j + 1) * edge] = sums[
-                        i * grid_rows + j
-                    ].astype(BF16)
-
-    smem = pl.BlockSpec(memory_space=pltpu.SMEM)
+        copies[0].wait()
+        copies[1].wait()
+        count = count_ref[0, 0]
+        for g in range(groups):
+            copies[2 + g].wait()
+            lax.fori_loop(g * group, jnp.clip(count, g * group, (g + 1) * group), add_tile, 0)
+        for i in range(grid_cols):
+            for j in range(grid_rows):
+                cell_ref[i * edge : (i + 1) * edge, j * edge : (j + 1) * edge] = sums[
+                    i * grid_rows + j
+                ].astype(BF16)
+
+    held = pl.BlockSpec(memory_space=pltpu.HBM)
+    stored = [
+        pltpu.with_memory_space_constraint(v, pltpu.HBM)
+        for v in (tile_rows, tile_cols, tiles)
+    ]
     return pl.pallas_call(
         body,
         out_shape=sds((grid_cols * edge, grid_rows * edge), BF16),
-        grid=(total // group,),
-        in_specs=[smem] * 3 + [pl.BlockSpec((group, edge, edge), lambda i: (i, 0, 0))],
-        out_specs=pl.BlockSpec((grid_cols * edge, grid_rows * edge), lambda i: (0, 0)),
-        scratch_shapes=[pltpu.VMEM((grid_rows * grid_cols, edge, edge), F32)],
+        in_specs=[pl.BlockSpec(memory_space=pltpu.SMEM)] * 2 + [held] * 3,
+        out_specs=pl.BlockSpec(memory_space=pltpu.VMEM),
+        scratch_shapes=[
+            pltpu.VMEM((grid_rows * grid_cols, edge, edge), F32),
+            pltpu.VMEM((total, edge, edge), BF16),
+            pltpu.SMEM((total,), jnp.int32),
+            pltpu.SMEM((total,), jnp.int32),
+            pltpu.SemaphoreType.DMA((groups + 2,)),
+        ],
         compiler_params=pltpu.CompilerParams(vmem_limit_bytes=24 << 20),
         cost_estimate=pl.CostEstimate(
             flops=1 << 24, bytes_accessed=4 * total * edge * edge, transcendentals=0
         ),
         name="build_cell",
-    )(place, tile_rows, tile_cols, tiles)
+    )(place, tile_counts, *stored)
 
 
 def swap(value, axis, distance):
     size = lax.axis_size(axis)
     return lax.ppermute(value, axis, [(i, i ^ distance) for i in range(size)])
+
+
+def swap_corner(value):
+    size = lax.axis_size("row") * lax.axis_size("col")
+    step = lax.axis_size("col") + 1
+    return lax.ppermute(value, ("row", "col"), [(i, i ^ step) for i in range(size)])
 
 
 def direct_form(
@@ -210,11 +236,13 @@
     half = grid_cols // 2
     n, width = node_feats.shape
     grad_scale = 1.0 / math.sqrt(grid_rows * grid_cols * n)
-    place = jnp.stack([lax.axis_index("row"), lax.axis_index("col"), tile_counts[0, 0]])
+    place = jnp.stack([lax.axis_index("row"), lax.axis_index("col")])
 
     feats = [node_feats] + [swap(node_feats, "row", k) for k in range(1, grid_rows)]
 
-    cell = build_cell(place, tile_rows[0, 0], tile_cols[0, 0], tiles[0, 0], grid_rows, grid_cols)
+    cell = build_cell(
+        place, tile_counts, tile_rows[0, 0], tile_cols[0, 0], tiles[0, 0], grid_rows, grid_cols
+    )
 
     def prepare(x_ref, w_ref, b_ref, d_ref, pre_ref, deg_ref, degrow_ref):
         pre_ref[...] = dot(x_ref[...], w_ref[...]) + b_ref[...]
@@ -268,84 +296,65 @@
     )
     parts_in = [swap(part, "col", 2 * (q + 1)) for q, part in enumerate(parts)]
 
-    def dense(own_ref, *refs):
-        *in_refs, pre_ref, deg_ref, degrow_ref, w_ref, g_ref, spread_ref, preact_ref, agg_ref = refs
+    pad = 16
+    piece = width // 2
+    small = sds((piece + pad, width), BF16)
+    inward = half - 1
+
+    def dense(place_ref, own_ref, *refs):
+        in_refs, refs = refs[:inward], refs[inward:]
+        x_ref, pre_ref, deg_ref, degrow_ref, ws_ref, wn_ref, g_ref = refs[:7]
+        spread_ref, preact_ref, back_ref, *out_refs = refs[7:]
         total = own_ref[...]
         for ref in in_refs:
             total = total + ref[...].astype(F32)
         d = deg_ref[...]
         agg = (total / jnp.concatenate([d] * (width // n), axis=1)).astype(BF16)
-        agg_ref[...] = agg
-        v = pre_ref[...] + dot(agg, w_ref[...])
+        v = pre_ref[...] + dot(agg, wn_ref[...])
         preact_ref[...] = v
         s = jax.nn.sigmoid(v)
         dpre = g_ref[...].astype(F32) * s * (1.0 + v * (1.0 - s))
-        back = lax.dot_general(
-            w_ref[...], dpre.astype(BF16), LAST, preferred_element_type=F32
-        )
+        dpre_b = dpre.astype(BF16)
+        line = jnp.broadcast_to(jnp.sum(dpre, axis=0, keepdims=True), (pad, width)).astype(BF16)
+        on_first = (place_ref[1] & 1) == 0
+        on_left = (place_ref[0] & 1) == 0
+        feats_own = x_ref[...]
+        mine = jnp.where(on_first, feats_own, agg)
+        other = jnp.where(on_first, agg, feats_own)
+        for ref, source, left in (
+            (out_refs[1], other, on_left),
+            (out_refs[2], mine, ~on_left),
+            (out_refs[3], other, ~on_left),
+            (out_refs[0], mine, on_left),
+        ):
+            block = jnp.where(left, source[:, :piece], source[:, piece:])
+            ref[:piece] = lax.dot_general(
+                block, dpre_b, FIRST, preferred_element_type=F32
+            ).astype(BF16)
+            ref[piece:] = line
+        back = lax.dot_general(wn_ref[...], dpre_b, LAST, preferred_element_type=F32)
         spread_ref[...] = (back / degrow_ref[...]).astype(BF16)
-
-    spread, preact, aggregate = call(
+        back_ref[...] = lax.dot_general(ws_ref[...], dpre_b, LAST, preferred_element_type=F32)
+
+    spread, preact, own_grad, g_own, g_core, g_side, g_corner = call(
         dense,
-        [sds((width, n), BF16), sds((n, width), F32), sds((n, width), BF16)],
-        [own_sum, *parts_in, pre, deg, deg_row, neigh_weight, out_grad],
+        [sds((width, n), BF16), sds((n, width), F32), sds((width, n), F32)] + [small] * 4,
+        [
+            place,
+            own_sum,
+            *parts_in[::-1],
+            node_feats,
+            pre,
+            deg,
+            deg_row,
+            self_weight,
+            neigh_weight,
+            out_grad,
+        ],
         "dense",
+        smem=1,
     )
     near = [spread] + [swap(spread, "col", 2 * q) for q in range(1, half)]
-
-    pad = 16
-
-    def terms(place_ref, v_ref, agg_ref, x_ref, w_ref, g_ref, hid_ref, own_ref, keep_ref, send_ref):
-        v = v_ref[...]
-        s = jax.nn.sigmoid(v)
-        hid_ref[...] = (v * s).astype(BF16)
-        dpre = g_ref[...].astype(F32) * s * (1.0 + v * (1.0 - s))
-        dpre_b = dpre.astype(BF16)
-        own_ref[...] = lax.dot_general(w_ref[...], dpre_b, LAST, preferred_element_type=F32)
-        self_term = lax.dot_general(x_ref[...], dpre_b, FIRST, preferred_element_type=F32)
-        neigh_term = lax.dot_general(agg_ref[...], dpre_b, FIRST, preferred_element_type=F32)
-        first = (place_ref[1] & 1) == 0
-        keep_ref[:width] = jnp.where(first, self_term, neigh_term).astype(BF16)
-        send_ref[:width] = jnp.where(first, neigh_term, self_term).astype(BF16)
-        line = jnp.broadcast_to(jnp.sum(dpre, axis=0, keepdims=True), (pad, width)).astype(BF16)
-        keep_ref[width:] = line
-        send_ref[width:] = line
-
-    hidden, own_grad, g_keep, g_send = call(
-        terms,
-        [
-            sds((n, width), BF16),
-            sds((width, n), F32),
-            sds((width + pad, width), BF16),
-            sds((width + pad, width), BF16),
-        ],
-        [place, preact, aggregate, node_feats, self_weight, out_grad],
-        "terms",
-        smem=1,
-    )
-    g_in = swap(g_send, "col", 1)
-    piece = width // 2
-
-    def halves(place_ref, a_ref, b_ref, keep_ref, send_ref):
-        x = place_ref[0] & 1
-        mine = pl.ds(pl.multiple_of(x * piece, piece), piece)
-        other = pl.ds(pl.multiple_of((1 - x) * piece, piece), piece)
-        tail = pl.ds(width, pad)
-        for ref, span in ((keep_ref, mine), (send_ref, other)):
-            ref[:piece] = (a_ref[span, :].astype(F32) + b_ref[span, :].astype(F32)).astype(BF16)
-            ref[piece:] = (a_ref[tail, :].astype(F32) + b_ref[tail, :].astype(F32)).astype(BF16)
-
-    small = sds((piece + pad, width), BF16)
-    h_keep, h_send = call(halves, [small, small], [place, g_keep, g_in], "halves", smem=1)
-    h_in = swap(h_send, "row", 1)
-
-    def add_two(a_ref, b_ref, out_ref):
-        out_ref[...] = (a_ref[...].astype(F32) + b_ref[...].astype(F32)).astype(BF16)
-
-    y_part = call(add_two, small, [h_keep, h_in], "add_x")
-    for k in (2 ** i for i in range(1, grid_rows.bit_length() - 1)):
-        y_part = call(add_two, small, [y_part, swap(y_part, "row", k)], "add_y")
-    z_parts = [y_part] + [swap(y_part, "col", 2 * q) for q in range(1, half)]
 
     def add_many(*refs):
         *in_refs, out_ref = refs
@@ -354,8 +363,9 @@
             vals = [vals[i] + vals[i + 1] for i in range(0, len(vals), 2)]
         out_ref[...] = vals[0].astype(BF16)
 
-    g_piece = call(add_many, small, z_parts, "add_z")
-    g_other = swap(g_piece, "row", 1)
+    g_in = [swap_corner(g_corner), swap(g_side, "row", 1), swap(g_core, "col", 1)]
+    g_part = call(add_many, small, [g_own, *g_in[::-1]], "add_corner", after=())
+    y_in = [swap(g_part, "row", 2 ** i) for i in range(1, grid_rows.bit_length() - 1)]
 
     far = [swap(part, "col", 1) for part in near]
 
@@ -385,6 +395,12 @@
     )
     back_in = [swap(part, "row", k + 1) for k, part in enumerate(back_parts)]
 
+    def activate(v_ref, hid_ref):
+        v = v_ref[...]
+        hid_ref[...] = (v * jax.nn.sigmoid(v)).astype(BF16)
+
+    hidden = call(activate, sds((n, width), BF16), [preact], "activate", after=[own_back])
+
     def finish(own_ref, *refs):
         *in_refs, out_ref = refs
         total = own_ref[...]
@@ -394,28 +410,63 @@
 
     feat_grad = call(finish, sds((n, width), BF16), [own_back, *back_in], "finish")
 
-    def join(place_ref, mine_ref, other_ref, out_ref):
-        x = place_ref[0] & 1
-        out_ref[pl.ds(pl.multiple_of(x * piece, piece), piece), :] = mine_ref[:piece]
-        out_ref[pl.ds(pl.multiple_of((1 - x) * piece, piece), piece), :] = other_ref[:piece]
-
-    g_half = call(join, sds((width, width), BF16), [place, g_piece, g_other], "join", smem=1)
-    g_half_in = swap(g_half, "col", 1)
-
-    def scale(place_ref, a_ref, b_ref, line_ref, self_ref, neigh_ref, bias_ref):
+    z_part = g_part
+    for got in y_in:
+        z_part = call(add_many, small, [z_part, got], "add_y", after=near[1:])
+    z_in = [swap(z_part, "col", 2 * q) for q in range(1, half)]
+    g_piece = call(add_many, small, [z_part, *z_in], "add_z", after=[own_back])
+    pieces = g_piece[:piece]
+    pieces_in = [swap_corner(pieces), swap(pieces, "row", 1), swap(pieces, "col", 1)]
+
+    def write(flip, place_ref, a_ref, b_ref, self_hbm, neigh_hbm, blocks, sems):
         first = (place_ref[1] & 1) == 0
-        a, b = a_ref[...].astype(F32), b_ref[...].astype(F32)
-        self_ref[...] = jnp.where(first, a, b) * grad_scale
-        neigh_ref[...] = jnp.where(first, b, a) * grad_scale
-        bias_ref[...] = line_ref[piece : piece + 1].astype(F32) * grad_scale
-
-    grad_self, grad_neigh, grad_bias = call(
-        scale,
-        [sds((width, width), F32), sds((width, width), F32), sds((1, width), F32)],
-        [place, g_half, g_half_in, g_piece],
-        "scale",
-        smem=1,
-    )
+        row = (place_ref[0] & 1) ^ flip
+        span = pl.ds(pl.multiple_of(row * piece, piece), piece)
+        a = a_ref[:piece].astype(F32) * grad_scale
+        b = b_ref[:piece].astype(F32) * grad_scale
+        copies = []
+        for j, (value, out) in enumerate(
+            ((jnp.where(first, a, b), self_hbm), (jnp.where(first, b, a), neigh_hbm))
+        ):
+            blocks[j] = value
+            copies.append(pltpu.make_async_copy(blocks.at[j], out.at[span], sems.at[j]))
+            copies[-1].start()
+        for copy in copies:
+            copy.wait()
+
+    def write_first(place_ref, a_ref, b_ref, self_hbm, neigh_hbm, bias_ref, blocks, sems):
+        bias_ref[...] = a_ref[piece : piece + 1].astype(F32) * grad_scale
+        write(0, place_ref, a_ref, b_ref, self_hbm, neigh_hbm, blocks, sems)
+
+    def write_second(place_ref, a_ref, b_ref, s_ref, n_ref, self_hbm, neigh_hbm, blocks, sems):
+        write(1, place_ref, a_ref, b_ref, self_hbm, neigh_hbm, blocks, sems)
+
+    held, fast = (pl.BlockSpec(memory_space=m) for m in (pltpu.HBM, pltpu.VMEM))
+    whole = [sds((width, width), F32)] * 2
+    common = dict(
+        scratch_shapes=[pltpu.VMEM((2, piece, width), F32), pltpu.SemaphoreType.DMA((2,))],
+        compiler_params=pltpu.CompilerParams(vmem_limit_bytes=24 << 20),
+        cost_estimate=pl.CostEstimate(flops=1 << 20, bytes_accessed=1 << 18, transcendentals=0),
+    )
+    scalars = pl.BlockSpec(memory_space=pltpu.SMEM)
+    corner_in, side_in, core_in = pieces_in
+    *grads, grad_bias = pl.pallas_call(
+        write_first,
+        out_shape=whole + [sds((1, width), F32)],
+        in_specs=[scalars, fast, fast],
+        out_specs=[held, held, fast],
+        name="write_first",
+        **common,
+    )(place, g_piece, core_in)
+    grad_self, grad_neigh = pl.pallas_call(
+        write_second,
+        out_shape=whole,
+        in_specs=[scalars, fast, fast, held, held],
+        out_specs=[held, held],
+        input_output_aliases={3: 0, 4: 1},
+        name="write_second",
+        **common,
+    )(place, side_in, corner_in, *grads)
     return hidden, feat_grad, grad_self, grad_neigh, grad_bias.reshape(width)
 
 

time: 62.3 us -> 50.8 us (0.82)
  waiting for transfers between devices: 21.4 us -> 11.4 us
  local copies, waits for them, and re-layouts: 3.09 us -> 0.04 us
  Pallas kernels: 7.55 us -> 9.47 us
    ppermute x25, waiting for transfers between devices: 21.4 us -> 11.4 us  [swap(): return lax.ppermute(value, axis, [(i, i ^ distance) for i in range(size)])]
    pallas_call x0 -> x2, Pallas kernels: none -> 3.12 us  [the longest x1 1.84 us: direct_form(): pl.pallas_call(write_first, out_shape=whole + [sds((1, width), F32)], in_...]
    unnamed x18 -> x12, local copies, waits for them, and re-layouts: 3.09 us -> 0.04 us
    ppermute x25, starting transfers between devices: 28.7 us -> 26.3 us  [swap(): return lax.ppermute(value, axis, [(i, i ^ distance) for i in range(size)])]
    pallas_call x15 -> x12, Pallas kernels: 6.33 us -> 3.94 us  [call(): pl.pallas_call(body, out_shape=outs, in_specs=in_specs, out_specs=[pl.Blo...]
    ppermute x0 -> x2, starting transfers between devices: none -> 1.88 us  [swap_corner(): lax.ppermute(value, ('row', 'col'), [(i, i ^ step) for i in range(size)])]
    pallas_call x1, Pallas kernels: 1.23 us -> 2.41 us  [build_cell(): pl.pallas_call(body, out_shape=sds((grid_cols * edge, grid_rows * edge),...]
  transfers between devices with their start and end apart: 25 -> 27, of which waited for: 13 -> 10; matrix products, arithmetic and copies ran while one was open for 0% -> 0% of each run, Pallas kernels for 6% -> 13%
where the time goes in v2:
time: 50.8 us; the launch traced here: 50.6 us
  starting transfers between devices  28.2 us (56%)
  waiting for transfers between devices  11.4 us (22%)
  Pallas kernels  9.47 us (19%)
  between operations  1.49 us (3%)
    ppermute x25, starting transfers between devices, swap(): return lax.ppermute(value, axis, [(i, i ^ distance) for i in range(size)])  26.3 us
    ppermute x25, waiting for transfers between devices, swap(): return lax.ppermute(value, axis, [(i, i ^ distance) for i in range(size)])  11.4 us
    pallas_call x12, Pallas kernels, call(): pl.pallas_call(body, out_shape=outs, in_specs=in_specs, out_specs=[pl.Blo...  3.94 us
    pallas_call x1, Pallas kernels, build_cell(): pl.pallas_call(body, out_shape=sds((grid_cols * edge, grid_rows * edge),...  2.41 us
    ppermute x2, starting transfers between devices, swap_corner(): lax.ppermute(value, ('row', 'col'), [(i, i ^ step) for i in range(size)])  1.88 us
    pallas_call x1, Pallas kernels, direct_form(): pl.pallas_call(write_first, out_shape=whole + [sds((1, width), F32)], in_...  1.84 us
    pallas_call x1, Pallas kernels, direct_form(): pl.pallas_call(write_second, out_shape=whole, in_specs=[scalars, fast, fa...  1.28 us
  transfers between devices with their start and end apart: 27, of which 10 were waited for; matrix products, arithmetic and copies ran while one was open for 0% of the time, Pallas kernels for 13%

profile of v2, /device:TPU:0, one launch (start us, length us, event | category | flops | bytes accessed | tf_op | source)
XLA Modules:
  0.0 50.6 jit_solution(7048016925297289310)
XLA Ops:
  0.6 4.0 %collective-permute-start.2 = (bf16[128,256]{1,0:T(8,128)(2,1)}, bf16[128,256]{1,0:T(8,128)(2,1)S(1)}, u32[]{:S(2)}, u32[]{:S(2)}) collective-permute-start(bf16[128,256]{1,0:T(8,128)(2,1)} %refs_5_.1), channel_id=1, source_target_pairs={{0,24},{8,16},{16,8},{24,0},{1,25},{9,17},{17,9},{25,1},{2,26},{10... | collective-permute-start | bytes 196616 | tf_op jit(solution)/shard_map/ppermute | solution.py:213
  6.0 2.4 %build_cell.1.refs_0_ = bf16[1024,512]{1,0:T(8,128)(2,1)S(1)} custom-call(s32[2]{0:T(128)S(1)} %pad_add_fusion.place_ref.refs_0_, s32[1,1]{1,0:T(1,128)S(6)} %copy.19.refs_0_, s32[80]{0:T(128)} %bitcast.11, s32[80]{0:T(128)} %bitcast.12, bf16[80,128,128]{2,1,0:T(8,128)(2,1)} %bitcast.10), custom_call_target="tpu_custom_call" | custom-call | flops 16777216 | bytes 5242880 | tf_op jit(solution)/shard_map/build_cell/pallas_call | solution.py:191
  10.3 1.2 %collective-permute-done.3.refs_1_ = bf16[512,256]{1,0:T(8,128)(2,1)S(1)} collective-permute-done((bf16[512,256]{1,0:T(8,128)(2,1)S(1)}, bf16[512,256]{1,0:T(8,128)(2,1)S(1)}, u32[]{:S(2)}, u32[]{:S(2)}) %collective-permute-start.3) | collective-permute-done | bytes 262176 | tf_op jit(solution)/shard_map/ppermute | solution.py:213
  11.6 3.7 %collective-permute-start.4 = (bf16[128,256]{1,0:T(8,128)(2,1)S(1)}, bf16[128,256]{1,0:T(8,128)(2,1)S(1)}, u32[]{:S(2)}, u32[]{:S(2)}) collective-permute-start(bf16[128,256]{1,0:T(8,128)(2,1)S(1)} %get-tuple-element.29), channel_id=1, source_target_pairs={{0,6},{1,7},{2,4},{3,5},{4,2},{5,3},{6,0},{7,1},{8,14},{9,15},{10,... | collective-permute-start | bytes 196616 | tf_op jit(solution)/shard_map/ppermute | solution.py:213
  15.2 0.8 %collective-permute-start.6 = (bf16[128,256]{1,0:T(8,128)(2,1)S(1)}, bf16[128,256]{1,0:T(8,128)(2,1)S(1)}, u32[]{:S(2)}, u32[]{:S(2)}) collective-permute-start(bf16[128,256]{1,0:T(8,128)(2,1)S(1)} %get-tuple-element.31), channel_id=1, source_target_pairs={{0,2},{1,3},{2,0},{3,1},{4,6},{5,7},{6,4},{7,5},{8,10},{9,11},{10,... | collective-permute-start | bytes 196616 | tf_op jit(solution)/shard_map/ppermute | solution.py:213
  16.2 1.7 %collective-permute-done.4.refs_2_ = bf16[128,256]{1,0:T(8,128)(2,1)S(1)} collective-permute-done((bf16[128,256]{1,0:T(8,128)(2,1)S(1)}, bf16[128,256]{1,0:T(8,128)(2,1)S(1)}, u32[]{:S(2)}, u32[]{:S(2)}) %collective-permute-start.4) | collective-permute-done | bytes 65568 | tf_op jit(solution)/shard_map/ppermute | solution.py:213
  17.9 3.3 %collective-permute-done.5.refs_3_ = bf16[128,256]{1,0:T(8,128)(2,1)S(1)} collective-permute-done((bf16[128,256]{1,0:T(8,128)(2,1)S(1)}, bf16[128,256]{1,0:T(8,128)(2,1)S(1)}, u32[]{:S(2)}, u32[]{:S(2)}) %collective-permute-start.5) | collective-permute-done | bytes 65568 | tf_op jit(solution)/shard_map/ppermute | solution.py:213
  21.1 1.0 %dense.1 = (bf16[256,128]{1,0:T(8,128)(2,1)S(1)}, f32[128,256]{1,0:T(8,128)S(1)}, f32[256,128]{1,0:T(8,128)S(1)}, bf16[144,256]{1,0:T(8,128)(2,1)S(1)}, bf16[144...) custom-call(s32[2]{0:T(128)S(1)} %pad_add_fusion.place_ref.refs_0_, ...), custom_call_target="tpu_custom_call" | custom-call | flops 1048576 | bytes 262144 | tf_op jit(solution)/shard_map/dense/pallas_call | solution.py:130
  22.3 0.9 %collective-permute-start.18 = (bf16[144,256]{1,0:T(8,128)(2,1)S(1)}, bf16[144,256]{1,0:T(8,128)(2,1)S(1)}, u32[]{:S(2)}, u32[]{:S(2)}) collective-permute-start(bf16[144,256]{1,0:T(8,128)(2,1)S(1)} %get-tuple-element.44), channel_id=1, source_target_pairs={{0,8},{8,0},{16,24},{24,16},{1,9},{9,1},{17,25},{25,17},{2,10},{10... | collective-permute-start | bytes 221192 | tf_op jit(solution)/shard_map/ppermute | solution.py:213
  23.1 1.0 %collective-permute-start.19 = (bf16[144,256]{1,0:T(8,128)(2,1)S(1)}, bf16[144,256]{1,0:T(8,128)(2,1)S(1)}, u32[]{:S(2)}, u32[]{:S(2)}) collective-permute-start(bf16[144,256]{1,0:T(8,128)(2,1)S(1)} %get-tuple-element.45), channel_id=1, source_target_pairs={{0,9},{1,8},{2,11},{3,10},{4,13},{5,12},{6,15},{7,14},{8,1},{9,0},... | collective-permute-start | bytes 221192 | tf_op jit(solution)/shard_map/ppermute | solution.py:219
  24.1 2.5 %collective-permute-start.9 = (bf16[256,128]{1,0:T(8,128)(2,1)S(1)}, bf16[256,128]{1,0:T(8,128)(2,1)S(1)}, u32[]{:S(2)}, u32[]{:S(2)}) collective-permute-start(bf16[256,128]{1,0:T(8,128)(2,1)S(1)} %get-tuple-element.36.refs_1_), channel_id=1, source_target_pairs={{0,6},{1,7},{2,4},{3,5},{4,2},{5,3},{6,0},{7,1},{8,14},{9,15},{10,... | collective-permute-start | bytes 196616 | tf_op jit(solution)/shard_map/ppermute | solution.py:213
  26.7 1.8 %collective-permute-start.7 = (bf16[256,128]{1,0:T(8,128)(2,1)S(1)}, bf16[256,128]{1,0:T(8,128)(2,1)S(1)}, u32[]{:S(2)}, u32[]{:S(2)}) collective-permute-start(bf16[256,128]{1,0:T(8,128)(2,1)S(1)} %get-tuple-element.36.refs_1_), channel_id=1, source_target_pairs={{0,2},{1,3},{2,0},{3,1},{4,6},{5,7},{6,4},{7,5},{8,10},{9,11},{10,... | collective-permute-start | bytes 196616 | tf_op jit(solution)/shard_map/ppermute | solution.py:213
  28.6 1.6 %collective-permute-start.20 = (bf16[144,256]{1,0:T(8,128)(2,1)S(1)}, bf16[144,256]{1,0:T(8,128)(2,1)S(1)}, u32[]{:S(2)}, u32[]{:S(2)}) collective-permute-start(bf16[144,256]{1,0:T(8,128)(2,1)S(1)} %add_corner.1.refs_0_), channel_id=1, source_target_pairs={{0,16},{8,24},{16,0},{24,8},{1,17},{9,25},{17,1},{25,9},{2,18},{10... | collective-permute-start | bytes 221192 | tf_op jit(solution)/shard_map/ppermute | solution.py:213
  30.1 0.8 %collective-permute-done.9.refs_4_ = bf16[256,128]{1,0:T(8,128)(2,1)S(1)} collective-permute-done((bf16[256,128]{1,0:T(8,128)(2,1)S(1)}, bf16[256,128]{1,0:T(8,128)(2,1)S(1)}, u32[]{:S(2)}, u32[]{:S(2)}) %collective-permute-start.9) | collective-permute-done | bytes 65568 | tf_op jit(solution)/shard_map/ppermute | solution.py:213
  31.0 2.2 %collective-permute-done.8.refs_3_ = bf16[256,128]{1,0:T(8,128)(2,1)S(1)} collective-permute-done((bf16[256,128]{1,0:T(8,128)(2,1)S(1)}, bf16[256,128]{1,0:T(8,128)(2,1)S(1)}, u32[]{:S(2)}, u32[]{:S(2)}) %collective-permute-start.8) | collective-permute-done | bytes 65568 | tf_op jit(solution)/shard_map/ppermute | solution.py:213
  34.1 2.4 %collective-permute-start.23 = (bf16[144,256]{1,0:T(8,128)(2,1)S(1)}, bf16[144,256]{1,0:T(8,128)(2,1)S(1)}, u32[]{:S(2)}, u32[]{:S(2)}) collective-permute-start(bf16[144,256]{1,0:T(8,128)(2,1)S(1)} %add_y.1.refs_0_), channel_id=1, source_target_pairs={{0,6},{1,7},{2,4},{3,5},{4,2},{5,3},{6,0},{7,1},{8,14},{9,15},{10,... | collective-permute-start | bytes 221192 | tf_op jit(solution)/shard_map/ppermute | solution.py:213
  36.5 2.0 %collective-permute-start.21 = (bf16[144,256]{1,0:T(8,128)(2,1)S(1)}, bf16[144,256]{1,0:T(8,128)(2,1)S(1)}, u32[]{:S(2)}, u32[]{:S(2)}) collective-permute-start(bf16[144,256]{1,0:T(8,128)(2,1)S(1)} %add_y.1.refs_0_), channel_id=1, source_target_pairs={{0,2},{1,3},{2,0},{3,1},{4,6},{5,7},{6,4},{7,5},{8,10},{9,11},{10,... | collective-permute-start | bytes 221192 | tf_op jit(solution)/shard_map/ppermute | solution.py:213
  38.9 0.9 %collective-permute-start.14 = (bf16[256,128]{1,0:T(8,128)(2,1)S(1)}, bf16[256,128]{1,0:T(8,128)(2,1)S(1)}, u32[]{:S(2)}, u32[]{:S(2)}) collective-permute-start(bf16[256,128]{1,0:T(8,128)(2,1)S(1)} %get-tuple-element.39), channel_id=1, source_target_pairs={{0,8},{8,0},{16,24},{24,16},{1,9},{9,1},{17,25},{25,17},{2,10},{10... | collective-permute-start | bytes 196616 | tf_op jit(solution)/shard_map/ppermute | solution.py:213
  39.7 1.5 %collective-permute-start.15 = (bf16[256,128]{1,0:T(8,128)(2,1)S(1)}, bf16[256,128]{1,0:T(8,128)(2,1)S(1)}, u32[]{:S(2)}, u32[]{:S(2)}) collective-permute-start(bf16[256,128]{1,0:T(8,128)(2,1)S(1)} %get-tuple-element.40), channel_id=1, source_target_pairs={{0,16},{8,24},{16,0},{24,8},{1,17},{9,25},{17,1},{25,9},{2,18},{10... | collective-permute-start | bytes 196616 | tf_op jit(solution)/shard_map/ppermute | solution.py:213
  41.2 1.6 %collective-permute-start.16 = (bf16[256,128]{1,0:T(8,128)(2,1)S(1)}, bf16[256,128]{1,0:T(8,128)(2,1)S(1)}, u32[]{:S(2)}, u32[]{:S(2)}) collective-permute-start(bf16[256,128]{1,0:T(8,128)(2,1)S(1)} %get-tuple-element.41), channel_id=1, source_target_pairs={{0,24},{8,16},{16,8},{24,0},{1,25},{9,17},{17,9},{25,1},{2,26},{10... | collective-permute-start | bytes 196616 | tf_op jit(solution)/shard_map/ppermute | solution.py:213
  43.5 0.9 %collective-permute-start.25 = (bf16[128,256]{1,0:T(8,128)(2,1)S(1)}, bf16[128,256]{1,0:T(8,128)(2,1)S(1)}, u32[]{:S(2)}, u32[]{:S(2)}) collective-permute-start(bf16[128,256]{1,0:T(8,128)(2,1)S(1)} %slice.4), channel_id=1, source_target_pairs={{0,9},{1,8},{2,11},{3,10},{4,13},{5,12},{6,15},{7,14},{8,1},{9,0},... | collective-permute-start | bytes 196616 | tf_op jit(solution)/shard_map/ppermute | solution.py:219
  44.4 1.2 %collective-permute-start.24 = (bf16[128,256]{1,0:T(8,128)(2,1)S(1)}, bf16[128,256]{1,0:T(8,128)(2,1)S(1)}, u32[]{:S(2)}, u32[]{:S(2)}) collective-permute-start(bf16[128,256]{1,0:T(8,128)(2,1)S(1)} %slice.4), channel_id=1, source_target_pairs={{0,8},{8,0},{16,24},{24,16},{1,9},{9,1},{17,25},{25,17},{2,10},{10... | collective-permute-start | bytes 196616 | tf_op jit(solution)/shard_map/ppermute | solution.py:213
  47.1 1.8 %write_first.1 = (f32[256,256]{1,0:T(8,128)}, f32[256,256]{1,0:T(8,128)}, f32[1,256]{1,0:T(1,128)}) custom-call(s32[2]{0:T(128)S(1)} %pad_add_fusion.place_ref.refs_0_, bf16[144,256]{1,0:T(8,128)(2,1)S(1)} %add_z.1.a_ref, bf16[128,256]{1,0:T(8,128)(2,1)S(1)} %collective-permute-done.26.b_ref), custom_call_target="tpu_custom_call" | custom-call | flops 1048576 | bytes 262144 | tf_op jit(solution)/shard_map/write_first/pallas_call | solution.py:453
  49.3 1.3 %write_second.1 = (f32[256,256]{1,0:T(8,128)}, f32[256,256]{1,0:T(8,128)}) custom-call(s32[2]{0:T(128)S(1)} %pad_add_fusion.place_ref.refs_0_, bf16[128,256]{1,0:T(8,128)(2,1)S(1)} %collective-permute-done.24.a_ref, bf16[128,256]{1,0:T(8,128)(2,1)S(1)} %collective-permute-done.25.b_ref, ...), custom_call_target="tpu_custom_call", output_to_operand_aliasing={{0}: (3, {}), {1}: (4, {})} | custom-call | flops 1048576 | bytes 262144 | tf_op jit(solution)/shard_map/write_second/pallas_call | solution.py:461
  (59 shorter events, 6.6 us)
Async XLA Ops:
  0.6 7.8 %collective-permute-start.2 = (bf16[128,256]{1,0:T(8,128)(2,1)}, bf16[128,256]{1,0:T(8,128)(2,1)S(1)}, u32[]{:S(2)}, u32[]{:S(2)}) collective-permute-start(bf16[128,256]{1,0:T(8,128)(2,1)} %refs_5_.1), channel_id=1, source_target_pairs={{0,24},{8,16},{16,8},{24,0},{1,25},{9,17},{17,9},{25,1},{2,26},{10... | collective-permute-start | bytes 196616 | tf_op jit(solution)/shard_map/ppermute | solution.py:213
  5.1 4.5 %collective-permute-start = (bf16[128,256]{1,0:T(8,128)(2,1)}, bf16[128,256]{1,0:T(8,128)(2,1)S(1)}, u32[]{:S(2)}, u32[]{:S(2)}) collective-permute-start(bf16[128,256]{1,0:T(8,128)(2,1)} %refs_5_.1), channel_id=1, source_target_pairs={{0,8},{8,0},{16,24},{24,16},{1,9},{9,1},{17,25},{25,17},{2,10},{10... | collective-permute-start | bytes 196616 | tf_op jit(solution)/shard_map/ppermute | solution.py:213
  11.6 6.3 %collective-permute-start.4 = (bf16[128,256]{1,0:T(8,128)(2,1)S(1)}, bf16[128,256]{1,0:T(8,128)(2,1)S(1)}, u32[]{:S(2)}, u32[]{:S(2)}) collective-permute-start(bf16[128,256]{1,0:T(8,128)(2,1)S(1)} %get-tuple-element.29), channel_id=1, source_target_pairs={{0,6},{1,7},{2,4},{3,5},{4,2},{5,3},{6,0},{7,1},{8,14},{9,15},{10,... | collective-permute-start | bytes 196616 | tf_op jit(solution)/shard_map/ppermute | solution.py:213
  15.2 5.9 %collective-permute-start.5 = (bf16[128,256]{1,0:T(8,128)(2,1)S(1)}, bf16[128,256]{1,0:T(8,128)(2,1)S(1)}, u32[]{:S(2)}, u32[]{:S(2)}) collective-permute-start(bf16[128,256]{1,0:T(8,128)(2,1)S(1)} %get-tuple-element.30), channel_id=1, source_target_pairs={{0,4},{1,5},{2,6},{3,7},{4,0},{5,1},{6,2},{7,3},{8,12},{9,13},{10,... | collective-permute-start | bytes 196616 | tf_op jit(solution)/shard_map/ppermute | solution.py:213
  15.2 5.9 %collective-permute-start.6 = (bf16[128,256]{1,0:T(8,128)(2,1)S(1)}, bf16[128,256]{1,0:T(8,128)(2,1)S(1)}, u32[]{:S(2)}, u32[]{:S(2)}) collective-permute-start(bf16[128,256]{1,0:T(8,128)(2,1)S(1)} %get-tuple-element.31), channel_id=1, source_target_pairs={{0,2},{1,3},{2,0},{3,1},{4,6},{5,7},{6,4},{7,5},{8,10},{9,11},{10,... | collective-permute-start | bytes 196616 | tf_op jit(solution)/shard_map/ppermute | solution.py:213
  22.2 4.5 %collective-permute-start.17 = (bf16[144,256]{1,0:T(8,128)(2,1)S(1)}, bf16[144,256]{1,0:T(8,128)(2,1)S(1)}, u32[]{:S(2)}, u32[]{:S(2)}) collective-permute-start(bf16[144,256]{1,0:T(8,128)(2,1)S(1)} %get-tuple-element.43), channel_id=1, source_target_pairs={{0,1},{1,0},{2,3},{3,2},{4,5},{5,4},{6,7},{7,6},{8,9},{9,8},{10,11... | collective-permute-start | bytes 221192 | tf_op jit(solution)/shard_map/ppermute | solution.py:213
  22.3 6.2 %collective-permute-start.18 = (bf16[144,256]{1,0:T(8,128)(2,1)S(1)}, bf16[144,256]{1,0:T(8,128)(2,1)S(1)}, u32[]{:S(2)}, u32[]{:S(2)}) collective-permute-start(bf16[144,256]{1,0:T(8,128)(2,1)S(1)} %get-tuple-element.44), channel_id=1, source_target_pairs={{0,8},{8,0},{16,24},{24,16},{1,9},{9,1},{17,25},{25,17},{2,10},{10... | collective-permute-start | bytes 221192 | tf_op jit(solution)/shard_map/ppermute | solution.py:213
  23.1 5.4 %collective-permute-start.19 = (bf16[144,256]{1,0:T(8,128)(2,1)S(1)}, bf16[144,256]{1,0:T(8,128)(2,1)S(1)}, u32[]{:S(2)}, u32[]{:S(2)}) collective-permute-start(bf16[144,256]{1,0:T(8,128)(2,1)S(1)} %get-tuple-element.45), channel_id=1, source_target_pairs={{0,9},{1,8},{2,11},{3,10},{4,13},{5,12},{6,15},{7,14},{8,1},{9,0},... | collective-permute-start | bytes 221192 | tf_op jit(solution)/shard_map/ppermute | solution.py:219
  24.1 6.9 %collective-permute-start.9 = (bf16[256,128]{1,0:T(8,128)(2,1)S(1)}, bf16[256,128]{1,0:T(8,128)(2,1)S(1)}, u32[]{:S(2)}, u32[]{:S(2)}) collective-permute-start(bf16[256,128]{1,0:T(8,128)(2,1)S(1)} %get-tuple-element.36.refs_1_), channel_id=1, source_target_pairs={{0,6},{1,7},{2,4},{3,5},{4,2},{5,3},{6,0},{7,1},{8,14},{9,15},{10,... | collective-permute-start | bytes 196616 | tf_op jit(solution)/shard_map/ppermute | solution.py:213
  26.6 6.6 %collective-permute-start.8 = (bf16[256,128]{1,0:T(8,128)(2,1)S(1)}, bf16[256,128]{1,0:T(8,128)(2,1)S(1)}, u32[]{:S(2)}, u32[]{:S(2)}) collective-permute-start(bf16[256,128]{1,0:T(8,128)(2,1)S(1)} %get-tuple-element.36.refs_1_), channel_id=1, source_target_pairs={{0,4},{1,5},{2,6},{3,7},{4,0},{5,1},{6,2},{7,3},{8,12},{9,13},{10,... | collective-permute-start | bytes 196616 | tf_op jit(solution)/shard_map/ppermute | solution.py:213
  26.7 6.6 %collective-permute-start.7 = (bf16[256,128]{1,0:T(8,128)(2,1)S(1)}, bf16[256,128]{1,0:T(8,128)(2,1)S(1)}, u32[]{:S(2)}, u32[]{:S(2)}) collective-permute-start(bf16[256,128]{1,0:T(8,128)(2,1)S(1)} %get-tuple-element.36.refs_1_), channel_id=1, source_target_pairs={{0,2},{1,3},{2,0},{3,1},{4,6},{5,7},{6,4},{7,5},{8,10},{9,11},{10,... | collective-permute-start | bytes 196616 | tf_op jit(solution)/shard_map/ppermute | solution.py:213
  28.6 5.5 %collective-permute-start.20 = (bf16[144,256]{1,0:T(8,128)(2,1)S(1)}, bf16[144,256]{1,0:T(8,128)(2,1)S(1)}, u32[]{:S(2)}, u32[]{:S(2)}) collective-permute-start(bf16[144,256]{1,0:T(8,128)(2,1)S(1)} %add_corner.1.refs_0_), channel_id=1, source_target_pairs={{0,16},{8,24},{16,0},{24,8},{1,17},{9,25},{17,1},{25,9},{2,18},{10... | collective-permute-start | bytes 221192 | tf_op jit(solution)/shard_map/ppermute | solution.py:213
  30.1 6.3 %collective-permute-start.10 = (bf16[256,128]{1,0:T(8,128)(2,1)S(1)}, bf16[256,128]{1,0:T(8,128)(2,1)S(1)}, u32[]{:S(2)}, u32[]{:S(2)}) collective-permute-start(bf16[256,128]{1,0:T(8,128)(2,1)S(1)} %get-tuple-element.36.refs_1_), channel_id=1, source_target_pairs={{0,1},{1,0},{2,3},{3,2},{4,5},{5,4},{6,7},{7,6},{8,9},{9,8},{10,11... | collective-permute-start | bytes 196616 | tf_op jit(solution)/shard_map/ppermute | solution.py:213
  31.0 5.5 %collective-permute-start.13 = (bf16[256,128]{1,0:T(8,128)(2,1)S(1)}, bf16[256,128]{1,0:T(8,128)(2,1)S(1)}, u32[]{:S(2)}, u32[]{:S(2)}) collective-permute-start(bf16[256,128]{1,0:T(8,128)(2,1)S(1)} %collective-permute-done.9.refs_4_), channel_id=1, source_target_pairs={{0,1},{1,0},{2,3},{3,2},{4,5},{5,4},{6,7},{7,6},{8,9},{9,8},{10,11... | collective-permute-start | bytes 196616 | tf_op jit(solution)/shard_map/ppermute | solution.py:213
  33.2 5.3 %collective-permute-start.12 = (bf16[256,128]{1,0:T(8,128)(2,1)S(1)}, bf16[256,128]{1,0:T(8,128)(2,1)S(1)}, u32[]{:S(2)}, u32[]{:S(2)}) collective-permute-start(bf16[256,128]{1,0:T(8,128)(2,1)S(1)} %collective-permute-done.8.refs_3_), channel_id=1, source_target_pairs={{0,1},{1,0},{2,3},{3,2},{4,5},{5,4},{6,7},{7,6},{8,9},{9,8},{10,11... | collective-permute-start | bytes 196616 | tf_op jit(solution)/shard_map/ppermute | solution.py:213
  33.3 5.2 %collective-permute-start.11 = (bf16[256,128]{1,0:T(8,128)(2,1)S(1)}, bf16[256,128]{1,0:T(8,128)(2,1)S(1)}, u32[]{:S(2)}, u32[]{:S(2)}) collective-permute-start(bf16[256,128]{1,0:T(8,128)(2,1)S(1)} %collective-permute-done.7.refs_2_), channel_id=1, source_target_pairs={{0,1},{1,0},{2,3},{3,2},{4,5},{5,4},{6,7},{7,6},{8,9},{9,8},{10,11... | collective-permute-start | bytes 196616 | tf_op jit(solution)/shard_map/ppermute | solution.py:213
  34.1 7.2 %collective-permute-start.23 = (bf16[144,256]{1,0:T(8,128)(2,1)S(1)}, bf16[144,256]{1,0:T(8,128)(2,1)S(1)}, u32[]{:S(2)}, u32[]{:S(2)}) collective-permute-start(bf16[144,256]{1,0:T(8,128)(2,1)S(1)} %add_y.1.refs_0_), channel_id=1, source_target_pairs={{0,6},{1,7},{2,4},{3,5},{4,2},{5,3},{6,0},{7,1},{8,14},{9,15},{10,... | collective-permute-start | bytes 221192 | tf_op jit(solution)/shard_map/ppermute | solution.py:213
  36.5 6.9 %collective-permute-start.22 = (bf16[144,256]{1,0:T(8,128)(2,1)S(1)}, bf16[144,256]{1,0:T(8,128)(2,1)S(1)}, u32[]{:S(2)}, u32[]{:S(2)}) collective-permute-start(bf16[144,256]{1,0:T(8,128)(2,1)S(1)} %add_y.1.refs_0_), channel_id=1, source_target_pairs={{0,4},{1,5},{2,6},{3,7},{4,0},{5,1},{6,2},{7,3},{8,12},{9,13},{10,... | collective-permute-start | bytes 221192 | tf_op jit(solution)/shard_map/ppermute | solution.py:213
  36.5 6.9 %collective-permute-start.21 = (bf16[144,256]{1,0:T(8,128)(2,1)S(1)}, bf16[144,256]{1,0:T(8,128)(2,1)S(1)}, u32[]{:S(2)}, u32[]{:S(2)}) collective-permute-start(bf16[144,256]{1,0:T(8,128)(2,1)S(1)} %add_y.1.refs_0_), channel_id=1, source_target_pairs={{0,2},{1,3},{2,0},{3,1},{4,6},{5,7},{6,4},{7,5},{8,10},{9,11},{10,... | collective-permute-start | bytes 221192 | tf_op jit(solution)/shard_map/ppermute | solution.py:213
  38.9 5.5 %collective-permute-start.14 = (bf16[256,128]{1,0:T(8,128)(2,1)S(1)}, bf16[256,128]{1,0:T(8,128)(2,1)S(1)}, u32[]{:S(2)}, u32[]{:S(2)}) collective-permute-start(bf16[256,128]{1,0:T(8,128)(2,1)S(1)} %get-tuple-element.39), channel_id=1, source_target_pairs={{0,8},{8,0},{16,24},{24,16},{1,9},{9,1},{17,25},{25,17},{2,10},{10... | collective-permute-start | bytes 196616 | tf_op jit(solution)/shard_map/ppermute | solution.py:213
  39.7 6.6 %collective-permute-start.15 = (bf16[256,128]{1,0:T(8,128)(2,1)S(1)}, bf16[256,128]{1,0:T(8,128)(2,1)S(1)}, u32[]{:S(2)}, u32[]{:S(2)}) collective-permute-start(bf16[256,128]{1,0:T(8,128)(2,1)S(1)} %get-tuple-element.40), channel_id=1, source_target_pairs={{0,16},{8,24},{16,0},{24,8},{1,17},{9,25},{17,1},{25,9},{2,18},{10... | collective-permute-start | bytes 196616 | tf_op jit(solution)/shard_map/ppermute | solution.py:213
  41.2 5.2 %collective-permute-start.16 = (bf16[256,128]{1,0:T(8,128)(2,1)S(1)}, bf16[256,128]{1,0:T(8,128)(2,1)S(1)}, u32[]{:S(2)}, u32[]{:S(2)}) collective-permute-start(bf16[256,128]{1,0:T(8,128)(2,1)S(1)} %get-tuple-element.41), channel_id=1, source_target_pairs={{0,24},{8,16},{16,8},{24,0},{1,25},{9,17},{17,9},{25,1},{2,26},{10... | collective-permute-start | bytes 196616 | tf_op jit(solution)/shard_map/ppermute | solution.py:213
  43.5 5.5 %collective-permute-start.25 = (bf16[128,256]{1,0:T(8,128)(2,1)S(1)}, bf16[128,256]{1,0:T(8,128)(2,1)S(1)}, u32[]{:S(2)}, u32[]{:S(2)}) collective-permute-start(bf16[128,256]{1,0:T(8,128)(2,1)S(1)} %slice.4), channel_id=1, source_target_pairs={{0,9},{1,8},{2,11},{3,10},{4,13},{5,12},{6,15},{7,14},{8,1},{9,0},... | collective-permute-start | bytes 196616 | tf_op jit(solution)/shard_map/ppermute | solution.py:219
  44.4 5.0 %collective-permute-start.24 = (bf16[128,256]{1,0:T(8,128)(2,1)S(1)}, bf16[128,256]{1,0:T(8,128)(2,1)S(1)}, u32[]{:S(2)}, u32[]{:S(2)}) collective-permute-start(bf16[128,256]{1,0:T(8,128)(2,1)S(1)} %slice.4), channel_id=1, source_target_pairs={{0,8},{8,0},{16,24},{24,16},{1,9},{9,1},{17,25},{25,17},{2,10},{10... | collective-permute-start | bytes 196616 | tf_op jit(solution)/shard_map/ppermute | solution.py:213
  (9 other events, 66.9 us)

commit v3 on v2

--- a/solution.py
+++ b/solution.py
@@ -10,6 +10,7 @@
 
 F32 = jnp.float32
 BF16 = jnp.bfloat16
+STRIP = 16
 LAST = (((1,), (1,)), ((), ()))
 FIRST = (((0,), (0,)), ((), ()))
 
@@ -115,12 +116,11 @@
     return jax.ShapeDtypeStruct(shape, dtype)
 
 
-def call(kernel, outs, args, name, smem=0, after=(), cost=None):
+def call(kernel, outs, args, name, after=(), cost=None):
     single = not isinstance(outs, (list, tuple))
     outs = [outs] if single else list(outs)
     count = len(args)
-    in_specs = [pl.BlockSpec(memory_space=pltpu.SMEM)] * smem
-    in_specs += [pl.BlockSpec(memory_space=pltpu.VMEM)] * (count - smem)
+    in_specs = [pl.BlockSpec(memory_space=pltpu.VMEM)] * count
     in_specs += [pl.BlockSpec(memory_space=pl.ANY)] * len(after)
 
     def body(*refs):
@@ -143,13 +143,13 @@
     return jnp.dot(a, b, preferred_element_type=F32)
 
 
-def build_cell(place, tile_counts, tile_rows, tile_cols, tiles, grid_rows, grid_cols):
+def build_cell(tile_counts, tile_rows, tile_cols, tiles, grid_rows, grid_cols):
     total, edge = tiles.shape[0], tiles.shape[-1]
     group = 16 if total % 16 == 0 else total
     groups = total // group
     half = grid_cols // 2
 
-    def body(place_ref, *refs):
+    def body(*refs):
         count_ref, rows_hbm, cols_hbm, tiles_hbm, cell_ref = refs[:5]
         sums, vals, rows, cols, sems = refs[5:]
         copies = [
@@ -162,7 +162,7 @@
         for copy in copies:
             copy.start()
         sums[...] = jnp.zeros_like(sums)
-        my_row, my_col = place_ref[0], place_ref[1]
+        my_row, my_col = lax.axis_index("row"), lax.axis_index("col")
 
         def add_tile(k, carry):
             near = rows[k] ^ my_col
@@ -191,7 +191,7 @@
     return pl.pallas_call(
         body,
         out_shape=sds((grid_cols * edge, grid_rows * edge), BF16),
-        in_specs=[pl.BlockSpec(memory_space=pltpu.SMEM)] * 2 + [held] * 3,
+        in_specs=[pl.BlockSpec(memory_space=pltpu.SMEM)] + [held] * 3,
         out_specs=pl.BlockSpec(memory_space=pltpu.VMEM),
         scratch_shapes=[
             pltpu.VMEM((grid_rows * grid_cols, edge, edge), F32),
@@ -205,7 +205,7 @@
             flops=1 << 24, bytes_accessed=4 * total * edge * edge, transcendentals=0
         ),
         name="build_cell",
-    )(place, tile_counts, *stored)
+    )(tile_counts, *stored)
 
 
 def swap(value, axis, distance):
@@ -236,12 +236,11 @@
     half = grid_cols // 2
     n, width = node_feats.shape
     grad_scale = 1.0 / math.sqrt(grid_rows * grid_cols * n)
-    place = jnp.stack([lax.axis_index("row"), lax.axis_index("col")])
 
     feats = [node_feats] + [swap(node_feats, "row", k) for k in range(1, grid_rows)]
 
     cell = build_cell(
-        place, tile_counts, tile_rows[0, 0], tile_cols[0, 0], tiles[0, 0], grid_rows, grid_cols
+        tile_counts, tile_rows[0, 0], tile_cols[0, 0], tiles[0, 0], grid_rows, grid_cols
     )
 
     def prepare(x_ref, w_ref, b_ref, d_ref, pre_ref, deg_ref, degrow_ref):
@@ -301,10 +300,10 @@
     small = sds((piece + pad, width), BF16)
     inward = half - 1
 
-    def dense(place_ref, own_ref, *refs):
+    def dense(own_ref, *refs):
         in_refs, refs = refs[:inward], refs[inward:]
-        x_ref, pre_ref, deg_ref, degrow_ref, ws_ref, wn_ref, g_ref = refs[:7]
-        spread_ref, preact_ref, back_ref, *out_refs = refs[7:]
+        x_ref, pre_ref, deg_ref, degrow_ref, wn_ref, g_ref = refs[:6]
+        spread_ref, preact_ref, dpre_ref, *out_refs = refs[6:]
         total = own_ref[...]
         for ref in in_refs:
             total = total + ref[...].astype(F32)
@@ -315,9 +314,10 @@
         s = jax.nn.sigmoid(v)
         dpre = g_ref[...].astype(F32) * s * (1.0 + v * (1.0 - s))
         dpre_b = dpre.astype(BF16)
+        dpre_ref[...] = dpre_b
         line = jnp.broadcast_to(jnp.sum(dpre, axis=0, keepdims=True), (pad, width)).astype(BF16)
-        on_first = (place_ref[1] & 1) == 0
-        on_left = (place_ref[0] & 1) == 0
+        on_first = (lax.axis_index("col") & 1) == 0
+        on_left = (lax.axis_index("row") & 1) == 0
         feats_own = x_ref[...]
         mine = jnp.where(on_first, feats_own, agg)
         other = jnp.where(on_first, agg, feats_own)
@@ -334,25 +334,21 @@
             ref[piece:] = line
         back = lax.dot_general(wn_ref[...], dpre_b, LAST, preferred_element_type=F32)
         spread_ref[...] = (back / degrow_ref[...]).astype(BF16)
-        back_ref[...] = lax.dot_general(ws_ref[...], dpre_b, LAST, preferred_element_type=F32)
-
-    spread, preact, own_grad, g_own, g_core, g_side, g_corner = call(
+
+    spread, preact, dpre_b, g_own, g_core, g_side, g_corner = call(
         dense,
-        [sds((width, n), BF16), sds((n, width), F32), sds((width, n), F32)] + [small] * 4,
+        [sds((width, n), BF16), sds((n, width), F32), sds((n, width), BF16)] + [small] * 4,
         [
-            place,
             own_sum,
             *parts_in[::-1],
             node_feats,
             pre,
             deg,
             deg_row,
-            self_weight,
             neigh_weight,
             out_grad,
         ],
         "dense",
-        smem=1,
     )
     near = [spread] + [swap(spread, "col", 2 * q) for q in range(1, half)]
 
@@ -378,37 +374,44 @@
         back_first, sds((width, grid_rows * n), F32), [cell, *near], "back_first", cost=work
     )
 
-    def back_second(cell_ref, a_ref, base_ref, *refs):
+    def back_second(cell_ref, a_ref, *refs):
         s_refs, out_refs = refs[:half], refs[half:]
         left = jnp.concatenate([r[...] for r in s_refs], axis=1)
         total = a_ref[...] + dot(left, cell_ref[half * n :, :])
-        out_refs[0][...] = total[:, :n] + base_ref[...]
+        out_refs[0][...] = total[:, :n]
         for k in range(1, grid_rows):
             out_refs[k][...] = total[:, k * n : (k + 1) * n].astype(BF16)
 
     own_back, *back_parts = call(
         back_second,
         [sds((width, n), F32)] + [sds((width, n), BF16)] * (grid_rows - 1),
-        [cell, back_a, own_grad, *far],
+        [cell, back_a, *far],
         "back_second",
         cost=work,
     )
     back_in = [swap(part, "row", k + 1) for k, part in enumerate(back_parts)]
 
-    def activate(v_ref, hid_ref):
+    def activate(v_ref, w_ref, d_ref, hid_ref, own_ref):
         v = v_ref[...]
         hid_ref[...] = (v * jax.nn.sigmoid(v)).astype(BF16)
-
-    hidden = call(activate, sds((n, width), BF16), [preact], "activate", after=[own_back])
-
-    def finish(own_ref, *refs):
+        own_ref[...] = lax.dot_general(w_ref[...], d_ref[...], LAST, preferred_element_type=F32)
+
+    hidden, own_grad = call(
+        activate,
+        [sds((n, width), BF16), sds((width, n), F32)],
+        [preact, self_weight, dpre_b],
+        "activate",
+        after=[own_back],
+    )
+
+    def finish(grad_ref, own_ref, *refs):
         *in_refs, out_ref = refs
-        total = own_ref[...]
+        total = grad_ref[...] + own_ref[...]
         for ref in in_refs:
             total = total + ref[...].astype(F32)
         out_ref[...] = total.T.astype(BF16)
 
-    feat_grad = call(finish, sds((n, width), BF16), [own_back, *back_in], "finish")
+    feat_grad = call(finish, sds((n, width), BF16), [own_grad, own_back, *back_in], "finish")
 
     z_part = g_part
     for got in y_in:
@@ -418,55 +421,67 @@
     pieces = g_piece[:piece]
     pieces_in = [swap_corner(pieces), swap(pieces, "row", 1), swap(pieces, "col", 1)]
 
-    def write(flip, place_ref, a_ref, b_ref, self_hbm, neigh_hbm, blocks, sems):
-        first = (place_ref[1] & 1) == 0
-        row = (place_ref[0] & 1) ^ flip
-        span = pl.ds(pl.multiple_of(row * piece, piece), piece)
-        a = a_ref[:piece].astype(F32) * grad_scale
-        b = b_ref[:piece].astype(F32) * grad_scale
-        copies = []
-        for j, (value, out) in enumerate(
-            ((jnp.where(first, a, b), self_hbm), (jnp.where(first, b, a), neigh_hbm))
-        ):
-            blocks[j] = value
-            copies.append(pltpu.make_async_copy(blocks.at[j], out.at[span], sems.at[j]))
-            copies[-1].start()
-        for copy in copies:
-            copy.wait()
-
-    def write_first(place_ref, a_ref, b_ref, self_hbm, neigh_hbm, bias_ref, blocks, sems):
-        bias_ref[...] = a_ref[piece : piece + 1].astype(F32) * grad_scale
-        write(0, place_ref, a_ref, b_ref, self_hbm, neigh_hbm, blocks, sems)
-
-    def write_second(place_ref, a_ref, b_ref, s_ref, n_ref, self_hbm, neigh_hbm, blocks, sems):
-        write(1, place_ref, a_ref, b_ref, self_hbm, neigh_hbm, blocks, sems)
+    def write(parts, hbms, blocks, sems):
+        x, c = lax.axis_index("row") & 1, lax.axis_index("col") & 1
+        for j, (ref, side, core) in enumerate(parts):
+            blocks[j] = ref[:piece].astype(F32) * grad_scale
+            base = (x ^ side) * piece
+            for which, hbm in enumerate(hbms):
+
+                @pl.when((c ^ core) == which)
+                def _():
+                    for i in range(0, piece, STRIP):
+                        to = pl.ds(pl.multiple_of(base + i, STRIP), STRIP)
+                        pltpu.make_async_copy(
+                            blocks.at[j, pl.ds(i, STRIP)], hbm.at[to], sems.at[j]
+                        ).start()
+
+    def drain(count, hbm, blocks, sems):
+        for j in range(count):
+            pltpu.make_async_copy(blocks.at[j], hbm.at[pl.ds(0, piece)], sems.at[j]).wait()
+
+    def write_first(a_ref, b_ref, self_hbm, neigh_hbm, bias_hbm, blocks, sems, line):
+        line[...] = a_ref[piece : piece + 1].astype(F32) * grad_scale
+        copy = pltpu.make_async_copy(line, bias_hbm, sems.at[2])
+        copy.start()
+        parts = ((a_ref, 0, 0), (b_ref, 0, 1))
+        write(parts, (self_hbm, neigh_hbm), blocks, sems)
+        drain(2, self_hbm, blocks, sems)
+        copy.wait()
+
+    def write_next(core, a_ref, s_ref, n_ref, self_hbm, neigh_hbm, blocks, sems):
+        write(((a_ref, 1, core),), (self_hbm, neigh_hbm), blocks, sems)
+        drain(1, self_hbm, blocks, sems)
 
     held, fast = (pl.BlockSpec(memory_space=m) for m in (pltpu.HBM, pltpu.VMEM))
     whole = [sds((width, width), F32)] * 2
     common = dict(
-        scratch_shapes=[pltpu.VMEM((2, piece, width), F32), pltpu.SemaphoreType.DMA((2,))],
         compiler_params=pltpu.CompilerParams(vmem_limit_bytes=24 << 20),
         cost_estimate=pl.CostEstimate(flops=1 << 20, bytes_accessed=1 << 18, transcendentals=0),
     )
-    scalars = pl.BlockSpec(memory_space=pltpu.SMEM)
+    scratch = [pltpu.VMEM((2, piece, width), F32), pltpu.SemaphoreType.DMA((3,))]
     corner_in, side_in, core_in = pieces_in
     *grads, grad_bias = pl.pallas_call(
         write_first,
         out_shape=whole + [sds((1, width), F32)],
-        in_specs=[scalars, fast, fast],
-        out_specs=[held, held, fast],
+        in_specs=[fast, fast],
+        out_specs=[held, held, held],
+        scratch_shapes=scratch + [pltpu.VMEM((1, width), F32)],
         name="write_first",
         **common,
-    )(place, g_piece, core_in)
-    grad_self, grad_neigh = pl.pallas_call(
-        write_second,
-        out_shape=whole,
-        in_specs=[scalars, fast, fast, held, held],
-        out_specs=[held, held],
-        input_output_aliases={3: 0, 4: 1},
-        name="write_second",
-        **common,
-    )(place, side_in, corner_in, *grads)
+    )(g_piece, core_in)
+    for core, got in ((1, corner_in), (0, side_in)):
+        grads = pl.pallas_call(
+            functools.partial(write_next, core),
+            out_shape=whole,
+            in_specs=[fast, held, held],
+            out_specs=[held, held],
+            input_output_aliases={1: 0, 2: 1},
+            scratch_shapes=scratch,
+            name="write_next",
+            **common,
+        )(got, *grads)
+    grad_self, grad_neigh = grads
     return hidden, feat_grad, grad_self, grad_neigh, grad_bias.reshape(width)
 
 

time: 50.8 us -> 49.6 us (0.976)
  Pallas kernels: 9.47 us -> 7.42 us
  waiting for transfers between devices: 11.4 us -> 12.7 us
    ppermute x25, waiting for transfers between devices: 11.4 us -> 12.7 us  [swap(): return lax.ppermute(value, axis, [(i, i ^ distance) for i in range(size)])]
    pallas_call x1, Pallas kernels: 1.84 us -> 0.73 us  [direct_form(): pl.pallas_call(write_first, out_shape=whole + [sds((1, width), F32)], in_...]
    pallas_call x1, Pallas kernels: 2.41 us -> 1.87 us  [build_cell(): pl.pallas_call(body, out_shape=sds((grid_cols * edge, grid_rows * edge),...]
    ppermute x25, starting transfers between devices: 26.3 us -> 25.8 us  [swap(): return lax.ppermute(value, axis, [(i, i ^ distance) for i in range(size)])]
    pallas_call x1 -> x2, Pallas kernels: 1.28 us -> 1.38 us  [direct_form(): pl.pallas_call(functools.partial(write_next, core), out_shape=whole, in_s...]
  transfers between devices with their start and end apart: 27 -> 27, of which waited for: 10 -> 10; matrix products, arithmetic and copies ran while one was open for 0% -> 0% of each run, Pallas kernels for 13% -> 12%
where the time goes in v3:
time: 49.6 us; the launch traced here: 49.5 us
  starting transfers between devices  27.8 us (56%)
  waiting for transfers between devices  12.7 us (26%)
  Pallas kernels  7.42 us (15%)
  between operations  1.49 us (3%)
    ppermute x25, starting transfers between devices, swap(): return lax.ppermute(value, axis, [(i, i ^ distance) for i in range(size)])  25.8 us
    ppermute x25, waiting for transfers between devices, swap(): return lax.ppermute(value, axis, [(i, i ^ distance) for i in range(size)])  12.7 us
    pallas_call x12, Pallas kernels, call(): pl.pallas_call(body, out_shape=outs, in_specs=in_specs, out_specs=[pl.Blo...  3.44 us
    ppermute x2, starting transfers between devices, swap_corner(): lax.ppermute(value, ('row', 'col'), [(i, i ^ step) for i in range(size)])  2.06 us
    pallas_call x1, Pallas kernels, build_cell(): pl.pallas_call(body, out_shape=sds((grid_cols * edge, grid_rows * edge),...  1.87 us
    pallas_call x2, Pallas kernels, direct_form(): pl.pallas_call(functools.partial(write_next, core), out_shape=whole, in_s...  1.38 us
  transfers between devices with their start and end apart: 27, of which 10 were waited for; matrix products, arithmetic and copies ran while one was open for 0% of the time, Pallas kernels for 12%

profile of v3, /device:TPU:0, one launch (start us, length us, event | category | flops | bytes accessed | tf_op | source)
XLA Modules:
  0.0 49.5 jit_solution(4772838039099954905)
XLA Ops:
  0.6 4.0 %collective-permute-start.2 = (bf16[128,256]{1,0:T(8,128)(2,1)}, bf16[128,256]{1,0:T(8,128)(2,1)S(1)}, u32[]{:S(2)}, u32[]{:S(2)}) collective-permute-start(bf16[128,256]{1,0:T(8,128)(2,1)} %refs_4_.1), channel_id=1, source_target_pairs={{0,24},{8,16},{16,8},{24,0},{1,25},{9,17},{17,9},{25,1},{2,26},{10... | collective-permute-start | bytes 196616 | tf_op jit(solution)/shard_map/ppermute | solution.py:213
  5.9 1.9 %build_cell.1.refs_0_ = bf16[1024,512]{1,0:T(8,128)(2,1)S(1)} custom-call(s32[1,1]{1,0:T(1,128)S(6)} %copy.23.refs_0_, s32[80]{0:T(128)} %bitcast.9, s32[80]{0:T(128)} %bitcast.10, bf16[80,128,128]{2,1,0:T(8,128)(2,1)} %bitcast.8), custom_call_target="tpu_custom_call" | custom-call | flops 16777216 | bytes 5242880 | tf_op jit(solution)/shard_map/build_cell/pallas_call | solution.py:191
  7.9 1.2 %collective-permute-done.1.refs_3_ = bf16[128,256]{1,0:T(8,128)(2,1)S(1)} collective-permute-done((bf16[128,256]{1,0:T(8,128)(2,1)}, bf16[128,256]{1,0:T(8,128)(2,1)S(1)}, u32[]{:S(2)}, u32[]{:S(2)}) %collective-permute-start.1) | collective-permute-done | bytes 65568 | tf_op jit(solution)/shard_map/ppermute | solution.py:213
  10.3 1.2 %collective-permute-done.3.refs_1_ = bf16[512,256]{1,0:T(8,128)(2,1)S(1)} collective-permute-done((bf16[512,256]{1,0:T(8,128)(2,1)S(1)}, bf16[512,256]{1,0:T(8,128)(2,1)S(1)}, u32[]{:S(2)}, u32[]{:S(2)}) %collective-permute-start.3) | collective-permute-done | bytes 262176 | tf_op jit(solution)/shard_map/ppermute | solution.py:213
  11.6 3.7 %collective-permute-start.4 = (bf16[128,256]{1,0:T(8,128)(2,1)S(1)}, bf16[128,256]{1,0:T(8,128)(2,1)S(1)}, u32[]{:S(2)}, u32[]{:S(2)}) collective-permute-start(bf16[128,256]{1,0:T(8,128)(2,1)S(1)} %get-tuple-element.33), channel_id=1, source_target_pairs={{0,6},{1,7},{2,4},{3,5},{4,2},{5,3},{6,0},{7,1},{8,14},{9,15},{10,... | collective-permute-start | bytes 196616 | tf_op jit(solution)/shard_map/ppermute | solution.py:213
  15.2 0.8 %collective-permute-start.6 = (bf16[128,256]{1,0:T(8,128)(2,1)S(1)}, bf16[128,256]{1,0:T(8,128)(2,1)S(1)}, u32[]{:S(2)}, u32[]{:S(2)}) collective-permute-start(bf16[128,256]{1,0:T(8,128)(2,1)S(1)} %get-tuple-element.35), channel_id=1, source_target_pairs={{0,2},{1,3},{2,0},{3,1},{4,6},{5,7},{6,4},{7,5},{8,10},{9,11},{10,... | collective-permute-start | bytes 196616 | tf_op jit(solution)/shard_map/ppermute | solution.py:213
  16.2 1.7 %collective-permute-done.4.refs_1_ = bf16[128,256]{1,0:T(8,128)(2,1)S(1)} collective-permute-done((bf16[128,256]{1,0:T(8,128)(2,1)S(1)}, bf16[128,256]{1,0:T(8,128)(2,1)S(1)}, u32[]{:S(2)}, u32[]{:S(2)}) %collective-permute-start.4) | collective-permute-done | bytes 65568 | tf_op jit(solution)/shard_map/ppermute | solution.py:213
  17.9 3.3 %collective-permute-done.5.refs_2_ = bf16[128,256]{1,0:T(8,128)(2,1)S(1)} collective-permute-done((bf16[128,256]{1,0:T(8,128)(2,1)S(1)}, bf16[128,256]{1,0:T(8,128)(2,1)S(1)}, u32[]{:S(2)}, u32[]{:S(2)}) %collective-permute-start.5) | collective-permute-done | bytes 65568 | tf_op jit(solution)/shard_map/ppermute | solution.py:213
  22.3 1.2 %collective-permute-start.19 = (bf16[144,256]{1,0:T(8,128)(2,1)S(1)}, bf16[144,256]{1,0:T(8,128)(2,1)S(1)}, u32[]{:S(2)}, u32[]{:S(2)}) collective-permute-start(bf16[144,256]{1,0:T(8,128)(2,1)S(1)} %get-tuple-element.51), channel_id=1, source_target_pairs={{0,9},{1,8},{2,11},{3,10},{4,13},{5,12},{6,15},{7,14},{8,1},{9,0},... | collective-permute-start | bytes 221192 | tf_op jit(solution)/shard_map/ppermute | solution.py:219
  23.5 2.5 %collective-permute-start.9 = (bf16[256,128]{1,0:T(8,128)(2,1)S(1)}, bf16[256,128]{1,0:T(8,128)(2,1)S(1)}, u32[]{:S(2)}, u32[]{:S(2)}) collective-permute-start(bf16[256,128]{1,0:T(8,128)(2,1)S(1)} %get-tuple-element.41.refs_1_), channel_id=1, source_target_pairs={{0,6},{1,7},{2,4},{3,5},{4,2},{5,3},{6,0},{7,1},{8,14},{9,15},{10,... | collective-permute-start | bytes 196616 | tf_op jit(solution)/shard_map/ppermute | solution.py:213
  26.1 1.8 %collective-permute-start.7 = (bf16[256,128]{1,0:T(8,128)(2,1)S(1)}, bf16[256,128]{1,0:T(8,128)(2,1)S(1)}, u32[]{:S(2)}, u32[]{:S(2)}) collective-permute-start(bf16[256,128]{1,0:T(8,128)(2,1)S(1)} %get-tuple-element.41.refs_1_), channel_id=1, source_target_pairs={{0,2},{1,3},{2,0},{3,1},{4,6},{5,7},{6,4},{7,5},{8,10},{9,11},{10,... | collective-permute-start | bytes 196616 | tf_op jit(solution)/shard_map/ppermute | solution.py:213
  28.0 1.6 %collective-permute-start.20 = (bf16[144,256]{1,0:T(8,128)(2,1)S(1)}, bf16[144,256]{1,0:T(8,128)(2,1)S(1)}, u32[]{:S(2)}, u32[]{:S(2)}) collective-permute-start(bf16[144,256]{1,0:T(8,128)(2,1)S(1)} %add_corner.1.refs_0_), channel_id=1, source_target_pairs={{0,16},{8,24},{16,0},{24,8},{1,17},{9,25},{17,1},{25,9},{2,18},{10... | collective-permute-start | bytes 221192 | tf_op jit(solution)/shard_map/ppermute | solution.py:213
  29.6 0.8 %collective-permute-done.9.refs_4_ = bf16[256,128]{1,0:T(8,128)(2,1)S(1)} collective-permute-done((bf16[256,128]{1,0:T(8,128)(2,1)S(1)}, bf16[256,128]{1,0:T(8,128)(2,1)S(1)}, u32[]{:S(2)}, u32[]{:S(2)}) %collective-permute-start.9) | collective-permute-done | bytes 65568 | tf_op jit(solution)/shard_map/ppermute | solution.py:213
  30.4 2.2 %collective-permute-done.8.refs_3_ = bf16[256,128]{1,0:T(8,128)(2,1)S(1)} collective-permute-done((bf16[256,128]{1,0:T(8,128)(2,1)S(1)}, bf16[256,128]{1,0:T(8,128)(2,1)S(1)}, u32[]{:S(2)}, u32[]{:S(2)}) %collective-permute-start.8) | collective-permute-done | bytes 65568 | tf_op jit(solution)/shard_map/ppermute | solution.py:213
  33.5 2.4 %collective-permute-start.23 = (bf16[144,256]{1,0:T(8,128)(2,1)S(1)}, bf16[144,256]{1,0:T(8,128)(2,1)S(1)}, u32[]{:S(2)}, u32[]{:S(2)}) collective-permute-start(bf16[144,256]{1,0:T(8,128)(2,1)S(1)} %add_y.1.refs_0_), channel_id=1, source_target_pairs={{0,6},{1,7},{2,4},{3,5},{4,2},{5,3},{6,0},{7,1},{8,14},{9,15},{10,... | collective-permute-start | bytes 221192 | tf_op jit(solution)/shard_map/ppermute | solution.py:213
  35.9 2.0 %collective-permute-start.21 = (bf16[144,256]{1,0:T(8,128)(2,1)S(1)}, bf16[144,256]{1,0:T(8,128)(2,1)S(1)}, u32[]{:S(2)}, u32[]{:S(2)}) collective-permute-start(bf16[144,256]{1,0:T(8,128)(2,1)S(1)} %add_y.1.refs_0_), channel_id=1, source_target_pairs={{0,2},{1,3},{2,0},{3,1},{4,6},{5,7},{6,4},{7,5},{8,10},{9,11},{10,... | collective-permute-start | bytes 221192 | tf_op jit(solution)/shard_map/ppermute | solution.py:213
  38.9 1.5 %collective-permute-start.15 = (bf16[256,128]{1,0:T(8,128)(2,1)S(1)}, bf16[256,128]{1,0:T(8,128)(2,1)S(1)}, u32[]{:S(2)}, u32[]{:S(2)}) collective-permute-start(bf16[256,128]{1,0:T(8,128)(2,1)S(1)} %get-tuple-element.46), channel_id=1, source_target_pairs={{0,16},{8,24},{16,0},{24,8},{1,17},{9,25},{17,1},{25,9},{2,18},{10... | collective-permute-start | bytes 196616 | tf_op jit(solution)/shard_map/ppermute | solution.py:213
  40.5 1.5 %collective-permute-start.16 = (bf16[256,128]{1,0:T(8,128)(2,1)S(1)}, bf16[256,128]{1,0:T(8,128)(2,1)S(1)}, u32[]{:S(2)}, u32[]{:S(2)}) collective-permute-start(bf16[256,128]{1,0:T(8,128)(2,1)S(1)} %get-tuple-element.47), channel_id=1, source_target_pairs={{0,24},{8,16},{16,8},{24,0},{1,25},{9,17},{17,9},{25,1},{2,26},{10... | collective-permute-start | bytes 196616 | tf_op jit(solution)/shard_map/ppermute | solution.py:213
  42.0 0.8 %collective-permute-done.22.refs_2_ = bf16[144,256]{1,0:T(8,128)(2,1)S(1)} collective-permute-done((bf16[144,256]{1,0:T(8,128)(2,1)S(1)}, bf16[144,256]{1,0:T(8,128)(2,1)S(1)}, u32[]{:S(2)}, u32[]{:S(2)}) %collective-permute-start.22) | collective-permute-done | bytes 73760 | tf_op jit(solution)/shard_map/ppermute | solution.py:213
  42.9 0.8 %collective-permute-start.25 = (bf16[128,256]{1,0:T(8,128)(2,1)S(1)}, bf16[128,256]{1,0:T(8,128)(2,1)S(1)}, u32[]{:S(2)}, u32[]{:S(2)}) collective-permute-start(bf16[128,256]{1,0:T(8,128)(2,1)S(1)} %slice.4), channel_id=1, source_target_pairs={{0,9},{1,8},{2,11},{3,10},{4,13},{5,12},{6,15},{7,14},{8,1},{9,0},... | collective-permute-start | bytes 196616 | tf_op jit(solution)/shard_map/ppermute | solution.py:219
  43.7 1.3 %collective-permute-start.24 = (bf16[128,256]{1,0:T(8,128)(2,1)S(1)}, bf16[128,256]{1,0:T(8,128)(2,1)S(1)}, u32[]{:S(2)}, u32[]{:S(2)}) collective-permute-start(bf16[128,256]{1,0:T(8,128)(2,1)S(1)} %slice.4), channel_id=1, source_target_pairs={{0,8},{8,0},{16,24},{24,16},{1,9},{9,1},{17,25},{25,17},{2,10},{10... | collective-permute-start | bytes 196616 | tf_op jit(solution)/shard_map/ppermute | solution.py:213
  45.8 0.7 %finish.1 = bf16[128,256]{1,0:T(8,128)(2,1)} custom-call(f32[256,128]{1,0:T(8,128)S(1)} %get-tuple-element.44.refs_0_, f32[256,128]{1,0:T(8,128)S(1)} %get-tuple-element.42.refs_3_.refs_1_.refs_4_, bf16[256,128]{1,0:T(8,128)(2,1)S(1)} %collective-permute-done.14.refs_2_, bf16[256,128]{1,0:T(8,128)(2,1)S(1)} %collective-permute-done.15.refs_3_, ...), custom_call_target="tpu_custom_call" | custom-call | flops 1048576 | bytes 262144 | tf_op jit(solution)/shard_map/finish/pallas_call | solution.py:130
  46.5 0.7 %write_first.1 = (f32[256,256]{1,0:T(8,128)}, f32[256,256]{1,0:T(8,128)}, f32[1,256]{1,0:T(1,128)}) custom-call(bf16[144,256]{1,0:T(8,128)(2,1)S(1)} %add_z.1.a_ref, bf16[128,256]{1,0:T(8,128)(2,1)S(1)} %collective-permute-done.26.b_ref), custom_call_target="tpu_custom_call" | custom-call | flops 1048576 | bytes 262144 | tf_op jit(solution)/shard_map/write_first/pallas_call | solution.py:464
  48.0 0.8 %collective-permute-done.24.a_ref = bf16[128,256]{1,0:T(8,128)(2,1)S(1)} collective-permute-done((bf16[128,256]{1,0:T(8,128)(2,1)S(1)}, bf16[128,256]{1,0:T(8,128)(2,1)S(1)}, u32[]{:S(2)}, u32[]{:S(2)}) %collective-permute-start.24) | collective-permute-done | bytes 65568 | tf_op jit(solution)/shard_map/ppermute | solution.py:213
  (59 shorter events, 7.4 us)
Async XLA Ops:
  0.6 7.2 %collective-permute-start.2 = (bf16[128,256]{1,0:T(8,128)(2,1)}, bf16[128,256]{1,0:T(8,128)(2,1)S(1)}, u32[]{:S(2)}, u32[]{:S(2)}) collective-permute-start(bf16[128,256]{1,0:T(8,128)(2,1)} %refs_4_.1), channel_id=1, source_target_pairs={{0,24},{8,16},{16,8},{24,0},{1,25},{9,17},{17,9},{25,1},{2,26},{10... | collective-permute-start | bytes 196616 | tf_op jit(solution)/shard_map/ppermute | solution.py:213
  4.6 4.5 %collective-permute-start.1 = (bf16[128,256]{1,0:T(8,128)(2,1)}, bf16[128,256]{1,0:T(8,128)(2,1)S(1)}, u32[]{:S(2)}, u32[]{:S(2)}) collective-permute-start(bf16[128,256]{1,0:T(8,128)(2,1)} %refs_4_.1), channel_id=1, source_target_pairs={{0,16},{8,24},{16,0},{24,8},{1,17},{9,25},{17,1},{25,9},{2,18},{10... | collective-permute-start | bytes 196616 | tf_op jit(solution)/shard_map/ppermute | solution.py:213
  5.1 4.5 %collective-permute-start = (bf16[128,256]{1,0:T(8,128)(2,1)}, bf16[128,256]{1,0:T(8,128)(2,1)S(1)}, u32[]{:S(2)}, u32[]{:S(2)}) collective-permute-start(bf16[128,256]{1,0:T(8,128)(2,1)} %refs_4_.1), channel_id=1, source_target_pairs={{0,8},{8,0},{16,24},{24,16},{1,9},{9,1},{17,25},{25,17},{2,10},{10... | collective-permute-start | bytes 196616 | tf_op jit(solution)/shard_map/ppermute | solution.py:213
  11.6 6.3 %collective-permute-start.4 = (bf16[128,256]{1,0:T(8,128)(2,1)S(1)}, bf16[128,256]{1,0:T(8,128)(2,1)S(1)}, u32[]{:S(2)}, u32[]{:S(2)}) collective-permute-start(bf16[128,256]{1,0:T(8,128)(2,1)S(1)} %get-tuple-element.33), channel_id=1, source_target_pairs={{0,6},{1,7},{2,4},{3,5},{4,2},{5,3},{6,0},{7,1},{8,14},{9,15},{10,... | collective-permute-start | bytes 196616 | tf_op jit(solution)/shard_map/ppermute | solution.py:213
  15.2 5.9 %collective-permute-start.5 = (bf16[128,256]{1,0:T(8,128)(2,1)S(1)}, bf16[128,256]{1,0:T(8,128)(2,1)S(1)}, u32[]{:S(2)}, u32[]{:S(2)}) collective-permute-start(bf16[128,256]{1,0:T(8,128)(2,1)S(1)} %get-tuple-element.34), channel_id=1, source_target_pairs={{0,4},{1,5},{2,6},{3,7},{4,0},{5,1},{6,2},{7,3},{8,12},{9,13},{10,... | collective-permute-start | bytes 196616 | tf_op jit(solution)/shard_map/ppermute | solution.py:213
  15.2 5.9 %collective-permute-start.6 = (bf16[128,256]{1,0:T(8,128)(2,1)S(1)}, bf16[128,256]{1,0:T(8,128)(2,1)S(1)}, u32[]{:S(2)}, u32[]{:S(2)}) collective-permute-start(bf16[128,256]{1,0:T(8,128)(2,1)S(1)} %get-tuple-element.35), channel_id=1, source_target_pairs={{0,2},{1,3},{2,0},{3,1},{4,6},{5,7},{6,4},{7,5},{8,10},{9,11},{10,... | collective-permute-start | bytes 196616 | tf_op jit(solution)/shard_map/ppermute | solution.py:213
  21.6 4.5 %collective-permute-start.17 = (bf16[144,256]{1,0:T(8,128)(2,1)S(1)}, bf16[144,256]{1,0:T(8,128)(2,1)S(1)}, u32[]{:S(2)}, u32[]{:S(2)}) collective-permute-start(bf16[144,256]{1,0:T(8,128)(2,1)S(1)} %get-tuple-element.49), channel_id=1, source_target_pairs={{0,1},{1,0},{2,3},{3,2},{4,5},{5,4},{6,7},{7,6},{8,9},{9,8},{10,11... | collective-permute-start | bytes 221192 | tf_op jit(solution)/shard_map/ppermute | solution.py:213
  21.7 6.2 %collective-permute-start.18 = (bf16[144,256]{1,0:T(8,128)(2,1)S(1)}, bf16[144,256]{1,0:T(8,128)(2,1)S(1)}, u32[]{:S(2)}, u32[]{:S(2)}) collective-permute-start(bf16[144,256]{1,0:T(8,128)(2,1)S(1)} %get-tuple-element.50), channel_id=1, source_target_pairs={{0,8},{8,0},{16,24},{24,16},{1,9},{9,1},{17,25},{25,17},{2,10},{10... | collective-permute-start | bytes 221192 | tf_op jit(solution)/shard_map/ppermute | solution.py:213
  22.3 5.6 %collective-permute-start.19 = (bf16[144,256]{1,0:T(8,128)(2,1)S(1)}, bf16[144,256]{1,0:T(8,128)(2,1)S(1)}, u32[]{:S(2)}, u32[]{:S(2)}) collective-permute-start(bf16[144,256]{1,0:T(8,128)(2,1)S(1)} %get-tuple-element.51), channel_id=1, source_target_pairs={{0,9},{1,8},{2,11},{3,10},{4,13},{5,12},{6,15},{7,14},{8,1},{9,0},... | collective-permute-start | bytes 221192 | tf_op jit(solution)/shard_map/ppermute | solution.py:219
  23.5 6.9 %collective-permute-start.9 = (bf16[256,128]{1,0:T(8,128)(2,1)S(1)}, bf16[256,128]{1,0:T(8,128)(2,1)S(1)}, u32[]{:S(2)}, u32[]{:S(2)}) collective-permute-start(bf16[256,128]{1,0:T(8,128)(2,1)S(1)} %get-tuple-element.41.refs_1_), channel_id=1, source_target_pairs={{0,6},{1,7},{2,4},{3,5},{4,2},{5,3},{6,0},{7,1},{8,14},{9,15},{10,... | collective-permute-start | bytes 196616 | tf_op jit(solution)/shard_map/ppermute | solution.py:213
  26.0 6.6 %collective-permute-start.8 = (bf16[256,128]{1,0:T(8,128)(2,1)S(1)}, bf16[256,128]{1,0:T(8,128)(2,1)S(1)}, u32[]{:S(2)}, u32[]{:S(2)}) collective-permute-start(bf16[256,128]{1,0:T(8,128)(2,1)S(1)} %get-tuple-element.41.refs_1_), channel_id=1, source_target_pairs={{0,4},{1,5},{2,6},{3,7},{4,0},{5,1},{6,2},{7,3},{8,12},{9,13},{10,... | collective-permute-start | bytes 196616 | tf_op jit(solution)/shard_map/ppermute | solution.py:213
  26.1 6.6 %collective-permute-start.7 = (bf16[256,128]{1,0:T(8,128)(2,1)S(1)}, bf16[256,128]{1,0:T(8,128)(2,1)S(1)}, u32[]{:S(2)}, u32[]{:S(2)}) collective-permute-start(bf16[256,128]{1,0:T(8,128)(2,1)S(1)} %get-tuple-element.41.refs_1_), channel_id=1, source_target_pairs={{0,2},{1,3},{2,0},{3,1},{4,6},{5,7},{6,4},{7,5},{8,10},{9,11},{10,... | collective-permute-start | bytes 196616 | tf_op jit(solution)/shard_map/ppermute | solution.py:213
  28.0 5.5 %collective-permute-start.20 = (bf16[144,256]{1,0:T(8,128)(2,1)S(1)}, bf16[144,256]{1,0:T(8,128)(2,1)S(1)}, u32[]{:S(2)}, u32[]{:S(2)}) collective-permute-start(bf16[144,256]{1,0:T(8,128)(2,1)S(1)} %add_corner.1.refs_0_), channel_id=1, source_target_pairs={{0,16},{8,24},{16,0},{24,8},{1,17},{9,25},{17,1},{25,9},{2,18},{10... | collective-permute-start | bytes 221192 | tf_op jit(solution)/shard_map/ppermute | solution.py:213
  29.6 6.3 %collective-permute-start.10 = (bf16[256,128]{1,0:T(8,128)(2,1)S(1)}, bf16[256,128]{1,0:T(8,128)(2,1)S(1)}, u32[]{:S(2)}, u32[]{:S(2)}) collective-permute-start(bf16[256,128]{1,0:T(8,128)(2,1)S(1)} %get-tuple-element.41.refs_1_), channel_id=1, source_target_pairs={{0,1},{1,0},{2,3},{3,2},{4,5},{5,4},{6,7},{7,6},{8,9},{9,8},{10,11... | collective-permute-start | bytes 196616 | tf_op jit(solution)/shard_map/ppermute | solution.py:213
  30.4 5.5 %collective-permute-start.13 = (bf16[256,128]{1,0:T(8,128)(2,1)S(1)}, bf16[256,128]{1,0:T(8,128)(2,1)S(1)}, u32[]{:S(2)}, u32[]{:S(2)}) collective-permute-start(bf16[256,128]{1,0:T(8,128)(2,1)S(1)} %collective-permute-done.9.refs_4_), channel_id=1, source_target_pairs={{0,1},{1,0},{2,3},{3,2},{4,5},{5,4},{6,7},{7,6},{8,9},{9,8},{10,11... | collective-permute-start | bytes 196616 | tf_op jit(solution)/shard_map/ppermute | solution.py:213
  32.6 5.3 %collective-permute-start.12 = (bf16[256,128]{1,0:T(8,128)(2,1)S(1)}, bf16[256,128]{1,0:T(8,128)(2,1)S(1)}, u32[]{:S(2)}, u32[]{:S(2)}) collective-permute-start(bf16[256,128]{1,0:T(8,128)(2,1)S(1)} %collective-permute-done.8.refs_3_), channel_id=1, source_target_pairs={{0,1},{1,0},{2,3},{3,2},{4,5},{5,4},{6,7},{7,6},{8,9},{9,8},{10,11... | collective-permute-start | bytes 196616 | tf_op jit(solution)/shard_map/ppermute | solution.py:213
  32.7 5.2 %collective-permute-start.11 = (bf16[256,128]{1,0:T(8,128)(2,1)S(1)}, bf16[256,128]{1,0:T(8,128)(2,1)S(1)}, u32[]{:S(2)}, u32[]{:S(2)}) collective-permute-start(bf16[256,128]{1,0:T(8,128)(2,1)S(1)} %collective-permute-done.7.refs_2_), channel_id=1, source_target_pairs={{0,1},{1,0},{2,3},{3,2},{4,5},{5,4},{6,7},{7,6},{8,9},{9,8},{10,11... | collective-permute-start | bytes 196616 | tf_op jit(solution)/shard_map/ppermute | solution.py:213
  33.5 7.0 %collective-permute-start.23 = (bf16[144,256]{1,0:T(8,128)(2,1)S(1)}, bf16[144,256]{1,0:T(8,128)(2,1)S(1)}, u32[]{:S(2)}, u32[]{:S(2)}) collective-permute-start(bf16[144,256]{1,0:T(8,128)(2,1)S(1)} %add_y.1.refs_0_), channel_id=1, source_target_pairs={{0,6},{1,7},{2,4},{3,5},{4,2},{5,3},{6,0},{7,1},{8,14},{9,15},{10,... | collective-permute-start | bytes 221192 | tf_op jit(solution)/shard_map/ppermute | solution.py:213
  35.9 6.9 %collective-permute-start.22 = (bf16[144,256]{1,0:T(8,128)(2,1)S(1)}, bf16[144,256]{1,0:T(8,128)(2,1)S(1)}, u32[]{:S(2)}, u32[]{:S(2)}) collective-permute-start(bf16[144,256]{1,0:T(8,128)(2,1)S(1)} %add_y.1.refs_0_), channel_id=1, source_target_pairs={{0,4},{1,5},{2,6},{3,7},{4,0},{5,1},{6,2},{7,3},{8,12},{9,13},{10,... | collective-permute-start | bytes 221192 | tf_op jit(solution)/shard_map/ppermute | solution.py:213
  35.9 6.9 %collective-permute-start.21 = (bf16[144,256]{1,0:T(8,128)(2,1)S(1)}, bf16[144,256]{1,0:T(8,128)(2,1)S(1)}, u32[]{:S(2)}, u32[]{:S(2)}) collective-permute-start(bf16[144,256]{1,0:T(8,128)(2,1)S(1)} %add_y.1.refs_0_), channel_id=1, source_target_pairs={{0,2},{1,3},{2,0},{3,1},{4,6},{5,7},{6,4},{7,5},{8,10},{9,11},{10,... | collective-permute-start | bytes 221192 | tf_op jit(solution)/shard_map/ppermute | solution.py:213
  38.3 5.5 %collective-permute-start.14 = (bf16[256,128]{1,0:T(8,128)(2,1)S(1)}, bf16[256,128]{1,0:T(8,128)(2,1)S(1)}, u32[]{:S(2)}, u32[]{:S(2)}) collective-permute-start(bf16[256,128]{1,0:T(8,128)(2,1)S(1)} %get-tuple-element.45), channel_id=1, source_target_pairs={{0,8},{8,0},{16,24},{24,16},{1,9},{9,1},{17,25},{25,17},{2,10},{10... | collective-permute-start | bytes 196616 | tf_op jit(solution)/shard_map/ppermute | solution.py:213
  38.9 6.9 %collective-permute-start.15 = (bf16[256,128]{1,0:T(8,128)(2,1)S(1)}, bf16[256,128]{1,0:T(8,128)(2,1)S(1)}, u32[]{:S(2)}, u32[]{:S(2)}) collective-permute-start(bf16[256,128]{1,0:T(8,128)(2,1)S(1)} %get-tuple-element.46), channel_id=1, source_target_pairs={{0,16},{8,24},{16,0},{24,8},{1,17},{9,25},{17,1},{25,9},{2,18},{10... | collective-permute-start | bytes 196616 | tf_op jit(solution)/shard_map/ppermute | solution.py:213
  40.5 5.3 %collective-permute-start.16 = (bf16[256,128]{1,0:T(8,128)(2,1)S(1)}, bf16[256,128]{1,0:T(8,128)(2,1)S(1)}, u32[]{:S(2)}, u32[]{:S(2)}) collective-permute-start(bf16[256,128]{1,0:T(8,128)(2,1)S(1)} %get-tuple-element.47), channel_id=1, source_target_pairs={{0,24},{8,16},{16,8},{24,0},{1,25},{9,17},{17,9},{25,1},{2,26},{10... | collective-permute-start | bytes 196616 | tf_op jit(solution)/shard_map/ppermute | solution.py:213
  43.7 5.0 %collective-permute-start.24 = (bf16[128,256]{1,0:T(8,128)(2,1)S(1)}, bf16[128,256]{1,0:T(8,128)(2,1)S(1)}, u32[]{:S(2)}, u32[]{:S(2)}) collective-permute-start(bf16[128,256]{1,0:T(8,128)(2,1)S(1)} %slice.4), channel_id=1, source_target_pairs={{0,8},{8,0},{16,24},{24,16},{1,9},{9,1},{17,25},{25,17},{2,10},{10... | collective-permute-start | bytes 196616 | tf_op jit(solution)/shard_map/ppermute | solution.py:213
  (9 other events, 69.8 us)

commit v4 on v3

--- a/solution.py
+++ b/solution.py
@@ -264,35 +264,49 @@
             out_ref.dtype
         )
 
-    work = (2 * half * n * grid_rows * n * width, 1 << 20)
-    sent = call(
-        functools.partial(products, 1),
-        sds((half * n, width), BF16),
-        [cell, *feats],
-        "forward_sent",
-        cost=work,
-    )
-    sent_in = swap(sent, "col", 1)
+    work = (half * n * grid_rows * n * width, 1 << 19)
+    rows = half * n // 2
+
+    def strip(first):
+        def body(cell_ref, *refs):
+            *x_refs, out_ref = refs
+            stripe = jnp.concatenate([r[...] for r in x_refs], axis=0)
+            out_ref[...] = dot(cell_ref[first : first + out_ref.shape[0], :], stripe).astype(
+                out_ref.dtype
+            )
+
+        return body
+
+    sent_in = []
+    for part in (3, 2):
+        sent = call(
+            strip(part * rows), sds((rows, width), BF16), [cell, *feats], "forward_sent", cost=work
+        )
+        sent_in.append(swap(sent, "col", 1))
     kept = call(
-        functools.partial(products, 0),
-        sds((half * n, width), F32),
-        [cell, *feats],
-        "forward_kept",
-        cost=work,
-    )
-
-    def pair_sums(kept_ref, in_ref, own_ref, *out_refs):
-        total = kept_ref[...] + in_ref[...].astype(F32)
+        strip(0), sds((half * n, width), F32), [cell, *feats], "forward_kept", cost=work
+    )
+
+    def pair_far(kept_ref, in_ref, *out_refs):
+        total = kept_ref[rows:, :] + in_ref[...].astype(F32)
+        for q, ref in enumerate(out_refs):
+            ref[...] = total[q * n : (q + 1) * n].astype(BF16)
+
+    def pair_near(kept_ref, in_ref, own_ref, *out_refs):
+        total = kept_ref[:rows, :] + in_ref[...].astype(F32)
         own_ref[...] = total[:n]
         for q, ref in enumerate(out_refs):
             ref[...] = total[(q + 1) * n : (q + 2) * n].astype(BF16)
 
-    own_sum, *parts = call(
-        pair_sums,
-        [sds((n, width), F32)] + [sds((n, width), BF16)] * (half - 1),
-        [kept, sent_in],
-        "pair_sums",
-    )
+    block = sds((n, width), BF16)
+    far_parts = call(pair_far, [block] * (half // 2), [kept, sent_in[0]], "pair_far")
+    own_sum, *near_parts = call(
+        pair_near,
+        [sds((n, width), F32)] + [block] * (half // 2 - 1),
+        [kept, sent_in[1]],
+        "pair_near",
+    )
+    parts = [*near_parts, *far_parts]
     parts_in = [swap(part, "col", 2 * (q + 1)) for q, part in enumerate(parts)]
 
     pad = 16

time: 49.6 us -> 49.1 us (0.990)
  waiting for transfers between devices: 12.7 us -> 11.4 us
  starting transfers between devices: 27.8 us -> 28.4 us
    ppermute x25 -> x26, waiting for transfers between devices: 12.7 us -> 11.4 us  [swap(): return lax.ppermute(value, axis, [(i, i ^ distance) for i in range(size)])]
    ppermute x25 -> x26, starting transfers between devices: 25.8 us -> 26.3 us  [swap(): return lax.ppermute(value, axis, [(i, i ^ distance) for i in range(size)])]
    pallas_call x12 -> x14, Pallas kernels: 3.44 us -> 3.6 us  [call(): pl.pallas_call(body, out_shape=outs, in_specs=in_specs, out_specs=[pl.Blo...]
  transfers between devices with their start and end apart: 27 -> 28, of which waited for: 10 -> 10; matrix products, arithmetic and copies ran while one was open for 0% -> 0% of each run, Pallas kernels for 12% -> 13%
where the time goes in v4:
time: 49.1 us; the launch traced here: 48.9 us
  starting transfers between devices  28.4 us (58%)
  waiting for transfers between devices  11.4 us (23%)
  Pallas kernels  7.57 us (15%)
  between operations  1.51 us (3%)
    ppermute x26, starting transfers between devices, swap(): return lax.ppermute(value, axis, [(i, i ^ distance) for i in range(size)])  26.3 us
    ppermute x26, waiting for transfers between devices, swap(): return lax.ppermute(value, axis, [(i, i ^ distance) for i in range(size)])  11.4 us
    pallas_call x14, Pallas kernels, call(): pl.pallas_call(body, out_shape=outs, in_specs=in_specs, out_specs=[pl.Blo...  3.6 us
    ppermute x2, starting transfers between devices, swap_corner(): lax.ppermute(value, ('row', 'col'), [(i, i ^ step) for i in range(size)])  2.06 us
    pallas_call x1, Pallas kernels, build_cell(): pl.pallas_call(body, out_shape=sds((grid_cols * edge, grid_rows * edge),...  1.87 us
    pallas_call x2, Pallas kernels, direct_form(): pl.pallas_call(functools.partial(write_next, core), out_shape=whole, in_s...  1.38 us
  transfers between devices with their start and end apart: 28, of which 10 were waited for; matrix products, arithmetic and copies ran while one was open for 0% of the time, Pallas kernels for 13%

profile of v4, /device:TPU:0, one launch (start us, length us, event | category | flops | bytes accessed | tf_op | source)
XLA Modules:
  0.0 48.9 jit_solution(11977689122658322148)
XLA Ops:
  0.6 4.0 %collective-permute-start.2 = (bf16[128,256]{1,0:T(8,128)(2,1)}, bf16[128,256]{1,0:T(8,128)(2,1)S(1)}, u32[]{:S(2)}, u32[]{:S(2)}) collective-permute-start(bf16[128,256]{1,0:T(8,128)(2,1)} %refs_4_.1), channel_id=1, source_target_pairs={{0,24},{8,16},{16,8},{24,0},{1,25},{9,17},{17,9},{25,1},{2,26},{10... | collective-permute-start | bytes 196616 | tf_op jit(solution)/shard_map/ppermute | solution.py:213
  5.9 1.9 %build_cell.1.refs_0_ = bf16[1024,512]{1,0:T(8,128)(2,1)S(1)} custom-call(s32[1,1]{1,0:T(1,128)S(6)} %copy.23.refs_0_, s32[80]{0:T(128)} %bitcast.9, s32[80]{0:T(128)} %bitcast.10, bf16[80,128,128]{2,1,0:T(8,128)(2,1)} %bitcast.8), custom_call_target="tpu_custom_call" | custom-call | flops 16777216 | bytes 5242880 | tf_op jit(solution)/shard_map/build_cell/pallas_call | solution.py:191
  7.8 1.3 %collective-permute-done.1.refs_3_ = bf16[128,256]{1,0:T(8,128)(2,1)S(1)} collective-permute-done((bf16[128,256]{1,0:T(8,128)(2,1)}, bf16[128,256]{1,0:T(8,128)(2,1)S(1)}, u32[]{:S(2)}, u32[]{:S(2)}) %collective-permute-start.1) | collective-permute-done | bytes 65568 | tf_op jit(solution)/shard_map/ppermute | solution.py:213
  11.3 3.7 %collective-permute-start.5 = (bf16[128,256]{1,0:T(8,128)(2,1)S(1)}, bf16[128,256]{1,0:T(8,128)(2,1)S(1)}, u32[]{:S(2)}, u32[]{:S(2)}) collective-permute-start(bf16[128,256]{1,0:T(8,128)(2,1)S(1)} %get-tuple-element.33), channel_id=1, source_target_pairs={{0,6},{1,7},{2,4},{3,5},{4,2},{5,3},{6,0},{7,1},{8,14},{9,15},{10,... | collective-permute-start | bytes 196616 | tf_op jit(solution)/shard_map/ppermute | solution.py:213
  15.1 0.8 %collective-permute-start.7 = (bf16[128,256]{1,0:T(8,128)(2,1)S(1)}, bf16[128,256]{1,0:T(8,128)(2,1)S(1)}, u32[]{:S(2)}, u32[]{:S(2)}) collective-permute-start(bf16[128,256]{1,0:T(8,128)(2,1)S(1)} %get-tuple-element.35), channel_id=1, source_target_pairs={{0,2},{1,3},{2,0},{3,1},{4,6},{5,7},{6,4},{7,5},{8,10},{9,11},{10,... | collective-permute-start | bytes 196616 | tf_op jit(solution)/shard_map/ppermute | solution.py:213
  16.1 1.6 %collective-permute-done.5.refs_1_ = bf16[128,256]{1,0:T(8,128)(2,1)S(1)} collective-permute-done((bf16[128,256]{1,0:T(8,128)(2,1)S(1)}, bf16[128,256]{1,0:T(8,128)(2,1)S(1)}, u32[]{:S(2)}, u32[]{:S(2)}) %collective-permute-start.5) | collective-permute-done | bytes 65568 | tf_op jit(solution)/shard_map/ppermute | solution.py:213
  17.6 3.3 %collective-permute-done.6.refs_2_ = bf16[128,256]{1,0:T(8,128)(2,1)S(1)} collective-permute-done((bf16[128,256]{1,0:T(8,128)(2,1)S(1)}, bf16[128,256]{1,0:T(8,128)(2,1)S(1)}, u32[]{:S(2)}, u32[]{:S(2)}) %collective-permute-start.6) | collective-permute-done | bytes 65568 | tf_op jit(solution)/shard_map/ppermute | solution.py:213
  22.1 1.2 %collective-permute-start.20 = (bf16[144,256]{1,0:T(8,128)(2,1)S(1)}, bf16[144,256]{1,0:T(8,128)(2,1)S(1)}, u32[]{:S(2)}, u32[]{:S(2)}) collective-permute-start(bf16[144,256]{1,0:T(8,128)(2,1)S(1)} %get-tuple-element.51), channel_id=1, source_target_pairs={{0,9},{1,8},{2,11},{3,10},{4,13},{5,12},{6,15},{7,14},{8,1},{9,0},... | collective-permute-start | bytes 221192 | tf_op jit(solution)/shard_map/ppermute | solution.py:219
  23.3 2.5 %collective-permute-start.10 = (bf16[256,128]{1,0:T(8,128)(2,1)S(1)}, bf16[256,128]{1,0:T(8,128)(2,1)S(1)}, u32[]{:S(2)}, u32[]{:S(2)}) collective-permute-start(bf16[256,128]{1,0:T(8,128)(2,1)S(1)} %get-tuple-element.41.refs_1_), channel_id=1, source_target_pairs={{0,6},{1,7},{2,4},{3,5},{4,2},{5,3},{6,0},{7,1},{8,14},{9,15},{10,... | collective-permute-start | bytes 196616 | tf_op jit(solution)/shard_map/ppermute | solution.py:213
  25.9 1.8 %collective-permute-start.8 = (bf16[256,128]{1,0:T(8,128)(2,1)S(1)}, bf16[256,128]{1,0:T(8,128)(2,1)S(1)}, u32[]{:S(2)}, u32[]{:S(2)}) collective-permute-start(bf16[256,128]{1,0:T(8,128)(2,1)S(1)} %get-tuple-element.41.refs_1_), channel_id=1, source_target_pairs={{0,2},{1,3},{2,0},{3,1},{4,6},{5,7},{6,4},{7,5},{8,10},{9,11},{10,... | collective-permute-start | bytes 196616 | tf_op jit(solution)/shard_map/ppermute | solution.py:213
  27.8 1.6 %collective-permute-start.21 = (bf16[144,256]{1,0:T(8,128)(2,1)S(1)}, bf16[144,256]{1,0:T(8,128)(2,1)S(1)}, u32[]{:S(2)}, u32[]{:S(2)}) collective-permute-start(bf16[144,256]{1,0:T(8,128)(2,1)S(1)} %add_corner.1.refs_0_), channel_id=1, source_target_pairs={{0,16},{8,24},{16,0},{24,8},{1,17},{9,25},{17,1},{25,9},{2,18},{10... | collective-permute-start | bytes 221192 | tf_op jit(solution)/shard_map/ppermute | solution.py:213
  29.4 0.8 %collective-permute-done.10.refs_4_ = bf16[256,128]{1,0:T(8,128)(2,1)S(1)} collective-permute-done((bf16[256,128]{1,0:T(8,128)(2,1)S(1)}, bf16[256,128]{1,0:T(8,128)(2,1)S(1)}, u32[]{:S(2)}, u32[]{:S(2)}) %collective-permute-start.10) | collective-permute-done | bytes 65568 | tf_op jit(solution)/shard_map/ppermute | solution.py:213
  30.2 2.2 %collective-permute-done.9.refs_3_ = bf16[256,128]{1,0:T(8,128)(2,1)S(1)} collective-permute-done((bf16[256,128]{1,0:T(8,128)(2,1)S(1)}, bf16[256,128]{1,0:T(8,128)(2,1)S(1)}, u32[]{:S(2)}, u32[]{:S(2)}) %collective-permute-start.9) | collective-permute-done | bytes 65568 | tf_op jit(solution)/shard_map/ppermute | solution.py:213
  33.0 2.4 %collective-permute-start.24 = (bf16[144,256]{1,0:T(8,128)(2,1)S(1)}, bf16[144,256]{1,0:T(8,128)(2,1)S(1)}, u32[]{:S(2)}, u32[]{:S(2)}) collective-permute-start(bf16[144,256]{1,0:T(8,128)(2,1)S(1)} %add_y.1.refs_0_), channel_id=1, source_target_pairs={{0,6},{1,7},{2,4},{3,5},{4,2},{5,3},{6,0},{7,1},{8,14},{9,15},{10,... | collective-permute-start | bytes 221192 | tf_op jit(solution)/shard_map/ppermute | solution.py:213
  35.4 2.1 %collective-permute-start.22 = (bf16[144,256]{1,0:T(8,128)(2,1)S(1)}, bf16[144,256]{1,0:T(8,128)(2,1)S(1)}, u32[]{:S(2)}, u32[]{:S(2)}) collective-permute-start(bf16[144,256]{1,0:T(8,128)(2,1)S(1)} %add_y.1.refs_0_), channel_id=1, source_target_pairs={{0,2},{1,3},{2,0},{3,1},{4,6},{5,7},{6,4},{7,5},{8,10},{9,11},{10,... | collective-permute-start | bytes 221192 | tf_op jit(solution)/shard_map/ppermute | solution.py:213
  38.7 1.5 %collective-permute-start.16 = (bf16[256,128]{1,0:T(8,128)(2,1)S(1)}, bf16[256,128]{1,0:T(8,128)(2,1)S(1)}, u32[]{:S(2)}, u32[]{:S(2)}) collective-permute-start(bf16[256,128]{1,0:T(8,128)(2,1)S(1)} %get-tuple-element.46), channel_id=1, source_target_pairs={{0,16},{8,24},{16,0},{24,8},{1,17},{9,25},{17,1},{25,9},{2,18},{10... | collective-permute-start | bytes 196616 | tf_op jit(solution)/shard_map/ppermute | solution.py:213
  40.2 1.4 %collective-permute-start.17 = (bf16[256,128]{1,0:T(8,128)(2,1)S(1)}, bf16[256,128]{1,0:T(8,128)(2,1)S(1)}, u32[]{:S(2)}, u32[]{:S(2)}) collective-permute-start(bf16[256,128]{1,0:T(8,128)(2,1)S(1)} %get-tuple-element.47), channel_id=1, source_target_pairs={{0,24},{8,16},{16,8},{24,0},{1,25},{9,17},{17,9},{25,1},{2,26},{10... | collective-permute-start | bytes 196616 | tf_op jit(solution)/shard_map/ppermute | solution.py:213
  42.4 0.8 %collective-permute-start.26 = (bf16[128,256]{1,0:T(8,128)(2,1)S(1)}, bf16[128,256]{1,0:T(8,128)(2,1)S(1)}, u32[]{:S(2)}, u32[]{:S(2)}) collective-permute-start(bf16[128,256]{1,0:T(8,128)(2,1)S(1)} %slice.4), channel_id=1, source_target_pairs={{0,9},{1,8},{2,11},{3,10},{4,13},{5,12},{6,15},{7,14},{8,1},{9,0},... | collective-permute-start | bytes 196616 | tf_op jit(solution)/shard_map/ppermute | solution.py:219
  43.2 1.3 %collective-permute-start.25 = (bf16[128,256]{1,0:T(8,128)(2,1)S(1)}, bf16[128,256]{1,0:T(8,128)(2,1)S(1)}, u32[]{:S(2)}, u32[]{:S(2)}) collective-permute-start(bf16[128,256]{1,0:T(8,128)(2,1)S(1)} %slice.4), channel_id=1, source_target_pairs={{0,8},{8,0},{16,24},{24,16},{1,9},{9,1},{17,25},{25,17},{2,10},{10... | collective-permute-start | bytes 196616 | tf_op jit(solution)/shard_map/ppermute | solution.py:213
  44.5 0.7 %activate.1 = (bf16[128,256]{1,0:T(8,128)(2,1)}, f32[256,128]{1,0:T(8,128)S(1)}) custom-call(f32[128,256]{1,0:T(8,128)S(1)} %get-tuple-element.39.refs_0_, bf16[256,256]{1,0:T(8,128)(2,1)S(1)} %copy-done.1, bf16[128,256]{1,0:T(8,128)(2,1)S(1)} %get-tuple-element.40.refs_2_, f32[256,128]{1,0:T(8,128)S(1)} %get-tuple-element.42.refs_3_.refs_1_.refs_4_), custom_call_target="tpu_custom_call" | custom-call | flops 1048576 | bytes 262144 | tf_op jit(solution)/shard_map/activate/pallas_call | solution.py:130
  45.4 0.7 %finish.1 = bf16[128,256]{1,0:T(8,128)(2,1)} custom-call(f32[256,128]{1,0:T(8,128)S(1)} %get-tuple-element.44.refs_0_, f32[256,128]{1,0:T(8,128)S(1)} %get-tuple-element.42.refs_3_.refs_1_.refs_4_, bf16[256,128]{1,0:T(8,128)(2,1)S(1)} %collective-permute-done.15.refs_2_, bf16[256,128]{1,0:T(8,128)(2,1)S(1)} %collective-permute-done.16.refs_3_, ...), custom_call_target="tpu_custom_call" | custom-call | flops 1048576 | bytes 262144 | tf_op jit(solution)/shard_map/finish/pallas_call | solution.py:130
  46.1 0.7 %write_first.1 = (f32[256,256]{1,0:T(8,128)}, f32[256,256]{1,0:T(8,128)}, f32[1,256]{1,0:T(1,128)}) custom-call(bf16[144,256]{1,0:T(8,128)(2,1)S(1)} %add_z.1.a_ref, bf16[128,256]{1,0:T(8,128)(2,1)S(1)} %collective-permute-done.27.b_ref), custom_call_target="tpu_custom_call" | custom-call | flops 1048576 | bytes 262144 | tf_op jit(solution)/shard_map/write_first/pallas_call | solution.py:478
  46.9 0.7 %write_next.2 = (f32[256,256]{1,0:T(8,128)}, f32[256,256]{1,0:T(8,128)}) custom-call(bf16[128,256]{1,0:T(8,128)(2,1)S(1)} %collective-permute-done.26.a_ref, f32[256,256]{1,0:T(8,128)} %get-tuple-element.52.s_ref, f32[256,256]{1,0:T(8,128)} %get-tuple-element.53.n_ref), custom_call_target="tpu_custom_call", output_to_operand_aliasing={{0}: (1, {}), {1}: (2, {})} | custom-call | flops 1048576 | bytes 262144 | tf_op jit(solution)/shard_map/write_next/pallas_call | solution.py:488
  47.6 0.7 %collective-permute-done.25.a_ref = bf16[128,256]{1,0:T(8,128)(2,1)S(1)} collective-permute-done((bf16[128,256]{1,0:T(8,128)(2,1)S(1)}, bf16[128,256]{1,0:T(8,128)(2,1)S(1)}, u32[]{:S(2)}, u32[]{:S(2)}) %collective-permute-start.25) | collective-permute-done | bytes 65568 | tf_op jit(solution)/shard_map/ppermute | solution.py:213
  (63 shorter events, 7.6 us)
Async XLA Ops:
  0.6 7.2 %collective-permute-start.2 = (bf16[128,256]{1,0:T(8,128)(2,1)}, bf16[128,256]{1,0:T(8,128)(2,1)S(1)}, u32[]{:S(2)}, u32[]{:S(2)}) collective-permute-start(bf16[128,256]{1,0:T(8,128)(2,1)} %refs_4_.1), channel_id=1, source_target_pairs={{0,24},{8,16},{16,8},{24,0},{1,25},{9,17},{17,9},{25,1},{2,26},{10... | collective-permute-start | bytes 196616 | tf_op jit(solution)/shard_map/ppermute | solution.py:213
  4.6 4.5 %collective-permute-start.1 = (bf16[128,256]{1,0:T(8,128)(2,1)}, bf16[128,256]{1,0:T(8,128)(2,1)S(1)}, u32[]{:S(2)}, u32[]{:S(2)}) collective-permute-start(bf16[128,256]{1,0:T(8,128)(2,1)} %refs_4_.1), channel_id=1, source_target_pairs={{0,16},{8,24},{16,0},{24,8},{1,17},{9,25},{17,1},{25,9},{2,18},{10... | collective-permute-start | bytes 196616 | tf_op jit(solution)/shard_map/ppermute | solution.py:213
  10.2 4.8 %collective-permute-start.3 = (bf16[256,256]{1,0:T(8,128)(2,1)S(1)}, bf16[256,256]{1,0:T(8,128)(2,1)S(1)}, u32[]{:S(2)}, u32[]{:S(2)}) collective-permute-start(bf16[256,256]{1,0:T(8,128)(2,1)S(1)} %forward_sent.2), channel_id=1, source_target_pairs={{0,1},{1,0},{2,3},{3,2},{4,5},{5,4},{6,7},{7,6},{8,9},{9,8},{10,11... | collective-permute-start | bytes 393224 | tf_op jit(solution)/shard_map/ppermute | solution.py:213
  11.3 6.3 %collective-permute-start.5 = (bf16[128,256]{1,0:T(8,128)(2,1)S(1)}, bf16[128,256]{1,0:T(8,128)(2,1)S(1)}, u32[]{:S(2)}, u32[]{:S(2)}) collective-permute-start(bf16[128,256]{1,0:T(8,128)(2,1)S(1)} %get-tuple-element.33), channel_id=1, source_target_pairs={{0,6},{1,7},{2,4},{3,5},{4,2},{5,3},{6,0},{7,1},{8,14},{9,15},{10,... | collective-permute-start | bytes 196616 | tf_op jit(solution)/shard_map/ppermute | solution.py:213
  15.0 5.9 %collective-permute-start.6 = (bf16[128,256]{1,0:T(8,128)(2,1)S(1)}, bf16[128,256]{1,0:T(8,128)(2,1)S(1)}, u32[]{:S(2)}, u32[]{:S(2)}) collective-permute-start(bf16[128,256]{1,0:T(8,128)(2,1)S(1)} %get-tuple-element.34), channel_id=1, source_target_pairs={{0,4},{1,5},{2,6},{3,7},{4,0},{5,1},{6,2},{7,3},{8,12},{9,13},{10,... | collective-permute-start | bytes 196616 | tf_op jit(solution)/shard_map/ppermute | solution.py:213
  15.1 5.9 %collective-permute-start.7 = (bf16[128,256]{1,0:T(8,128)(2,1)S(1)}, bf16[128,256]{1,0:T(8,128)(2,1)S(1)}, u32[]{:S(2)}, u32[]{:S(2)}) collective-permute-start(bf16[128,256]{1,0:T(8,128)(2,1)S(1)} %get-tuple-element.35), channel_id=1, source_target_pairs={{0,2},{1,3},{2,0},{3,1},{4,6},{5,7},{6,4},{7,5},{8,10},{9,11},{10,... | collective-permute-start | bytes 196616 | tf_op jit(solution)/shard_map/ppermute | solution.py:213
  21.4 4.5 %collective-permute-start.18 = (bf16[144,256]{1,0:T(8,128)(2,1)S(1)}, bf16[144,256]{1,0:T(8,128)(2,1)S(1)}, u32[]{:S(2)}, u32[]{:S(2)}) collective-permute-start(bf16[144,256]{1,0:T(8,128)(2,1)S(1)} %get-tuple-element.49), channel_id=1, source_target_pairs={{0,1},{1,0},{2,3},{3,2},{4,5},{5,4},{6,7},{7,6},{8,9},{9,8},{10,11... | collective-permute-start | bytes 221192 | tf_op jit(solution)/shard_map/ppermute | solution.py:213
  21.5 6.2 %collective-permute-start.19 = (bf16[144,256]{1,0:T(8,128)(2,1)S(1)}, bf16[144,256]{1,0:T(8,128)(2,1)S(1)}, u32[]{:S(2)}, u32[]{:S(2)}) collective-permute-start(bf16[144,256]{1,0:T(8,128)(2,1)S(1)} %get-tuple-element.50), channel_id=1, source_target_pairs={{0,8},{8,0},{16,24},{24,16},{1,9},{9,1},{17,25},{25,17},{2,10},{10... | collective-permute-start | bytes 221192 | tf_op jit(solution)/shard_map/ppermute | solution.py:213
  22.1 5.6 %collective-permute-start.20 = (bf16[144,256]{1,0:T(8,128)(2,1)S(1)}, bf16[144,256]{1,0:T(8,128)(2,1)S(1)}, u32[]{:S(2)}, u32[]{:S(2)}) collective-permute-start(bf16[144,256]{1,0:T(8,128)(2,1)S(1)} %get-tuple-element.51), channel_id=1, source_target_pairs={{0,9},{1,8},{2,11},{3,10},{4,13},{5,12},{6,15},{7,14},{8,1},{9,0},... | collective-permute-start | bytes 221192 | tf_op jit(solution)/shard_map/ppermute | solution.py:219
  23.3 6.9 %collective-permute-start.10 = (bf16[256,128]{1,0:T(8,128)(2,1)S(1)}, bf16[256,128]{1,0:T(8,128)(2,1)S(1)}, u32[]{:S(2)}, u32[]{:S(2)}) collective-permute-start(bf16[256,128]{1,0:T(8,128)(2,1)S(1)} %get-tuple-element.41.refs_1_), channel_id=1, source_target_pairs={{0,6},{1,7},{2,4},{3,5},{4,2},{5,3},{6,0},{7,1},{8,14},{9,15},{10,... | collective-permute-start | bytes 196616 | tf_op jit(solution)/shard_map/ppermute | solution.py:213
  25.8 6.6 %collective-permute-start.9 = (bf16[256,128]{1,0:T(8,128)(2,1)S(1)}, bf16[256,128]{1,0:T(8,128)(2,1)S(1)}, u32[]{:S(2)}, u32[]{:S(2)}) collective-permute-start(bf16[256,128]{1,0:T(8,128)(2,1)S(1)} %get-tuple-element.41.refs_1_), channel_id=1, source_target_pairs={{0,4},{1,5},{2,6},{3,7},{4,0},{5,1},{6,2},{7,3},{8,12},{9,13},{10,... | collective-permute-start | bytes 196616 | tf_op jit(solution)/shard_map/ppermute | solution.py:213
  25.9 6.6 %collective-permute-start.8 = (bf16[256,128]{1,0:T(8,128)(2,1)S(1)}, bf16[256,128]{1,0:T(8,128)(2,1)S(1)}, u32[]{:S(2)}, u32[]{:S(2)}) collective-permute-start(bf16[256,128]{1,0:T(8,128)(2,1)S(1)} %get-tuple-element.41.refs_1_), channel_id=1, source_target_pairs={{0,2},{1,3},{2,0},{3,1},{4,6},{5,7},{6,4},{7,5},{8,10},{9,11},{10,... | collective-permute-start | bytes 196616 | tf_op jit(solution)/shard_map/ppermute | solution.py:213
  27.8 5.2 %collective-permute-start.21 = (bf16[144,256]{1,0:T(8,128)(2,1)S(1)}, bf16[144,256]{1,0:T(8,128)(2,1)S(1)}, u32[]{:S(2)}, u32[]{:S(2)}) collective-permute-start(bf16[144,256]{1,0:T(8,128)(2,1)S(1)} %add_corner.1.refs_0_), channel_id=1, source_target_pairs={{0,16},{8,24},{16,0},{24,8},{1,17},{9,25},{17,1},{25,9},{2,18},{10... | collective-permute-start | bytes 221192 | tf_op jit(solution)/shard_map/ppermute | solution.py:213
  29.4 6.0 %collective-permute-start.11 = (bf16[256,128]{1,0:T(8,128)(2,1)S(1)}, bf16[256,128]{1,0:T(8,128)(2,1)S(1)}, u32[]{:S(2)}, u32[]{:S(2)}) collective-permute-start(bf16[256,128]{1,0:T(8,128)(2,1)S(1)} %get-tuple-element.41.refs_1_), channel_id=1, source_target_pairs={{0,1},{1,0},{2,3},{3,2},{4,5},{5,4},{6,7},{7,6},{8,9},{9,8},{10,11... | collective-permute-start | bytes 196616 | tf_op jit(solution)/shard_map/ppermute | solution.py:213
  30.2 5.2 %collective-permute-start.14 = (bf16[256,128]{1,0:T(8,128)(2,1)S(1)}, bf16[256,128]{1,0:T(8,128)(2,1)S(1)}, u32[]{:S(2)}, u32[]{:S(2)}) collective-permute-start(bf16[256,128]{1,0:T(8,128)(2,1)S(1)} %collective-permute-done.10.refs_4_), channel_id=1, source_target_pairs={{0,1},{1,0},{2,3},{3,2},{4,5},{5,4},{6,7},{7,6},{8,9},{9,8},{10,11... | collective-permute-start | bytes 196616 | tf_op jit(solution)/shard_map/ppermute | solution.py:213
  32.4 5.3 %collective-permute-start.13 = (bf16[256,128]{1,0:T(8,128)(2,1)S(1)}, bf16[256,128]{1,0:T(8,128)(2,1)S(1)}, u32[]{:S(2)}, u32[]{:S(2)}) collective-permute-start(bf16[256,128]{1,0:T(8,128)(2,1)S(1)} %collective-permute-done.9.refs_3_), channel_id=1, source_target_pairs={{0,1},{1,0},{2,3},{3,2},{4,5},{5,4},{6,7},{7,6},{8,9},{9,8},{10,11... | collective-permute-start | bytes 196616 | tf_op jit(solution)/shard_map/ppermute | solution.py:213
  32.5 5.2 %collective-permute-start.12 = (bf16[256,128]{1,0:T(8,128)(2,1)S(1)}, bf16[256,128]{1,0:T(8,128)(2,1)S(1)}, u32[]{:S(2)}, u32[]{:S(2)}) collective-permute-start(bf16[256,128]{1,0:T(8,128)(2,1)S(1)} %collective-permute-done.8.refs_2_), channel_id=1, source_target_pairs={{0,1},{1,0},{2,3},{3,2},{4,5},{5,4},{6,7},{7,6},{8,9},{9,8},{10,11... | collective-permute-start | bytes 196616 | tf_op jit(solution)/shard_map/ppermute | solution.py:213
  33.0 7.2 %collective-permute-start.24 = (bf16[144,256]{1,0:T(8,128)(2,1)S(1)}, bf16[144,256]{1,0:T(8,128)(2,1)S(1)}, u32[]{:S(2)}, u32[]{:S(2)}) collective-permute-start(bf16[144,256]{1,0:T(8,128)(2,1)S(1)} %add_y.1.refs_0_), channel_id=1, source_target_pairs={{0,6},{1,7},{2,4},{3,5},{4,2},{5,3},{6,0},{7,1},{8,14},{9,15},{10,... | collective-permute-start | bytes 221192 | tf_op jit(solution)/shard_map/ppermute | solution.py:213
  35.4 6.9 %collective-permute-start.23 = (bf16[144,256]{1,0:T(8,128)(2,1)S(1)}, bf16[144,256]{1,0:T(8,128)(2,1)S(1)}, u32[]{:S(2)}, u32[]{:S(2)}) collective-permute-start(bf16[144,256]{1,0:T(8,128)(2,1)S(1)} %add_y.1.refs_0_), channel_id=1, source_target_pairs={{0,4},{1,5},{2,6},{3,7},{4,0},{5,1},{6,2},{7,3},{8,12},{9,13},{10,... | collective-permute-start | bytes 221192 | tf_op jit(solution)/shard_map/ppermute | solution.py:213
  35.4 6.9 %collective-permute-start.22 = (bf16[144,256]{1,0:T(8,128)(2,1)S(1)}, bf16[144,256]{1,0:T(8,128)(2,1)S(1)}, u32[]{:S(2)}, u32[]{:S(2)}) collective-permute-start(bf16[144,256]{1,0:T(8,128)(2,1)S(1)} %add_y.1.refs_0_), channel_id=1, source_target_pairs={{0,2},{1,3},{2,0},{3,1},{4,6},{5,7},{6,4},{7,5},{8,10},{9,11},{10,... | collective-permute-start | bytes 221192 | tf_op jit(solution)/shard_map/ppermute | solution.py:213
  38.1 5.1 %collective-permute-start.15 = (bf16[256,128]{1,0:T(8,128)(2,1)S(1)}, bf16[256,128]{1,0:T(8,128)(2,1)S(1)}, u32[]{:S(2)}, u32[]{:S(2)}) collective-permute-start(bf16[256,128]{1,0:T(8,128)(2,1)S(1)} %get-tuple-element.45), channel_id=1, source_target_pairs={{0,8},{8,0},{16,24},{24,16},{1,9},{9,1},{17,25},{25,17},{2,10},{10... | collective-permute-start | bytes 196616 | tf_op jit(solution)/shard_map/ppermute | solution.py:213
  38.7 6.6 %collective-permute-start.16 = (bf16[256,128]{1,0:T(8,128)(2,1)S(1)}, bf16[256,128]{1,0:T(8,128)(2,1)S(1)}, u32[]{:S(2)}, u32[]{:S(2)}) collective-permute-start(bf16[256,128]{1,0:T(8,128)(2,1)S(1)} %get-tuple-element.46), channel_id=1, source_target_pairs={{0,16},{8,24},{16,0},{24,8},{1,17},{9,25},{17,1},{25,9},{2,18},{10... | collective-permute-start | bytes 196616 | tf_op jit(solution)/shard_map/ppermute | solution.py:213
  40.2 5.2 %collective-permute-start.17 = (bf16[256,128]{1,0:T(8,128)(2,1)S(1)}, bf16[256,128]{1,0:T(8,128)(2,1)S(1)}, u32[]{:S(2)}, u32[]{:S(2)}) collective-permute-start(bf16[256,128]{1,0:T(8,128)(2,1)S(1)} %get-tuple-element.47), channel_id=1, source_target_pairs={{0,24},{8,16},{16,8},{24,0},{1,25},{9,17},{17,9},{25,1},{2,26},{10... | collective-permute-start | bytes 196616 | tf_op jit(solution)/shard_map/ppermute | solution.py:213
  43.2 5.0 %collective-permute-start.25 = (bf16[128,256]{1,0:T(8,128)(2,1)S(1)}, bf16[128,256]{1,0:T(8,128)(2,1)S(1)}, u32[]{:S(2)}, u32[]{:S(2)}) collective-permute-start(bf16[128,256]{1,0:T(8,128)(2,1)S(1)} %slice.4), channel_id=1, source_target_pairs={{0,8},{8,0},{16,24},{24,16},{1,9},{9,1},{17,25},{25,17},{2,10},{10... | collective-permute-start | bytes 196616 | tf_op jit(solution)/shard_map/ppermute | solution.py:213
  (10 other events, 63.3 us)

commit v5 on v4

--- a/solution.py
+++ b/solution.py
@@ -309,7 +309,7 @@
     parts = [*near_parts, *far_parts]
     parts_in = [swap(part, "col", 2 * (q + 1)) for q, part in enumerate(parts)]
 
-    pad = 16
+    pad = 8
     piece = width // 2
     small = sds((piece + pad, width), BF16)
     inward = half - 1

time: 49.1 us -> 49.1 us (level)
  no operation moved by 1% of the time
where the time goes in v5:
time: 49.1 us; the launch traced here: 49 us
  starting transfers between devices  28.4 us (58%)
  waiting for transfers between devices  11.4 us (23%)
  Pallas kernels  7.57 us (15%)
  between operations  1.5 us (3%)
    ppermute x26, starting transfers between devices, swap(): return lax.ppermute(value, axis, [(i, i ^ distance) for i in range(size)])  26.2 us
    ppermute x26, waiting for transfers between devices, swap(): return lax.ppermute(value, axis, [(i, i ^ distance) for i in range(size)])  11.4 us
    pallas_call x14, Pallas kernels, call(): pl.pallas_call(body, out_shape=outs, in_specs=in_specs, out_specs=[pl.Blo...  3.59 us
    ppermute x2, starting transfers between devices, swap_corner(): lax.ppermute(value, ('row', 'col'), [(i, i ^ step) for i in range(size)])  2.17 us
    pallas_call x1, Pallas kernels, build_cell(): pl.pallas_call(body, out_shape=sds((grid_cols * edge, grid_rows * edge),...  1.87 us
    pallas_call x2, Pallas kernels, direct_form(): pl.pallas_call(functools.partial(write_next, core), out_shape=whole, in_s...  1.38 us
  transfers between devices with their start and end apart: 28, of which 10 were waited for; matrix products, arithmetic and copies ran while one was open for 0% of the time, Pallas kernels for 13%

profile of v5, /device:TPU:0, one launch (start us, length us, event | category | flops | bytes accessed | tf_op | source)
XLA Modules:
  0.0 49.0 jit_solution(12401619680807105811)
XLA Ops:
  0.6 4.0 %collective-permute-start.2 = (bf16[128,256]{1,0:T(8,128)(2,1)}, bf16[128,256]{1,0:T(8,128)(2,1)S(1)}, u32[]{:S(2)}, u32[]{:S(2)}) collective-permute-start(bf16[128,256]{1,0:T(8,128)(2,1)} %refs_4_.1), channel_id=1, source_target_pairs={{0,24},{8,16},{16,8},{24,0},{1,25},{9,17},{17,9},{25,1},{2,26},{10... | collective-permute-start | bytes 196616 | tf_op jit(solution)/shard_map/ppermute | solution.py:213
  5.9 1.9 %build_cell.1.refs_0_ = bf16[1024,512]{1,0:T(8,128)(2,1)S(1)} custom-call(s32[1,1]{1,0:T(1,128)S(6)} %copy.23.refs_0_, s32[80]{0:T(128)} %bitcast.9, s32[80]{0:T(128)} %bitcast.10, bf16[80,128,128]{2,1,0:T(8,128)(2,1)} %bitcast.8), custom_call_target="tpu_custom_call" | custom-call | flops 16777216 | bytes 5242880 | tf_op jit(solution)/shard_map/build_cell/pallas_call | solution.py:191
  7.8 1.3 %collective-permute-done.1.refs_3_ = bf16[128,256]{1,0:T(8,128)(2,1)S(1)} collective-permute-done((bf16[128,256]{1,0:T(8,128)(2,1)}, bf16[128,256]{1,0:T(8,128)(2,1)S(1)}, u32[]{:S(2)}, u32[]{:S(2)}) %collective-permute-start.1) | collective-permute-done | bytes 65568 | tf_op jit(solution)/shard_map/ppermute | solution.py:213
  11.3 3.7 %collective-permute-start.5 = (bf16[128,256]{1,0:T(8,128)(2,1)S(1)}, bf16[128,256]{1,0:T(8,128)(2,1)S(1)}, u32[]{:S(2)}, u32[]{:S(2)}) collective-permute-start(bf16[128,256]{1,0:T(8,128)(2,1)S(1)} %get-tuple-element.33), channel_id=1, source_target_pairs={{0,6},{1,7},{2,4},{3,5},{4,2},{5,3},{6,0},{7,1},{8,14},{9,15},{10,... | collective-permute-start | bytes 196616 | tf_op jit(solution)/shard_map/ppermute | solution.py:213
  15.1 0.8 %collective-permute-start.7 = (bf16[128,256]{1,0:T(8,128)(2,1)S(1)}, bf16[128,256]{1,0:T(8,128)(2,1)S(1)}, u32[]{:S(2)}, u32[]{:S(2)}) collective-permute-start(bf16[128,256]{1,0:T(8,128)(2,1)S(1)} %get-tuple-element.35), channel_id=1, source_target_pairs={{0,2},{1,3},{2,0},{3,1},{4,6},{5,7},{6,4},{7,5},{8,10},{9,11},{10,... | collective-permute-start | bytes 196616 | tf_op jit(solution)/shard_map/ppermute | solution.py:213
  16.1 1.6 %collective-permute-done.5.refs_1_ = bf16[128,256]{1,0:T(8,128)(2,1)S(1)} collective-permute-done((bf16[128,256]{1,0:T(8,128)(2,1)S(1)}, bf16[128,256]{1,0:T(8,128)(2,1)S(1)}, u32[]{:S(2)}, u32[]{:S(2)}) %collective-permute-start.5) | collective-permute-done | bytes 65568 | tf_op jit(solution)/shard_map/ppermute | solution.py:213
  17.6 3.3 %collective-permute-done.6.refs_2_ = bf16[128,256]{1,0:T(8,128)(2,1)S(1)} collective-permute-done((bf16[128,256]{1,0:T(8,128)(2,1)S(1)}, bf16[128,256]{1,0:T(8,128)(2,1)S(1)}, u32[]{:S(2)}, u32[]{:S(2)}) %collective-permute-start.6) | collective-permute-done | bytes 65568 | tf_op jit(solution)/shard_map/ppermute | solution.py:213
  22.1 1.2 %collective-permute-start.20 = (bf16[136,256]{1,0:T(8,128)(2,1)S(1)}, bf16[136,256]{1,0:T(8,128)(2,1)S(1)}, u32[]{:S(2)}, u32[]{:S(2)}) collective-permute-start(bf16[136,256]{1,0:T(8,128)(2,1)S(1)} %get-tuple-element.51), channel_id=1, source_target_pairs={{0,9},{1,8},{2,11},{3,10},{4,13},{5,12},{6,15},{7,14},{8,1},{9,0},... | collective-permute-start | bytes 208904 | tf_op jit(solution)/shard_map/ppermute | solution.py:219
  23.3 2.5 %collective-permute-start.10 = (bf16[256,128]{1,0:T(8,128)(2,1)S(1)}, bf16[256,128]{1,0:T(8,128)(2,1)S(1)}, u32[]{:S(2)}, u32[]{:S(2)}) collective-permute-start(bf16[256,128]{1,0:T(8,128)(2,1)S(1)} %get-tuple-element.41.refs_1_), channel_id=1, source_target_pairs={{0,6},{1,7},{2,4},{3,5},{4,2},{5,3},{6,0},{7,1},{8,14},{9,15},{10,... | collective-permute-start | bytes 196616 | tf_op jit(solution)/shard_map/ppermute | solution.py:213
  25.9 1.8 %collective-permute-start.8 = (bf16[256,128]{1,0:T(8,128)(2,1)S(1)}, bf16[256,128]{1,0:T(8,128)(2,1)S(1)}, u32[]{:S(2)}, u32[]{:S(2)}) collective-permute-start(bf16[256,128]{1,0:T(8,128)(2,1)S(1)} %get-tuple-element.41.refs_1_), channel_id=1, source_target_pairs={{0,2},{1,3},{2,0},{3,1},{4,6},{5,7},{6,4},{7,5},{8,10},{9,11},{10,... | collective-permute-start | bytes 196616 | tf_op jit(solution)/shard_map/ppermute | solution.py:213
  27.8 1.6 %collective-permute-start.21 = (bf16[136,256]{1,0:T(8,128)(2,1)S(1)}, bf16[136,256]{1,0:T(8,128)(2,1)S(1)}, u32[]{:S(2)}, u32[]{:S(2)}) collective-permute-start(bf16[136,256]{1,0:T(8,128)(2,1)S(1)} %add_corner.1.refs_0_), channel_id=1, source_target_pairs={{0,16},{8,24},{16,0},{24,8},{1,17},{9,25},{17,1},{25,9},{2,18},{10... | collective-permute-start | bytes 208904 | tf_op jit(solution)/shard_map/ppermute | solution.py:213
  29.4 0.8 %collective-permute-done.10.refs_4_ = bf16[256,128]{1,0:T(8,128)(2,1)S(1)} collective-permute-done((bf16[256,128]{1,0:T(8,128)(2,1)S(1)}, bf16[256,128]{1,0:T(8,128)(2,1)S(1)}, u32[]{:S(2)}, u32[]{:S(2)}) %collective-permute-start.10) | collective-permute-done | bytes 65568 | tf_op jit(solution)/shard_map/ppermute | solution.py:213
  30.2 2.2 %collective-permute-done.9.refs_3_ = bf16[256,128]{1,0:T(8,128)(2,1)S(1)} collective-permute-done((bf16[256,128]{1,0:T(8,128)(2,1)S(1)}, bf16[256,128]{1,0:T(8,128)(2,1)S(1)}, u32[]{:S(2)}, u32[]{:S(2)}) %collective-permute-start.9) | collective-permute-done | bytes 65568 | tf_op jit(solution)/shard_map/ppermute | solution.py:213
  33.3 2.4 %collective-permute-start.24 = (bf16[136,256]{1,0:T(8,128)(2,1)S(1)}, bf16[136,256]{1,0:T(8,128)(2,1)S(1)}, u32[]{:S(2)}, u32[]{:S(2)}) collective-permute-start(bf16[136,256]{1,0:T(8,128)(2,1)S(1)} %add_y.1.refs_0_), channel_id=1, source_target_pairs={{0,6},{1,7},{2,4},{3,5},{4,2},{5,3},{6,0},{7,1},{8,14},{9,15},{10,... | collective-permute-start | bytes 208904 | tf_op jit(solution)/shard_map/ppermute | solution.py:213
  35.7 2.1 %collective-permute-start.22 = (bf16[136,256]{1,0:T(8,128)(2,1)S(1)}, bf16[136,256]{1,0:T(8,128)(2,1)S(1)}, u32[]{:S(2)}, u32[]{:S(2)}) collective-permute-start(bf16[136,256]{1,0:T(8,128)(2,1)S(1)} %add_y.1.refs_0_), channel_id=1, source_target_pairs={{0,2},{1,3},{2,0},{3,1},{4,6},{5,7},{6,4},{7,5},{8,10},{9,11},{10,... | collective-permute-start | bytes 208904 | tf_op jit(solution)/shard_map/ppermute | solution.py:213
  38.7 1.5 %collective-permute-start.16 = (bf16[256,128]{1,0:T(8,128)(2,1)S(1)}, bf16[256,128]{1,0:T(8,128)(2,1)S(1)}, u32[]{:S(2)}, u32[]{:S(2)}) collective-permute-start(bf16[256,128]{1,0:T(8,128)(2,1)S(1)} %get-tuple-element.46), channel_id=1, source_target_pairs={{0,16},{8,24},{16,0},{24,8},{1,17},{9,25},{17,1},{25,9},{2,18},{10... | collective-permute-start | bytes 196616 | tf_op jit(solution)/shard_map/ppermute | solution.py:213
  40.2 1.5 %collective-permute-start.17 = (bf16[256,128]{1,0:T(8,128)(2,1)S(1)}, bf16[256,128]{1,0:T(8,128)(2,1)S(1)}, u32[]{:S(2)}, u32[]{:S(2)}) collective-permute-start(bf16[256,128]{1,0:T(8,128)(2,1)S(1)} %get-tuple-element.47), channel_id=1, source_target_pairs={{0,24},{8,16},{16,8},{24,0},{1,25},{9,17},{17,9},{25,1},{2,26},{10... | collective-permute-start | bytes 196616 | tf_op jit(solution)/shard_map/ppermute | solution.py:213
  42.4 0.9 %collective-permute-start.26 = (bf16[128,256]{1,0:T(8,128)(2,1)S(1)}, bf16[128,256]{1,0:T(8,128)(2,1)S(1)}, u32[]{:S(2)}, u32[]{:S(2)}) collective-permute-start(bf16[128,256]{1,0:T(8,128)(2,1)S(1)} %slice.4), channel_id=1, source_target_pairs={{0,9},{1,8},{2,11},{3,10},{4,13},{5,12},{6,15},{7,14},{8,1},{9,0},... | collective-permute-start | bytes 196616 | tf_op jit(solution)/shard_map/ppermute | solution.py:219
  43.4 1.2 %collective-permute-start.25 = (bf16[128,256]{1,0:T(8,128)(2,1)S(1)}, bf16[128,256]{1,0:T(8,128)(2,1)S(1)}, u32[]{:S(2)}, u32[]{:S(2)}) collective-permute-start(bf16[128,256]{1,0:T(8,128)(2,1)S(1)} %slice.4), channel_id=1, source_target_pairs={{0,8},{8,0},{16,24},{24,16},{1,9},{9,1},{17,25},{25,17},{2,10},{10... | collective-permute-start | bytes 196616 | tf_op jit(solution)/shard_map/ppermute | solution.py:213
  44.6 0.7 %activate.1 = (bf16[128,256]{1,0:T(8,128)(2,1)}, f32[256,128]{1,0:T(8,128)S(1)}) custom-call(f32[128,256]{1,0:T(8,128)S(1)} %get-tuple-element.39.refs_0_, bf16[256,256]{1,0:T(8,128)(2,1)S(1)} %copy-done.1, bf16[128,256]{1,0:T(8,128)(2,1)S(1)} %get-tuple-element.40.refs_2_, f32[256,128]{1,0:T(8,128)S(1)} %get-tuple-element.42.refs_3_.refs_1_.refs_4_), custom_call_target="tpu_custom_call" | custom-call | flops 1048576 | bytes 262144 | tf_op jit(solution)/shard_map/activate/pallas_call | solution.py:130
  45.4 0.7 %finish.1 = bf16[128,256]{1,0:T(8,128)(2,1)} custom-call(f32[256,128]{1,0:T(8,128)S(1)} %get-tuple-element.44.refs_0_, f32[256,128]{1,0:T(8,128)S(1)} %get-tuple-element.42.refs_3_.refs_1_.refs_4_, bf16[256,128]{1,0:T(8,128)(2,1)S(1)} %collective-permute-done.15.refs_2_, bf16[256,128]{1,0:T(8,128)(2,1)S(1)} %collective-permute-done.16.refs_3_, ...), custom_call_target="tpu_custom_call" | custom-call | flops 1048576 | bytes 262144 | tf_op jit(solution)/shard_map/finish/pallas_call | solution.py:130
  46.1 0.7 %write_first.1 = (f32[256,256]{1,0:T(8,128)}, f32[256,256]{1,0:T(8,128)}, f32[1,256]{1,0:T(1,128)}) custom-call(bf16[136,256]{1,0:T(8,128)(2,1)S(1)} %add_z.1.a_ref, bf16[128,256]{1,0:T(8,128)(2,1)S(1)} %collective-permute-done.27.b_ref), custom_call_target="tpu_custom_call" | custom-call | flops 1048576 | bytes 262144 | tf_op jit(solution)/shard_map/write_first/pallas_call | solution.py:478
  46.9 0.7 %write_next.2 = (f32[256,256]{1,0:T(8,128)}, f32[256,256]{1,0:T(8,128)}) custom-call(bf16[128,256]{1,0:T(8,128)(2,1)S(1)} %collective-permute-done.26.a_ref, f32[256,256]{1,0:T(8,128)} %get-tuple-element.52.s_ref, f32[256,256]{1,0:T(8,128)} %get-tuple-element.53.n_ref), custom_call_target="tpu_custom_call", output_to_operand_aliasing={{0}: (1, {}), {1}: (2, {})} | custom-call | flops 1048576 | bytes 262144 | tf_op jit(solution)/shard_map/write_next/pallas_call | solution.py:488
  47.6 0.7 %collective-permute-done.25.a_ref = bf16[128,256]{1,0:T(8,128)(2,1)S(1)} collective-permute-done((bf16[128,256]{1,0:T(8,128)(2,1)S(1)}, bf16[128,256]{1,0:T(8,128)(2,1)S(1)}, u32[]{:S(2)}, u32[]{:S(2)}) %collective-permute-start.25) | collective-permute-done | bytes 65568 | tf_op jit(solution)/shard_map/ppermute | solution.py:213
  (63 shorter events, 7.6 us)
Async XLA Ops:
  0.6 7.2 %collective-permute-start.2 = (bf16[128,256]{1,0:T(8,128)(2,1)}, bf16[128,256]{1,0:T(8,128)(2,1)S(1)}, u32[]{:S(2)}, u32[]{:S(2)}) collective-permute-start(bf16[128,256]{1,0:T(8,128)(2,1)} %refs_4_.1), channel_id=1, source_target_pairs={{0,24},{8,16},{16,8},{24,0},{1,25},{9,17},{17,9},{25,1},{2,26},{10... | collective-permute-start | bytes 196616 | tf_op jit(solution)/shard_map/ppermute | solution.py:213
  5.1 4.5 %collective-permute-start = (bf16[128,256]{1,0:T(8,128)(2,1)}, bf16[128,256]{1,0:T(8,128)(2,1)S(1)}, u32[]{:S(2)}, u32[]{:S(2)}) collective-permute-start(bf16[128,256]{1,0:T(8,128)(2,1)} %refs_4_.1), channel_id=1, source_target_pairs={{0,8},{8,0},{16,24},{24,16},{1,9},{9,1},{17,25},{25,17},{2,10},{10... | collective-permute-start | bytes 196616 | tf_op jit(solution)/shard_map/ppermute | solution.py:213
  10.2 4.8 %collective-permute-start.3 = (bf16[256,256]{1,0:T(8,128)(2,1)S(1)}, bf16[256,256]{1,0:T(8,128)(2,1)S(1)}, u32[]{:S(2)}, u32[]{:S(2)}) collective-permute-start(bf16[256,256]{1,0:T(8,128)(2,1)S(1)} %forward_sent.2), channel_id=1, source_target_pairs={{0,1},{1,0},{2,3},{3,2},{4,5},{5,4},{6,7},{7,6},{8,9},{9,8},{10,11... | collective-permute-start | bytes 393224 | tf_op jit(solution)/shard_map/ppermute | solution.py:213
  11.3 6.3 %collective-permute-start.5 = (bf16[128,256]{1,0:T(8,128)(2,1)S(1)}, bf16[128,256]{1,0:T(8,128)(2,1)S(1)}, u32[]{:S(2)}, u32[]{:S(2)}) collective-permute-start(bf16[128,256]{1,0:T(8,128)(2,1)S(1)} %get-tuple-element.33), channel_id=1, source_target_pairs={{0,6},{1,7},{2,4},{3,5},{4,2},{5,3},{6,0},{7,1},{8,14},{9,15},{10,... | collective-permute-start | bytes 196616 | tf_op jit(solution)/shard_map/ppermute | solution.py:213
  15.0 5.9 %collective-permute-start.6 = (bf16[128,256]{1,0:T(8,128)(2,1)S(1)}, bf16[128,256]{1,0:T(8,128)(2,1)S(1)}, u32[]{:S(2)}, u32[]{:S(2)}) collective-permute-start(bf16[128,256]{1,0:T(8,128)(2,1)S(1)} %get-tuple-element.34), channel_id=1, source_target_pairs={{0,4},{1,5},{2,6},{3,7},{4,0},{5,1},{6,2},{7,3},{8,12},{9,13},{10,... | collective-permute-start | bytes 196616 | tf_op jit(solution)/shard_map/ppermute | solution.py:213
  15.1 5.9 %collective-permute-start.7 = (bf16[128,256]{1,0:T(8,128)(2,1)S(1)}, bf16[128,256]{1,0:T(8,128)(2,1)S(1)}, u32[]{:S(2)}, u32[]{:S(2)}) collective-permute-start(bf16[128,256]{1,0:T(8,128)(2,1)S(1)} %get-tuple-element.35), channel_id=1, source_target_pairs={{0,2},{1,3},{2,0},{3,1},{4,6},{5,7},{6,4},{7,5},{8,10},{9,11},{10,... | collective-permute-start | bytes 196616 | tf_op jit(solution)/shard_map/ppermute | solution.py:213
  21.4 4.5 %collective-permute-start.18 = (bf16[136,256]{1,0:T(8,128)(2,1)S(1)}, bf16[136,256]{1,0:T(8,128)(2,1)S(1)}, u32[]{:S(2)}, u32[]{:S(2)}) collective-permute-start(bf16[136,256]{1,0:T(8,128)(2,1)S(1)} %get-tuple-element.49), channel_id=1, source_target_pairs={{0,1},{1,0},{2,3},{3,2},{4,5},{5,4},{6,7},{7,6},{8,9},{9,8},{10,11... | collective-permute-start | bytes 208904 | tf_op jit(solution)/shard_map/ppermute | solution.py:213
  21.5 6.2 %collective-permute-start.19 = (bf16[136,256]{1,0:T(8,128)(2,1)S(1)}, bf16[136,256]{1,0:T(8,128)(2,1)S(1)}, u32[]{:S(2)}, u32[]{:S(2)}) collective-permute-start(bf16[136,256]{1,0:T(8,128)(2,1)S(1)} %get-tuple-element.50), channel_id=1, source_target_pairs={{0,8},{8,0},{16,24},{24,16},{1,9},{9,1},{17,25},{25,17},{2,10},{10... | collective-permute-start | bytes 208904 | tf_op jit(solution)/shard_map/ppermute | solution.py:213
  22.1 5.6 %collective-permute-start.20 = (bf16[136,256]{1,0:T(8,128)(2,1)S(1)}, bf16[136,256]{1,0:T(8,128)(2,1)S(1)}, u32[]{:S(2)}, u32[]{:S(2)}) collective-permute-start(bf16[136,256]{1,0:T(8,128)(2,1)S(1)} %get-tuple-element.51), channel_id=1, source_target_pairs={{0,9},{1,8},{2,11},{3,10},{4,13},{5,12},{6,15},{7,14},{8,1},{9,0},... | collective-permute-start | bytes 208904 | tf_op jit(solution)/shard_map/ppermute | solution.py:219
  23.3 6.9 %collective-permute-start.10 = (bf16[256,128]{1,0:T(8,128)(2,1)S(1)}, bf16[256,128]{1,0:T(8,128)(2,1)S(1)}, u32[]{:S(2)}, u32[]{:S(2)}) collective-permute-start(bf16[256,128]{1,0:T(8,128)(2,1)S(1)} %get-tuple-element.41.refs_1_), channel_id=1, source_target_pairs={{0,6},{1,7},{2,4},{3,5},{4,2},{5,3},{6,0},{7,1},{8,14},{9,15},{10,... | collective-permute-start | bytes 196616 | tf_op jit(solution)/shard_map/ppermute | solution.py:213
  25.8 6.6 %collective-permute-start.9 = (bf16[256,128]{1,0:T(8,128)(2,1)S(1)}, bf16[256,128]{1,0:T(8,128)(2,1)S(1)}, u32[]{:S(2)}, u32[]{:S(2)}) collective-permute-start(bf16[256,128]{1,0:T(8,128)(2,1)S(1)} %get-tuple-element.41.refs_1_), channel_id=1, source_target_pairs={{0,4},{1,5},{2,6},{3,7},{4,0},{5,1},{6,2},{7,3},{8,12},{9,13},{10,... | collective-permute-start | bytes 196616 | tf_op jit(solution)/shard_map/ppermute | solution.py:213
  25.9 6.6 %collective-permute-start.8 = (bf16[256,128]{1,0:T(8,128)(2,1)S(1)}, bf16[256,128]{1,0:T(8,128)(2,1)S(1)}, u32[]{:S(2)}, u32[]{:S(2)}) collective-permute-start(bf16[256,128]{1,0:T(8,128)(2,1)S(1)} %get-tuple-element.41.refs_1_), channel_id=1, source_target_pairs={{0,2},{1,3},{2,0},{3,1},{4,6},{5,7},{6,4},{7,5},{8,10},{9,11},{10,... | collective-permute-start | bytes 196616 | tf_op jit(solution)/shard_map/ppermute | solution.py:213
  27.8 5.5 %collective-permute-start.21 = (bf16[136,256]{1,0:T(8,128)(2,1)S(1)}, bf16[136,256]{1,0:T(8,128)(2,1)S(1)}, u32[]{:S(2)}, u32[]{:S(2)}) collective-permute-start(bf16[136,256]{1,0:T(8,128)(2,1)S(1)} %add_corner.1.refs_0_), channel_id=1, source_target_pairs={{0,16},{8,24},{16,0},{24,8},{1,17},{9,25},{17,1},{25,9},{2,18},{10... | collective-permute-start | bytes 208904 | tf_op jit(solution)/shard_map/ppermute | solution.py:213
  29.4 6.3 %collective-permute-start.11 = (bf16[256,128]{1,0:T(8,128)(2,1)S(1)}, bf16[256,128]{1,0:T(8,128)(2,1)S(1)}, u32[]{:S(2)}, u32[]{:S(2)}) collective-permute-start(bf16[256,128]{1,0:T(8,128)(2,1)S(1)} %get-tuple-element.41.refs_1_), channel_id=1, source_target_pairs={{0,1},{1,0},{2,3},{3,2},{4,5},{5,4},{6,7},{7,6},{8,9},{9,8},{10,11... | collective-permute-start | bytes 196616 | tf_op jit(solution)/shard_map/ppermute | solution.py:213
  30.2 5.5 %collective-permute-start.14 = (bf16[256,128]{1,0:T(8,128)(2,1)S(1)}, bf16[256,128]{1,0:T(8,128)(2,1)S(1)}, u32[]{:S(2)}, u32[]{:S(2)}) collective-permute-start(bf16[256,128]{1,0:T(8,128)(2,1)S(1)} %collective-permute-done.10.refs_4_), channel_id=1, source_target_pairs={{0,1},{1,0},{2,3},{3,2},{4,5},{5,4},{6,7},{7,6},{8,9},{9,8},{10,11... | collective-permute-start | bytes 196616 | tf_op jit(solution)/shard_map/ppermute | solution.py:213
  32.4 5.3 %collective-permute-start.13 = (bf16[256,128]{1,0:T(8,128)(2,1)S(1)}, bf16[256,128]{1,0:T(8,128)(2,1)S(1)}, u32[]{:S(2)}, u32[]{:S(2)}) collective-permute-start(bf16[256,128]{1,0:T(8,128)(2,1)S(1)} %collective-permute-done.9.refs_3_), channel_id=1, source_target_pairs={{0,1},{1,0},{2,3},{3,2},{4,5},{5,4},{6,7},{7,6},{8,9},{9,8},{10,11... | collective-permute-start | bytes 196616 | tf_op jit(solution)/shard_map/ppermute | solution.py:213
  32.5 5.2 %collective-permute-start.12 = (bf16[256,128]{1,0:T(8,128)(2,1)S(1)}, bf16[256,128]{1,0:T(8,128)(2,1)S(1)}, u32[]{:S(2)}, u32[]{:S(2)}) collective-permute-start(bf16[256,128]{1,0:T(8,128)(2,1)S(1)} %collective-permute-done.8.refs_2_), channel_id=1, source_target_pairs={{0,1},{1,0},{2,3},{3,2},{4,5},{5,4},{6,7},{7,6},{8,9},{9,8},{10,11... | collective-permute-start | bytes 196616 | tf_op jit(solution)/shard_map/ppermute | solution.py:213
  33.3 6.9 %collective-permute-start.24 = (bf16[136,256]{1,0:T(8,128)(2,1)S(1)}, bf16[136,256]{1,0:T(8,128)(2,1)S(1)}, u32[]{:S(2)}, u32[]{:S(2)}) collective-permute-start(bf16[136,256]{1,0:T(8,128)(2,1)S(1)} %add_y.1.refs_0_), channel_id=1, source_target_pairs={{0,6},{1,7},{2,4},{3,5},{4,2},{5,3},{6,0},{7,1},{8,14},{9,15},{10,... | collective-permute-start | bytes 208904 | tf_op jit(solution)/shard_map/ppermute | solution.py:213
  35.7 6.6 %collective-permute-start.23 = (bf16[136,256]{1,0:T(8,128)(2,1)S(1)}, bf16[136,256]{1,0:T(8,128)(2,1)S(1)}, u32[]{:S(2)}, u32[]{:S(2)}) collective-permute-start(bf16[136,256]{1,0:T(8,128)(2,1)S(1)} %add_y.1.refs_0_), channel_id=1, source_target_pairs={{0,4},{1,5},{2,6},{3,7},{4,0},{5,1},{6,2},{7,3},{8,12},{9,13},{10,... | collective-permute-start | bytes 208904 | tf_op jit(solution)/shard_map/ppermute | solution.py:213
  35.7 6.6 %collective-permute-start.22 = (bf16[136,256]{1,0:T(8,128)(2,1)S(1)}, bf16[136,256]{1,0:T(8,128)(2,1)S(1)}, u32[]{:S(2)}, u32[]{:S(2)}) collective-permute-start(bf16[136,256]{1,0:T(8,128)(2,1)S(1)} %add_y.1.refs_0_), channel_id=1, source_target_pairs={{0,2},{1,3},{2,0},{3,1},{4,6},{5,7},{6,4},{7,5},{8,10},{9,11},{10,... | collective-permute-start | bytes 208904 | tf_op jit(solution)/shard_map/ppermute | solution.py:213
  38.1 5.3 %collective-permute-start.15 = (bf16[256,128]{1,0:T(8,128)(2,1)S(1)}, bf16[256,128]{1,0:T(8,128)(2,1)S(1)}, u32[]{:S(2)}, u32[]{:S(2)}) collective-permute-start(bf16[256,128]{1,0:T(8,128)(2,1)S(1)} %get-tuple-element.45), channel_id=1, source_target_pairs={{0,8},{8,0},{16,24},{24,16},{1,9},{9,1},{17,25},{25,17},{2,10},{10... | collective-permute-start | bytes 196616 | tf_op jit(solution)/shard_map/ppermute | solution.py:213
  38.7 6.6 %collective-permute-start.16 = (bf16[256,128]{1,0:T(8,128)(2,1)S(1)}, bf16[256,128]{1,0:T(8,128)(2,1)S(1)}, u32[]{:S(2)}, u32[]{:S(2)}) collective-permute-start(bf16[256,128]{1,0:T(8,128)(2,1)S(1)} %get-tuple-element.46), channel_id=1, source_target_pairs={{0,16},{8,24},{16,0},{24,8},{1,17},{9,25},{17,1},{25,9},{2,18},{10... | collective-permute-start | bytes 196616 | tf_op jit(solution)/shard_map/ppermute | solution.py:213
  40.2 5.2 %collective-permute-start.17 = (bf16[256,128]{1,0:T(8,128)(2,1)S(1)}, bf16[256,128]{1,0:T(8,128)(2,1)S(1)}, u32[]{:S(2)}, u32[]{:S(2)}) collective-permute-start(bf16[256,128]{1,0:T(8,128)(2,1)S(1)} %get-tuple-element.47), channel_id=1, source_target_pairs={{0,24},{8,16},{16,8},{24,0},{1,25},{9,17},{17,9},{25,1},{2,26},{10... | collective-permute-start | bytes 196616 | tf_op jit(solution)/shard_map/ppermute | solution.py:213
  43.4 4.9 %collective-permute-start.25 = (bf16[128,256]{1,0:T(8,128)(2,1)S(1)}, bf16[128,256]{1,0:T(8,128)(2,1)S(1)}, u32[]{:S(2)}, u32[]{:S(2)}) collective-permute-start(bf16[128,256]{1,0:T(8,128)(2,1)S(1)} %slice.4), channel_id=1, source_target_pairs={{0,8},{8,0},{16,24},{24,16},{1,9},{9,1},{17,25},{25,17},{2,10},{10... | collective-permute-start | bytes 196616 | tf_op jit(solution)/shard_map/ppermute | solution.py:213
  (10 other events, 63.2 us)
